TPU v7x, 32 devices: a whole 2x2x4 slice. The times are simulated.
32 devices in a mesh: group: 4 (over y, x), fsdp: 8 (over z, core).
Axes of the slice: x: 2, y: 2, z: 4, core: 2. Of those that a mesh axis runs over, the one named last changes fastest.
Arguments:
- hidden_in: bfloat16 [128, 512, 768], P(('group', 'fsdp')), may hold values from -6 to 6
- lengths: int32 [128], P(('group', 'fsdp')), may hold values from 40 to 512, as said below
- out_grad: bfloat16 [128, 256, 768], P(('group', 'fsdp')), may hold values from -6 to 6
- weights: float32 [2, 9216, 768], P(None, 'fsdp')
- weight_m: float32 [4, 2, 9216, 768], P('group', None, 'fsdp')
- weight_v: float32 [4, 2, 9216, 768], P('group', None, 'fsdp'), as said below
- outer_mom: float32 [2, 9216, 768], P(None, 'fsdp'), may hold values from -0.12 to 0.12
- small: float32 [6168], replicated
- small_m: float32 [4, 6168], P('group')
- small_v: float32 [4, 6168], P('group'), as said below
- small_mom: float32 [6168], replicated, may hold values from -0.12 to 0.12
Outputs:
- block_out: bfloat16 [128, 256, 768], P(('group', 'fsdp'))
- input_grad: float32 [128, 512, 768], P(('group', 'fsdp'))
- new_weights: float32 [2, 9216, 768], P(None, 'fsdp')
- weights_low: bfloat16 [2, 9216, 768], P(None, 'fsdp')
- weight_m_new: float32 [4, 2, 9216, 768], P('group', None, 'fsdp')
- weight_v_new: float32 [4, 2, 9216, 768], P('group', None, 'fsdp')
- weight_delta: float32 [2, 9216, 768], P(None, 'fsdp')
- outer_mom_new: float32 [2, 9216, 768], P(None, 'fsdp')
- small_new: float32 [6168], replicated
- small_m_new: float32 [4, 6168], P('group')
- small_v_new: float32 [4, 6168], P('group')
- small_delta: float32 [6168], replicated
- small_mom_new: float32 [6168], replicated
Inputs may be any that keep to these rules, and one draw needn't show every extreme that they name: lengths[b] counts the valid tokens of sequence b; the shortest and the longest allowed length occur in every draw. `weight_v`: second moments are positive. `small_v`: second moments are positive.
All inputs are finite; a program needn't handle non-finite values.
Results may differ from a plain program's by a relative error of at most 0.023.
Values may be sent and summed in bfloat16 or wider, within the bound.
A program may use at most 320 MiB of HBM per device.

v0:
```python
import jax
import jax.numpy as jnp
from jax import lax
from jax.sharding import PartitionSpec as P

STEP = 10


EPS_NORM = 1e-06
MASK_FILL = -1e30
BETA_ONE = 0.9
BETA_TWO = 0.999
ADAM_EPS = 1e-08
DECAY_RATE = 0.01
INNER_RATE = 0.03
SMALL_RATE = 0.6
OUTER_RATE = 0.7
MOMENTUM = 0.9
GELU_COEF = 0.7978845608028654


def norm_apply(values, gain_vec, bias_vec):
    center = values - jnp.mean(values, axis=-1, keepdims=True)
    spread = jnp.mean(center * center, axis=-1, keepdims=True)
    return center * lax.rsqrt(spread + EPS_NORM) * gain_vec + bias_vec


def gelu_tanh(values):
    return (
        0.5 * values * (1.0 + jnp.tanh(GELU_COEF * (values + 0.044715 * values * values * values)))
    )


def split_matrix(matrix_low, model_width):
    inner_width = (matrix_low.shape[0] - 4 * model_width) // 2
    return (
        matrix_low[0:model_width],
        matrix_low[model_width : 2 * model_width],
        matrix_low[2 * model_width : 3 * model_width],
        matrix_low[3 * model_width : 4 * model_width],
        matrix_low[4 * model_width : 4 * model_width + inner_width],
        matrix_low[4 * model_width + inner_width :],
    )


def split_small(small_part, model_width):
    return (
        small_part[0:model_width],
        small_part[model_width : 2 * model_width],
        small_part[2 * model_width : 3 * model_width],
        small_part[3 * model_width : 4 * model_width],
        small_part[4 * model_width :],
    )


def head_split(values, head_count):
    return values.reshape(values.shape[0], values.shape[1], head_count, -1)


def attention_scores(query_heads, key_heads, slopes, key_mask, distance):
    head_size = query_heads.shape[3]
    raw_scores = jnp.einsum(
        "bqhd,bkhd->bhqk", query_heads, key_heads, preferred_element_type=jnp.float32
    ) * float(head_size) ** (-0.5)
    biased = raw_scores - slopes[None, :, None, None] * distance[None, None]
    return jnp.where(key_mask[:, None, None, :], biased, MASK_FILL)


def layer_ahead(
    residual, query_rows_reduced, memory_rows_reduced, matrix_low, small_part, key_mask, distance
):
    model_width = residual.shape[2]
    query_weight, key_weight, value_weight, output_weight, inner_weight, outer_weight = (
        split_matrix(matrix_low, model_width)
    )
    gain_one, bias_one, gain_two, bias_two, slopes = split_small(small_part, model_width)
    head_count = slopes.shape[0]
    query_rows = jnp.einsum(
        "mhv,vx->mhx", query_rows_reduced, query_weight, preferred_element_type=jnp.float32
    ).astype(jnp.bfloat16)
    every_key_row = jnp.einsum(
        "zho,og->zhg", memory_rows_reduced, key_weight, preferred_element_type=jnp.float32
    ).astype(jnp.bfloat16)
    every_value_row = jnp.einsum(
        "zho,og->zhg", memory_rows_reduced, value_weight, preferred_element_type=jnp.float32
    ).astype(jnp.bfloat16)
    scores = attention_scores(
        head_split(query_rows, head_count),
        head_split(every_key_row, head_count),
        slopes,
        key_mask,
        distance,
    )
    row_peak = jnp.max(scores, axis=-1, keepdims=True)
    lifted = jnp.exp(scores - row_peak)
    row_total = jnp.sum(lifted, axis=-1, keepdims=True)
    shares = (lifted / row_total).astype(jnp.bfloat16)
    log_total = row_peak + jnp.log(row_total)
    mixed_heads = jnp.einsum(
        "bhqk,bkhd->bqhd",
        shares,
        head_split(every_value_row, head_count),
        preferred_element_type=jnp.float32,
    )
    attention_result = mixed_heads.reshape(residual.shape).astype(jnp.bfloat16)
    total_one = residual + jnp.einsum(
        "mhv,vx->mhx", attention_result, output_weight, preferred_element_type=jnp.float32
    )
    normalized_rows = norm_apply(total_one, gain_one, bias_one)
    normalized_rows_reduced = normalized_rows.astype(jnp.bfloat16)
    hidden_preactivation = jnp.einsum(
        "aye,we->ayw", normalized_rows_reduced, inner_weight, preferred_element_type=jnp.float32
    )
    hidden_activation = gelu_tanh(hidden_preactivation).astype(jnp.bfloat16)
    total_two = normalized_rows + jnp.einsum(
        "wma,ar->wmr", hidden_activation, outer_weight, preferred_element_type=jnp.float32
    )
    kept_state = (
        query_rows_reduced,
        memory_rows_reduced,
        query_rows,
        every_key_row,
        every_value_row,
        log_total,
        attention_result,
        total_one,
        normalized_rows_reduced,
        hidden_preactivation,
        hidden_activation,
        total_two,
    )
    return (norm_apply(total_two, gain_two, bias_two), kept_state)


def layer_back(grad_out, kept_state, matrix_low, small_part, key_mask, distance):
    (
        query_rows_reduced,
        memory_rows_reduced,
        query_rows,
        every_key_row,
        every_value_row,
        log_total,
        attention_result,
        total_one,
        normalized_rows_reduced,
        hidden_preactivation,
        hidden_activation,
        total_two,
    ) = kept_state
    model_width = total_one.shape[2]
    query_weight, key_weight, value_weight, output_weight, inner_weight, outer_weight = (
        split_matrix(matrix_low, model_width)
    )
    gain_one, bias_one, gain_two, bias_two, slopes = split_small(small_part, model_width)
    head_count = slopes.shape[0]
    score_scale = float(model_width // head_count) ** (-0.5)
    norm_pull_two = jax.vjp(norm_apply, total_two, gain_two, bias_two)[1]
    back_two, back_gain_two, back_bias_two = norm_pull_two(grad_out)
    second_branch_gradient_reduced = back_two.astype(jnp.bfloat16)
    outer_weight_gradient = jnp.einsum(
        "hit,hiv->tv",
        hidden_activation,
        second_branch_gradient_reduced,
        preferred_element_type=jnp.float32,
    )
    back_hidden = jnp.einsum(
        "aye,we->ayw",
        second_branch_gradient_reduced,
        outer_weight,
        preferred_element_type=jnp.float32,
    )
    hidden_preact_gradient = jax.vjp(gelu_tanh, hidden_preactivation)[1](back_hidden)[0].astype(
        jnp.bfloat16
    )
    grad_inner = jnp.einsum(
        "hit,hiv->tv",
        hidden_preact_gradient,
        normalized_rows_reduced,
        preferred_element_type=jnp.float32,
    )
    back_normed = back_two + jnp.einsum(
        "wma,ar->wmr", hidden_preact_gradient, inner_weight, preferred_element_type=jnp.float32
    )
    norm_pull_one = jax.vjp(norm_apply, total_one, gain_one, bias_one)[1]
    back_one, back_gain_one, back_bias_one = norm_pull_one(back_normed)
    first_branch_gradient_reduced = back_one.astype(jnp.bfloat16)
    grad_output = jnp.einsum(
        "lzc,lzu->cu",
        attention_result,
        first_branch_gradient_reduced,
        preferred_element_type=jnp.float32,
    )
    back_attended = jnp.einsum(
        "ajp,rp->ajr",
        first_branch_gradient_reduced,
        output_weight,
        preferred_element_type=jnp.float32,
    ).astype(jnp.bfloat16)
    query_heads = head_split(query_rows, head_count)
    key_heads = head_split(every_key_row, head_count)
    value_heads = head_split(every_value_row, head_count)
    back_mixed = head_split(back_attended, head_count)
    scores = attention_scores(query_heads, key_heads, slopes, key_mask, distance)
    shares = jnp.exp(scores - log_total)
    back_shares = jnp.einsum(
        "bqhd,bkhd->bhqk", back_mixed, value_heads, preferred_element_type=jnp.float32
    )
    back_scores = shares * (back_shares - jnp.sum(shares * back_shares, axis=-1, keepdims=True))
    back_slopes = -jnp.sum(back_scores * distance[None, None], axis=(0, 2, 3))
    back_scores_low = back_scores.astype(jnp.bfloat16)
    query_rows_gradient = (
        (
            score_scale
            * jnp.einsum(
                "bhqk,bkhd->bqhd", back_scores_low, key_heads, preferred_element_type=jnp.float32
            )
        )
        .astype(jnp.bfloat16)
        .reshape(query_rows.shape)
    )
    key_rows_gradient = (
        (
            score_scale
            * jnp.einsum(
                "bhqk,bqhd->bkhd", back_scores_low, query_heads, preferred_element_type=jnp.float32
            )
        )
        .astype(jnp.bfloat16)
        .reshape(every_key_row.shape)
    )
    value_rows_gradient = (
        jnp.einsum(
            "bhqk,bqhd->bkhd",
            shares.astype(jnp.bfloat16),
            back_mixed,
            preferred_element_type=jnp.float32,
        )
        .astype(jnp.bfloat16)
        .reshape(every_value_row.shape)
    )
    grad_query = jnp.einsum(
        "lzc,lzu->cu", query_rows_reduced, query_rows_gradient, preferred_element_type=jnp.float32
    )
    key_weight_gradient = jnp.einsum(
        "jnx,jnp->xp", memory_rows_reduced, key_rows_gradient, preferred_element_type=jnp.float32
    )
    grad_value = jnp.einsum(
        "jnx,jnp->xp", memory_rows_reduced, value_rows_gradient, preferred_element_type=jnp.float32
    )
    back_query_in = back_one + jnp.einsum(
        "ajp,rp->ajr", query_rows_gradient, query_weight, preferred_element_type=jnp.float32
    )
    back_memory_in = jnp.einsum(
        "xtn,an->xta", key_rows_gradient, key_weight, preferred_element_type=jnp.float32
    ) + jnp.einsum(
        "xtn,an->xta", value_rows_gradient, value_weight, preferred_element_type=jnp.float32
    )
    grad_matrix = jnp.concatenate(
        [
            grad_query,
            key_weight_gradient,
            grad_value,
            grad_output,
            grad_inner,
            outer_weight_gradient,
        ],
        axis=0,
    )
    grad_small = jnp.concatenate(
        [back_gain_one, back_bias_one, back_gain_two, back_bias_two, back_slopes]
    )
    return (back_query_in, back_memory_in, grad_matrix, grad_small)


def adam_step(master, gradient, first_mom, second_mom, rate):
    first_new = BETA_ONE * first_mom + (1.0 - BETA_ONE) * gradient
    second_new = BETA_TWO * second_mom + (1.0 - BETA_TWO) * gradient * gradient
    first_hat = first_new / (1.0 - BETA_ONE**STEP)
    second_hat = second_new / (1.0 - BETA_TWO**STEP)
    inner_move = rate * (first_hat / (jnp.sqrt(second_hat) + ADAM_EPS) + DECAY_RATE * master)
    return (first_new, second_new, inner_move)


def outer_step(master, moves_sum, momentum_old, group_count):
    mean_move = moves_sum / group_count
    momentum_new = MOMENTUM * momentum_old + mean_move
    return (mean_move, momentum_new, master - OUTER_RATE * (mean_move + MOMENTUM * momentum_new))


def shards(
    hidden_in,
    lengths,
    out_grad,
    weights,
    weight_m,
    weight_v,
    outer_mom,
    small,
    small_m,
    small_v,
    small_mom,
):
    seq_length = hidden_in.shape[1]
    half_length = seq_length // 2
    part_size = small.shape[0] // 2
    positions = jnp.arange(seq_length, dtype=jnp.int32)
    halves = jnp.arange(half_length, dtype=jnp.int32)
    mask_one = positions[None, :] < lengths[:, None]
    mask_two = 2 * halves[None, :] < lengths[:, None]
    distance_one = jnp.abs(2 * halves[:, None] - positions[None, :]).astype(jnp.float32)
    distance_two = (2 * jnp.abs(halves[:, None] - halves[None, :])).astype(jnp.float32)
    masters_low = weights.astype(jnp.bfloat16)

    def fetch_ahead(layer_index):
        return lax.all_gather(masters_low[layer_index], "fsdp", axis=0, tiled=True)

    def fetch_again(layer_index):
        return lax.all_gather(masters_low[layer_index], "fsdp", axis=0, tiled=True)

    def reduce_layer(grad_rows):
        return lax.psum_scatter(
            grad_rows.astype(jnp.bfloat16), "fsdp", scatter_dimension=0, tiled=True
        ).astype(jnp.float32)

    hidden_wide = hidden_in.astype(jnp.float32)
    pooled = (hidden_wide[:, 0::2] + hidden_wide[:, 1::2]) * 0.5
    matrix_one = fetch_ahead(0)
    first_out, kept_one = layer_ahead(
        pooled,
        pooled.astype(jnp.bfloat16),
        hidden_in,
        matrix_one,
        small[:part_size],
        mask_one,
        distance_one,
    )
    matrix_two = fetch_ahead(1)
    first_low = first_out.astype(jnp.bfloat16)
    second_out, kept_two = layer_ahead(
        first_out, first_low, first_low, matrix_two, small[part_size:], mask_two, distance_two
    )
    block_out = second_out.astype(jnp.bfloat16)
    back_two = fetch_again(1)
    query_grad_two, memory_grad_two, matrix_grad_two, small_grad_two = layer_back(
        out_grad.astype(jnp.float32), kept_two, back_two, small[part_size:], mask_two, distance_two
    )
    first_grad = query_grad_two + memory_grad_two
    shard_two = reduce_layer(matrix_grad_two)
    back_one = fetch_again(0)
    query_grad_one, memory_grad_one, matrix_grad_one, small_grad_one = layer_back(
        first_grad, kept_one, back_one, small[:part_size], mask_one, distance_one
    )
    input_grad = memory_grad_one + jnp.repeat(query_grad_one * 0.5, 2, axis=1)
    shard_one = reduce_layer(matrix_grad_one)
    grad_shard = jnp.stack([shard_one, shard_two])
    small_grad = lax.psum(jnp.concatenate([small_grad_one, small_grad_two]), "fsdp")
    weight_first, weight_second, weight_move = adam_step(
        weights, grad_shard[None], weight_m, weight_v, INNER_RATE
    )
    small_first, small_second, small_move = adam_step(
        small, small_grad[None], small_m, small_v, SMALL_RATE
    )
    weight_sum, small_sum = (
        lax.psum(weight_move[0].astype(jnp.bfloat16), "group").astype(jnp.float32),
        lax.psum(small_move[0].astype(jnp.bfloat16), "group").astype(jnp.float32),
    )
    group_count = lax.axis_size("group")
    weight_mean, weight_mom, weight_new = outer_step(weights, weight_sum, outer_mom, group_count)
    small_mean, small_momentum, small_after = outer_step(small, small_sum, small_mom, group_count)
    return (
        block_out,
        input_grad,
        weight_new,
        weight_new.astype(jnp.bfloat16),
        weight_first,
        weight_second,
        weight_mean,
        weight_mom,
        small_after,
        small_first,
        small_second,
        small_mean,
        small_momentum,
    )


def solution(mesh):
    in_specs = (
        P(("group", "fsdp"), None, None),
        P(("group", "fsdp")),
        P(("group", "fsdp"), None, None),
        P(None, "fsdp", None),
        P("group", None, "fsdp", None),
        P("group", None, "fsdp", None),
        P(None, "fsdp", None),
        P(),
        P("group", None),
        P("group", None),
        P(),
    )
    out_specs = (
        P(("group", "fsdp"), None, None),
        P(("group", "fsdp"), None, None),
        P(None, "fsdp", None),
        P(None, "fsdp", None),
        P("group", None, "fsdp", None),
        P("group", None, "fsdp", None),
        P(None, "fsdp", None),
        P(None, "fsdp", None),
        P(),
        P("group", None),
        P("group", None),
        P(),
        P(),
    )
    return jax.shard_map(shards, mesh=mesh, in_specs=in_specs, out_specs=out_specs, check_vma=False)
```

profile of v0, /device:TPU:0, one launch (start us, length us, event | category | flops | bytes accessed | tf_op | source)
XLA Modules:
  0.0 854.5 jit_solution(9047452997751633927)
XLA Ops:
  13.4 13.8 %slice.112 = f32[4,256,768]{2,1,0:T(8,128)S(1)} slice(bf16[4,512,768]{2,1,0:T(8,128)(2,1)} %param.11), slice={[0:4:1], [0:512:2], [0:768:1]} | slice | bytes 6291456 | tf_op jit(solution)/shard_map/slice | solution.py:326
  27.3 16.0 %slice.113 = f32[4,256,768]{2,1,0:T(8,128)} slice(bf16[4,512,768]{2,1,0:T(8,128)(2,1)} %param.11), slice={[0:4:1], [1:512:2], [0:768:1]} | slice | bytes 6291456 | tf_op jit(solution)/shard_map/slice | solution.py:326
  51.6 93.5 %all-gather.5.cloned.1.call-done = bf16[1,9216,768]{2,1,0:T(8,128)(2,1)} async-done(((bf16[1,1152,768]{2,1,0:T(8,128)(2,1)}), bf16[1,9216,768]{2,1,0:T(8,128)(2,1)}) %all-gather.5.cloned.1.call-update) | async-done | bytes 14155792 | tf_op jit(solution)/shard_map/all_gather | solution.py:315
  173.1 14.4 %fusion.93 = (f32[4,12,256]{2,1,0:T(8,128)S(1)}, f32[4,12,256,512]{3,2,1,0:T(8,128)}) fusion(f32[12,256,512]{2,1,0:T(8,128)} %broadcast_multiply_fusion, bf16[4,256,12,64]{1,3,2,0:T(8,128)(2,1)} %bitcast.254, bf16[4,512,12,64]{1,3,2,0:T(8,128)(2,1)S(1)} %bitcast.246, pred[4,512]{1,0:T(4,128)(4,1)S(1)} %iota_compare_fusion), kind=kOutput, calls=%fused_computation.214 | convolution fusion | flops 830459904 | bytes 36227072 | tf_op jit(solution)/shard_map/bqhd,bkhd->bhqk/dot_general | solution.py:62
  187.5 11.7 %fusion = f32[4,12,256]{2,1,0:T(8,128)S(1)} fusion(f32[4,12,256,512]{3,2,1,0:T(8,128)} %get-tuple-element.68, f32[4,12,256]{2,1,0:T(8,128)S(1)} %get-tuple-element.67), kind=kLoop, calls=%fused_computation.7 | loop fusion | flops 12570624 | bytes 25264128 | tf_op jit(solution)/shard_map/reduce_sum | solution.py:96
  199.2 12.2 %fusion.56 = bf16[4,12,64,256]{3,2,1,0:T(8,128)(2,1)S(1)} fusion(bf16[4,512,12,64]{1,3,2,0:T(8,128)(2,1)S(1)} %bitcast.261, f32[4,12,256,512]{3,2,1,0:T(8,128)} %get-tuple-element.68, f32[4,12,256]{2,1,0:T(8,128)S(1)} %fusion, f32[4,12,256]{2,1,0:T(8,128)S(1)} %get-tuple-element.67), kind=kOutput, calls=%fused_computation.138 | convolution fusion | flops 824967168 | bytes 29982720 | tf_op jit(solution)/shard_map/bhqk,bkhd->bqhd/dot_general | solution.py:99
  215.6 7.9 fusion.34
  223.6 13.6 %fusion.95 = (f32[4,256]{1,0:T(4,128)S(1)}, f32[4,256,768]{2,1,0:T(8,128)S(1)}) fusion(bf16[1,9216,768]{2,1,0:T(8,128)(2,1)} %all-gather.5.cloned.1.call-done, f32[4,256,3072]{2,1,0:T(8,128)S(1)} %fusion.34, f32[768]{0:T(1024)S(1)} %get-tuple-element.61, f32[768]{0:T(1024)S(1)} %get-tuple-element.62, f32[4,256]{1,0:T(4,128)S(1)} %fusion.79, ...), kind=kOutput, calls=%fused_computation.216 | convolution fusion | flops 4864867328 | bytes 23611392 | tf_op jit(solution)/shard_map/wma,ar->wmr/dot_general | solution.py:115
  239.5 35.2 %all-gather.7.cloned.1.call-done = bf16[1,9216,768]{2,1,0:T(8,128)(2,1)} async-done(((bf16[1,1152,768]{2,1,0:T(8,128)(2,1)}), bf16[1,9216,768]{2,1,0:T(8,128)(2,1)}) %all-gather.7.cloned.1.call-update) | async-done | bytes 14155792 | tf_op jit(solution)/shard_map/all_gather | solution.py:315
  312.4 11.8 %fusion.38 = f32[4,256,3072]{2,1,0:T(8,128)} fusion(bf16[1,9216,768]{2,1,0:T(8,128)(2,1)} %all-gather.7.cloned.1.call-done, f32[4,256,768]{2,1,0:T(8,128)S(1)} %get-tuple-element.76, f32[768]{0:T(1024)S(1)} %get-tuple-element.57, f32[768]{0:T(1024)S(1)} %get-tuple-element.58, f32[4,256]{1,0:T(4,128)S(1)} %fusion.81, f32[4,256]{1,0:T(4,128)S(1)} %broadcast_multiply_fusion.5), kind=kOutput, calls=%fused_computation.83 | convolution fusion | flops 4835770368 | bytes 20461568 | tf_op jit(solution)/shard_map/aye,we->ayw/dot_general | solution.py:111
  324.2 11.1 %fusion.98 = (f32[4,256]{1,0:T(4,128)S(1)}, f32[4,256,768]{2,1,0:T(8,128)S(1)}) fusion(bf16[1,9216,768]{2,1,0:T(8,128)(2,1)S(1)} %bitcast.281, f32[4,256,3072]{2,1,0:T(8,128)} %fusion.38, f32[768]{0:T(1024)S(1)} %get-tuple-element.57, f32[768]{0:T(1024)S(1)} %get-tuple-element.58, f32[4,256]{1,0:T(4,128)S(1)} %fusion.81, ...), kind=kOutput, calls=%fused_computation.219 | convolution fusion | flops 4864867328 | bytes 23613440 | tf_op jit(solution)/shard_map/wma,ar->wmr/dot_general | solution.py:115
  340.8 17.2 %fusion.9 = bf16[4,256,3072]{2,1,0:T(8,128)(2,1)} fusion(f32[4,256,3072]{2,1,0:T(8,128)} %fusion.38, bf16[1,9216,768]{2,1,0:T(8,128)(2,1)S(1)} %bitcast.281, f32[4,256]{1,0:T(4,128)S(1)} %negate_multiply_fusion.3, bf16[4,256,768]{2,1,0:T(8,128)(2,1)S(1)} %copy-done.28, f32[4,256,768]{2,1,0:T(8,128)S(1)} %get-tuple-element.78, ...), kind=kOutput, calls=%fused_computation.24 | convolution fusion | flops 4914413568 | bytes 28332032 | tf_op jit(solution)/shard_map/aye,we->ayw/dot_general | solution.py:166
  358.0 9.6 %multiply_reduce_fusion.4 = (f32[768]{0:T(1024)}, f32[4,256]{1,0:T(4,128)S(1)}, f32[768]{0:T(1024)}, f32[4,256,768]{2,1,0:T(8,128)S(1)}) fusion(f32[4,256,768]{2,1,0:T(8,128)S(1)} %get-tuple-element.76, f32[4,256]{1,0:T(4,128)S(1)} %fusion.81, f32[4,256]{1,0:T(4,128)S(1)} %broadcast_multiply_fusion.5, f32[768]{0:T(1024)S(1)} %get-tuple-element.58, ...), kind=kOutput, calls=%fused_computation.93 | convolution fusion | flops 4845204480 | bytes 22063104 | tf_op jit(solution)/shard_map/wma,ar->wmr/dot_general | solution.py:181
  379.5 9.5 %multiply_reduce_fusion.3 = (f32[4,12,256]{2,1,0:T(8,128)S(1)}, f32[4,12,256,256]{2,3,1,0:T(8,128)}) fusion(f32[4,12,256,256]{2,3,1,0:T(8,128)} %copy-done, f32[4,12,256]{2,1,0:T(8,128)S(1)} %log_add_fusion, bf16[4,256,12,64]{1,3,2,0:T(8,128)(2,1)S(1)} %bitcast.259, bf16[4,256,12,64]{1,3,2,0:T(8,128)(2,1)S(1)} %bitcast.263), kind=kOutput, calls=%fused_computation.32 | convolution fusion | flops 412078080 | bytes 28409856 | tf_op jit(solution)/shard_map/bqhd,bkhd->bhqk/dot_general | solution.py:205
  389.0 7.8 multiply_reduce_fusion.2
  410.9 7.9 fusion.31
  418.9 10.7 %fusion.32 = bf16[9216,768]{1,0:T(8,128)(2,1)} fusion(bf16[9216,768]{1,0:T(8,128)(2,1)} %fusion.31, f32[4,256]{1,0:T(4,128)S(1)} %negate_multiply_fusion.3, bf16[4,256,768]{2,1,0:T(8,128)(2,1)S(1)} %copy-done.29, f32[4,256,768]{2,1,0:T(8,128)S(1)} %copy-done.22, f32[4,256]{1,0:T(4,128)S(1)} %get-tuple-element.65, f32[768]{0:T(1024)S(1)} %copy-done.67, ...), kind=kOutput, calls=%fused_computation.66 | convolution fusion | flops 4869586944 | bytes 22039552 | tf_op jit(solution)/shard_map/hit,hiv->tv/dot_general | solution.py:160
  444.5 17.4 %fusion.5 = bf16[4,256,3072]{2,1,0:T(8,128)(2,1)} fusion(f32[4,256,3072]{2,1,0:T(8,128)} %copy-done.88, bf16[1,9216,768]{2,1,0:T(8,128)(2,1)S(1)} %bitcast.279, f32[4,256,768]{2,1,0:T(8,128)S(1)} %get-tuple-element.43, f32[4,256]{1,0:T(4,128)S(1)} %negate_multiply_fusion.1), kind=kOutput, calls=%fused_computation.20 | convolution fusion | flops 4908908544 | bytes 26742784 | tf_op jit(solution)/shard_map/aye,we->ayw/dot_general | solution.py:166
  461.9 8.0 multiply_reduce_fusion.6
  478.0 22.4 %multiply_reduce_fusion.1 = (f32[4,12,256]{2,1,0:T(8,128)S(1)}, f32[4,12,256,512]{3,2,1,0:T(8,128)}) fusion(f32[4,12,256,512]{3,2,1,0:T(8,128)} %get-tuple-element.68, f32[4,12,256]{2,1,0:T(8,128)S(1)} %log_add_fusion.1, bf16[4,256,12,64]{1,3,2,0:T(8,128)(2,1)} %bitcast.256, bf16[4,512,12,64]{1,3,2,0:T(8,128)(2,1)} %bitcast.260), kind=kOutput, calls=%fused_computation.2 | convolution fusion | flops 824168448 | bytes 55148544 | tf_op jit(solution)/shard_map/bqhd,bkhd->bhqk/dot_general | solution.py:205
  500.5 22.1 %multiply_reduce_fusion = (f32[12]{0:T(128)S(1)}, bf16[4,12,256,512]{3,2,1,0:T(8,128)(2,1)}) fusion(f32[256,512]{1,0:T(8,128)S(1)} %copy-done.33, f32[4,12,256,512]{3,2,1,0:T(8,128)} %get-tuple-element.85, f32[4,12,256]{2,1,0:T(8,128)S(1)} %get-tuple-element.84, f32[4,12,256,512]{3,2,1,0:T(8,128)} %get-tuple-element.68, f32[4,12,256]{2,1,0:T(8,128)S(1)} %log_add_fusion.1), kind=kLoop, calls=%fused_computation | loop fusion | flops 37748724 | bytes 63537200 | tf_op jit(solution)/shard_map/reduce_sum | solution.py:209
  522.5 9.7 %multiply_convert_fusion.3 = bf16[4,12,64,256]{3,2,1,0:T(8,128)(2,1)} fusion(bf16[4,512,12,64]{1,3,2,0:T(8,128)(2,1)S(1)} %bitcast.247, bf16[4,12,256,512]{3,2,1,0:T(8,128)(2,1)} %get-tuple-element.47), kind=kOutput, calls=%fused_computation.97 | convolution fusion | flops 806879232 | bytes 17301504 | tf_op jit(solution)/shard_map/bhqk,bkhd->bqhd/dot_general | solution.py:214
  547.6 10.6 %fusion.53 = bf16[4,12,64,512]{3,2,1,0:T(8,128)(2,1)S(1)} fusion(bf16[4,256,12,64]{1,3,2,0:T(8,128)(2,1)S(1)} %bitcast.257, f32[4,12,256,512]{3,2,1,0:T(8,128)} %get-tuple-element.68, f32[4,12,256]{2,1,0:T(8,128)S(1)} %log_add_fusion.1), kind=kOutput, calls=%fused_computation.134 | convolution fusion | flops 819462144 | bytes 29933568 | tf_op jit(solution)/shard_map/bhqk,bqhd->bkhd/dot_general | solution.py:232
  564.6 11.0 %fusion.29 = bf16[9216,768]{1,0:T(8,128)(2,1)} fusion(bf16[9216,768]{1,0:T(8,128)(2,1)} %fusion.62, bf16[4,256,3072]{2,1,0:T(8,128)(2,1)} %fusion.5, f32[4,256,768]{2,1,0:T(8,128)S(1)} %copy-done.6, f32[768]{0:T(1024)S(1)} %copy-done.81, f32[768]{0:T(1024)S(1)} %copy-done.72, f32[4,256]{1,0:T(4,128)S(1)} %copy-done.74, f32[4,256]{1,0:T(4,128)S(1)} %copy-done.62), kind=kOutput, calls=%fused_computation.63 | convolution fusion | flops 4838129664 | bytes 14170112 | tf_op jit(solution)/shard_map/hit,hiv->tv/dot_general | solution.py:175
  575.6 9.2 %fusion.30 = bf16[9216,768]{1,0:T(8,128)(2,1)} fusion(bf16[9216,768]{1,0:T(8,128)(2,1)} %fusion.29, f32[4,256,768]{2,1,0:T(8,128)S(1)} %copy-done.38, f32[4,256]{1,0:T(4,128)S(1)} %negate_multiply_fusion.1, f32[4,256,3072]{2,1,0:T(8,128)S(1)} %bitcast.285), kind=kOutput, calls=%fused_computation.64 | convolution fusion | flops 4864081920 | bytes 20451328 | tf_op jit(solution)/shard_map/hit,hiv->tv/dot_general | solution.py:160
  584.8 142.5 %reduce-scatter.3.cloned.1.call-done = bf16[1152,768]{1,0:T(8,128)(2,1)} async-done(((bf16[9216,768]{1,0:T(8,128)(2,1)}), bf16[1152,768]{1,0:T(8,128)(2,1)}) %reduce-scatter.3.cloned.1.call-update) | async-done | bytes 1769488 | tf_op jit(solution)/shard_map/reduce_scatter | solution.py:321
  727.3 14.9 %fusion.43 = (bf16[2,1152,768]{2,1,0:T(8,128)(2,1)}, f32[1,2,1152,768]{3,2,1,0:T(8,128)}, f32[1,2,1152,768]{3,2,1,0:T(8,128)}) fusion(f32[2,1152,768]{2,1,0:T(8,128)} %param.14, bf16[1,1,1152,768]{3,2,1,0:T(8,128)(2,1)} %bitcast.270, bf16[1,1,1152,768]{3,2,1,0:T(8,128)(2,1)} %bitcast.271, f32[1,2,1152,768]{3,2,1,0:T(8,128)} %param.15, ...), kind=kLoop, calls=%fused_computation.89 | loop fusion | flops 30081024 | bytes 42467328 | tf_op jit(solution)/shard_map/convert_element_type | solution.py:364
  752.0 8.6 %reshape.426 = f32[4,512,768]{2,1,0:T(8,128)} reshape(f32[4,256,2,768]{3,2,1,0:T(2,128)} %broadcast_in_dim.66) | data formatting | bytes 12582912 | tf_op jit(solution)/shard_map/reshape | solution.py:353
  760.8 26.0 %psum.22 = f32[6168]{0:T(1024)S(1)} all-reduce(f32[6168]{0:T(1024)S(1)} %concatenate.34), channel_id=1, replica_groups=mesh['group'=4,'fsdp'=8] {'fsdp'}, use_global_device_ids=true, to_apply=%region_35.36 | all-reduce | flops 6168 | bytes 49344 | tf_op jit(solution)/shard_map/psum | solution.py:356
  787.5 16.8 %psum.23 = bf16[6168]{0:T(1024)(128)(2,1)S(1)} all-reduce(bf16[6168]{0:T(1024)(128)(2,1)S(1)} %get-tuple-element.30), channel_id=1, replica_groups=mesh['group'=4,'fsdp'=8] {'group'}, use_global_device_ids=true, to_apply=%region_36.37 | all-reduce | flops 6168 | bytes 24672 | tf_op jit(solution)/shard_map/psum | solution.py:365
  815.4 19.1 %all-reduce.2.cloned.1.call-done = bf16[2,1152,768]{2,1,0:T(8,128)(2,1)} async-done(((bf16[2,1152,768]{2,1,0:T(8,128)(2,1)}), bf16[2,1152,768]{2,1,0:T(8,128)(2,1)}) %all-reduce.2.cloned.1.call-update) | async-done | bytes 3538960 | tf_op jit(solution)/shard_map/psum | solution.py:364
  834.5 13.0 %fusion.84 = (bf16[2,1152,768]{2,1,0:T(8,128)(2,1)}, f32[2,1152,768]{2,1,0:T(8,128)}, f32[2,1152,768]{2,1,0:T(8,128)}, f32[2,1152,768]{2,1,0:T(8,128)}) fusion(f32[2,1152,768]{2,1,0:T(8,128)} %param.14, f32[2,1152,768]{2,1,0:T(8,128)} %param.17, bf16[2,1152,768]{2,1,0:T(8,128)(2,1)} %all-reduce.2.cloned.1.call-done), kind=kLoop, calls=%fused_computation.207 | loop fusion | flops 15925248 | bytes 42467328 | tf_op jit(solution)/shard_map/convert_element_type | solution.py:374
  (323 shorter events, 183.9 us)
Async XLA Ops:
  7.2 137.9 %all-gather.5.cloned.1.call-start = ((), (), s32[]{:S(2)}) async-start(), calls=%async_computation.5 | async-start | bytes 15925248 | tf_op jit(solution)/shard_map/all_gather | solution.py:315
  12.6 262.0 %all-gather.7.cloned.1.call-start = ((), (), s32[]{:S(2)}) async-start(), calls=%async_computation.6 | async-start | bytes 15925248 | tf_op jit(solution)/shard_map/all_gather | solution.py:315
  13.4 571.4 %reduce-scatter.5.cloned.1.call-start = ((), (), s32[]{:S(2)}) async-start(), calls=%async_computation.3 | async-start | bytes 15925248 | tf_op jit(solution)/shard_map/reduce_scatter | solution.py:321
  27.2 22.8 %copy-start.7 = (f32[4,256,768]{2,1,0:T(8,128)}, f32[4,256,768]{2,1,0:T(8,128)S(1)}, u32[]{:S(2)}) copy-start(f32[4,256,768]{2,1,0:T(8,128)S(1)} %slice.112) | copy-start | bytes 9437188
  27.2 16.1 %copy-start.84 = (s32[4]{0:T(128)S(1)}, s32[4]{0:T(128)}, u32[]{:S(2)}) copy-start(s32[4]{0:T(128)} %param.12) | copy-start | bytes 52
  27.2 16.3 %copy-start.51 = (f32[6168]{0:T(1024)S(1)}, f32[6168]{0:T(1024)}, u32[]{:S(2)}) copy-start(f32[6168]{0:T(1024)} %param.18) | copy-start | bytes 74020
  44.3 179.3 %copy-start.71 = (f32[768]{0:T(1024)}, f32[768]{0:T(1024)S(1)}, u32[]{:S(2)}) copy-start(f32[768]{0:T(1024)S(1)} %get-tuple-element.62) | copy-start | bytes 9220
  44.3 179.3 %copy-start.80 = (f32[768]{0:T(1024)}, f32[768]{0:T(1024)S(1)}, u32[]{:S(2)}) copy-start(f32[768]{0:T(1024)S(1)} %get-tuple-element.61) | copy-start | bytes 9220
  44.3 263.8 %copy-start.57 = (f32[768]{0:T(1024)}, f32[768]{0:T(1024)S(1)}, u32[]{:S(2)}) copy-start(f32[768]{0:T(1024)S(1)} %get-tuple-element.60) | copy-start | bytes 9220
  223.6 13.6 %copy-start.88 = (f32[4,256,3072]{2,1,0:T(8,128)}, f32[4,256,3072]{2,1,0:T(8,128)S(1)}, u32[]{:S(2)}) copy-start(f32[4,256,3072]{2,1,0:T(8,128)S(1)} %fusion.34) | copy-start | bytes 37748740
  237.2 70.8 %copy-start.1 = (f32[4,256,768]{2,1,0:T(8,128)}, f32[4,256,768]{2,1,0:T(8,128)S(1)}, u32[]{:S(2)}) copy-start(f32[4,256,768]{2,1,0:T(8,128)S(1)} %get-tuple-element.72) | copy-start | bytes 9437188
  237.2 70.8 %copy-start.55 = (f32[4,256]{1,0:T(4,128)}, f32[4,256]{1,0:T(4,128)S(1)}, u32[]{:S(2)}) copy-start(f32[4,256]{1,0:T(4,128)S(1)} %broadcast_multiply_fusion.6) | copy-start | bytes 12292
  237.7 41.2 %copy-start.65 = (f32[4,256]{1,0:T(4,128)}, f32[4,256]{1,0:T(4,128)S(1)}, u32[]{:S(2)}) copy-start(f32[4,256]{1,0:T(4,128)S(1)} %multiply_reduce_fusion.12) | copy-start | bytes 12292
  237.7 70.3 %copy-start.59 = (f32[4,256]{1,0:T(4,128)}, f32[4,256]{1,0:T(4,128)S(1)}, u32[]{:S(2)}) copy-start(f32[4,256]{1,0:T(4,128)S(1)} %fusion.80) | copy-start | bytes 12292
  311.8 55.8 %copy-start.19 = (f32[4,256,768]{2,1,0:T(8,128)}, f32[4,256,768]{2,1,0:T(8,128)S(1)}, u32[]{:S(2)}) copy-start(f32[4,256,768]{2,1,0:T(8,128)S(1)} %get-tuple-element.76) | copy-start | bytes 9437188
  335.3 22.7 %copy-start.21 = (f32[4,256,768]{2,1,0:T(8,128)}, f32[4,256,768]{2,1,0:T(8,128)S(1)}, u32[]{:S(2)}) copy-start(f32[4,256,768]{2,1,0:T(8,128)S(1)} %get-tuple-element.78) | copy-start | bytes 9437188
  372.6 16.4 %slice-start = ((s8[12582912]{0:T(1024)(128)(4,1)}), s8[4194304]{0:T(1024)(128)(4,1)S(1)}, s32[]{:S(2)}) async-start(s8[12582912]{0:T(1024)(128)(4,1)} %bitcast.242), calls=%async_computation.7 | async-start | bytes 8388608
  372.7 16.3 %slice-start.1 = ((s8[12582912]{0:T(1024)(128)(4,1)}), s8[4194304]{0:T(1024)(128)(4,1)S(1)}, s32[]{:S(2)}) async-start(s8[12582912]{0:T(1024)(128)(4,1)} %bitcast.242), calls=%async_computation.8 | async-start | bytes 8388608
  379.4 26.3 %copy-start.30 = (bf16[4,12,64,256]{3,2,1,0:T(8,128)(2,1)}, bf16[4,12,64,256]{3,2,1,0:T(8,128)(2,1)S(1)}, u32[]{:S(2)}) copy-start(bf16[4,12,64,256]{3,2,1,0:T(8,128)(2,1)S(1)} %fusion.57) | copy-start | bytes 4718596
  429.6 297.7 %reduce-scatter.3.cloned.1.call-start = ((), (), s32[]{:S(2)}) async-start(), calls=%async_computation.2 | async-start | bytes 15925248 | tf_op jit(solution)/shard_map/reduce_scatter | solution.py:321
  443.9 18.0 %copy-start.37 = (f32[4,256,768]{2,1,0:T(8,128)}, f32[4,256,768]{2,1,0:T(8,128)S(1)}, u32[]{:S(2)}) copy-start(f32[4,256,768]{2,1,0:T(8,128)S(1)} %get-tuple-element.43) | copy-start | bytes 9437188
  444.5 17.4 %copy-start.6 = (f32[4,256,768]{2,1,0:T(8,128)S(1)}, f32[4,256,768]{2,1,0:T(8,128)}, u32[]{:S(2)}) copy-start(f32[4,256,768]{2,1,0:T(8,128)} %copy-done.5) | copy-start | bytes 9437188
  444.5 17.4 %copy-start.62 = (f32[4,256]{1,0:T(4,128)S(1)}, f32[4,256]{1,0:T(4,128)}, u32[]{:S(2)}) copy-start(f32[4,256]{1,0:T(4,128)} %copy-done.61) | copy-start | bytes 12292
  444.5 17.4 %copy-start.72 = (f32[768]{0:T(1024)S(1)}, f32[768]{0:T(1024)}, u32[]{:S(2)}) copy-start(f32[768]{0:T(1024)} %copy-done.71) | copy-start | bytes 9220
  444.5 17.4 %copy-start.74 = (f32[4,256]{1,0:T(4,128)S(1)}, f32[4,256]{1,0:T(4,128)}, u32[]{:S(2)}) copy-start(f32[4,256]{1,0:T(4,128)} %copy-done.73) | copy-start | bytes 12292
  478.0 22.4 %copy-start.33 = (f32[256,512]{1,0:T(8,128)S(1)}, f32[256,512]{1,0:T(8,128)}, u32[]{:S(2)}) copy-start(f32[256,512]{1,0:T(8,128)} %copy-done.32) | copy-start | bytes 1572868
  500.5 22.1 %copy-start.4 = (bf16[4,512,768]{1,2,0:T(8,128)(2,1)S(1)}, bf16[4,512,768]{1,2,0:T(8,128)(2,1)}, u32[]{:S(2)}) copy-start(bf16[4,512,768]{1,2,0:T(8,128)(2,1)} %copy-done.3) | copy-start | bytes 9437188
  584.8 249.8 %all-reduce.2.cloned.1.call-start = ((), (), s32[]{:S(2)}) async-start(), calls=%async_computation.4 | async-start | bytes 7077888 | tf_op jit(solution)/shard_map/psum | solution.py:364
  752.0 34.8 %copy-start.69 = (f32[1,6168]{1,0:T(1,128)S(1)}, f32[1,6168]{1,0:T(1,128)}, u32[]{:S(2)}) copy-start(f32[1,6168]{1,0:T(1,128)} %param.19) | copy-start | bytes 74020
  752.0 34.8 %copy-start.70 = (f32[1,6168]{1,0:T(1,128)S(1)}, f32[1,6168]{1,0:T(1,128)}, u32[]{:S(2)}) copy-start(f32[1,6168]{1,0:T(1,128)} %param.20) | copy-start | bytes 74020
  752.0 52.3 %copy-start.68 = (f32[6168]{0:T(1024)S(1)}, f32[6168]{0:T(1024)}, u32[]{:S(2)}) copy-start(f32[6168]{0:T(1024)} %param.21) | copy-start | bytes 74020
  752.0 53.0 %copy-start.40 = (bf16[4,12,64,512]{3,2,1,0:T(8,128)(2,1)S(1)}, bf16[4,12,64,512]{3,2,1,0:T(8,128)(2,1)}, u32[]{:S(2)}) copy-start(bf16[4,12,64,512]{3,2,1,0:T(8,128)(2,1)} %copy-done.39) | copy-start | bytes 9437188
  (83 other events, 530.0 us)
Sparse Core Ops, SparseCore 0:
  12.7 132.3 all-gather.4
  146.7 127.8 all-gather.6
  429.7 142.2 reduce-scatter.4
  584.9 142.3 reduce-scatter.2
  742.3 92.1 all-reduce.1
where the time goes:
time: 865 us; the launch traced here: 855 us
  matrix products  331 us (38%)
  waiting for transfers between devices  291 us (34%)
  other arithmetic  97.8 us (11%)
  local copies, waits for them, and re-layouts  76 us (9%)
  blocking collectives  42.7 us (5%)
  between operations  15.7 us (2%)
    reduce_scatter x2, waiting for transfers between devices, reduce_layer(): lax.psum_scatter(grad_rows.astype(jnp.bfloat16), 'fsdp', scatter_dimensio...  142 us
    all_gather x2, waiting for transfers between devices, fetch_ahead(): return lax.all_gather(masters_low[layer_index], 'fsdp', axis=0, tiled=True)  129 us
    dot_general x2, matrix products, layer_back(): jnp.einsum('aye,we->ayw', second_branch_gradient_reduced, outer_weight, p...  34.5 us
    dot_general x2, matrix products, layer_back(): jnp.einsum('bqhd,bkhd->bhqk', back_mixed, value_heads, preferred_element_...  31.9 us
    reduce_sum x2, other arithmetic, layer_back(): back_slopes = -jnp.sum(back_scores * distance[None, None], axis=(0, 2, 3))  29.9 us
    slice x2, local copies, waits for them, and re-layouts, shards(): pooled = (hidden_wide[:, 0::2] + hidden_wide[:, 1::2]) * 0.5  29.8 us
    psum x1, blocking collectives, shards(): lax.psum(jnp.concatenate([small_grad_one, small_grad_two]), 'fsdp')  26 us
    dot_general x2, matrix products, layer_ahead(): jnp.einsum('wma,ar->wmr', hidden_activation, outer_weight, preferred_elem...  24.6 us
  transfers between devices with their start and end apart: 5, of which 4 were waited for; matrix products, arithmetic and copies ran while one was open for 37% of the time, Pallas kernels for 0%

commit v1 on v0

v1 whole, which is shorter than its diff:
```python
import functools

import jax
import jax.numpy as jnp
from jax import lax
from jax.experimental import pallas as pl
from jax.experimental.pallas import tpu as pltpu
from jax.sharding import PartitionSpec as P

STEP = 10


EPS_NORM = 1e-06
MASK_FILL = -1e30
BETA_ONE = 0.9
BETA_TWO = 0.999
ADAM_EPS = 1e-08
DECAY_RATE = 0.01
INNER_RATE = 0.03
SMALL_RATE = 0.6
OUTER_RATE = 0.7
MOMENTUM = 0.9
GELU_COEF = 0.7978845608028654
GELU_CUBE = 0.044715

BF = jnp.bfloat16
F32 = jnp.float32
VMEM_LIMIT = 60 * 1024 * 1024


def dot_nn(left, right):
    return lax.dot_general(left, right, (((1,), (0,)), ((), ())), preferred_element_type=F32)


def dot_nt(left, right):
    return lax.dot_general(left, right, (((1,), (1,)), ((), ())), preferred_element_type=F32)


def dot_tn(left, right):
    return lax.dot_general(left, right, (((0,), (0,)), ((), ())), preferred_element_type=F32)


def norm_parts(total):
    center = total - jnp.mean(total, axis=-1, keepdims=True)
    inverse = lax.rsqrt(jnp.mean(center * center, axis=-1, keepdims=True) + EPS_NORM)
    return center * inverse, inverse


def norm_back(grad, unit, inverse, gain):
    scaled = grad * gain
    lead = jnp.mean(scaled, axis=-1, keepdims=True)
    along = jnp.mean(scaled * unit, axis=-1, keepdims=True)
    return inverse * (scaled - lead - unit * along)


def fill_distance(dist_ref, key_step, query_step):
    shape = dist_ref.shape
    keys = lax.broadcasted_iota(jnp.int32, shape, 0) * key_step
    queries = lax.broadcasted_iota(jnp.int32, shape, 1) * query_step
    dist_ref[...] = jnp.abs(queries - keys).astype(F32)


def fill_mask(mask_ref, key_step, length):
    keys = lax.broadcasted_iota(jnp.int32, mask_ref.shape, 0) * key_step
    mask_ref[...] = jnp.where(keys < length, 0.0, MASK_FILL)


def pick_rows(pair_rows, which):
    half = pair_rows.shape[0] // 2
    zero = jnp.zeros((half, pair_rows.shape[1]), pair_rows.dtype)
    if which == 0:
        return jnp.concatenate([pair_rows[:half], zero], axis=0)
    return jnp.concatenate([zero, pair_rows[half:]], axis=0)


def lane_half(width, which):
    lanes = lax.broadcasted_iota(jnp.int32, (1, width), 1)
    inside = lanes < width // 2 if which == 0 else lanes >= width // 2
    return jnp.where(inside, 1.0, 0.0).astype(BF)


def pair_matrix(queries, keys, value, by_query):
    shape = (queries, keys) if by_query else (keys, queries)
    query_index = lax.broadcasted_iota(jnp.int32, shape, 0 if by_query else 1)
    key_index = lax.broadcasted_iota(jnp.int32, shape, 1 if by_query else 0)
    offset = key_index - 2 * query_index
    return jnp.where((offset == 0) | (offset == 1), value, 0.0).astype(BF)


def weight_copies(weight_hbm, weight_ref, sems, cuts):
    return [
        pltpu.make_async_copy(
            weight_hbm.at[pl.ds(cuts[index], cuts[index + 1] - cuts[index])],
            weight_ref.at[pl.ds(cuts[index], cuts[index + 1] - cuts[index])],
            sems.at[index],
        )
        for index in range(len(cuts) - 1)
    ]


def ahead_kernel(
    is_first,
    head_count,
    lengths_ref,
    slopes_ref,
    x_ref,
    gains_ref,
    weight_hbm,
    query_out,
    key_out,
    value_out,
    lse_out,
    att_out,
    total_one_out,
    hidden_out,
    slope_out,
    total_two_out,
    layer_out,
    weight_ref,
    dist_ref,
    mask_ref,
    query_t,
    value_t,
    att_t,
    sems,
):
    step = pl.program_id(0)
    width = weight_ref.shape[1]
    inner = (weight_ref.shape[0] - 4 * width) // 2
    queries, keys = query_out.shape[1], key_out.shape[1]
    head = width // head_count
    cuts = [0, width, 3 * width, 4 * width, 4 * width + inner, 4 * width + 2 * inner]
    copies = weight_copies(weight_hbm, weight_ref, sems, cuts)
    key_step = 1 if is_first else 2

    @pl.when(step == 0)
    def _():
        for copy in copies:
            copy.start()
        fill_distance(dist_ref, key_step, 2)

    def need(index):
        @pl.when(step == 0)
        def _():
            copies[index].wait()

    fill_mask(mask_ref, key_step, lengths_ref[step])
    if is_first:
        memory_low = x_ref[0]
        residual = dot_nn(pair_matrix(queries, keys, 0.5, True), memory_low)
        query_low = residual.astype(BF)
    else:
        residual = x_ref[0]
        query_low = residual.astype(BF)
        memory_low = query_low
    need(0)
    query_rows = dot_nn(query_low, weight_ref[0:width]).astype(BF)
    query_out[0] = query_rows
    query_t[...] = (query_rows.astype(F32) * float(head) ** (-0.5)).T.astype(BF)
    need(1)
    key_out[0] = dot_nn(memory_low, weight_ref[width : 2 * width]).astype(BF)
    value_rows = dot_nn(memory_low, weight_ref[2 * width : 3 * width]).astype(BF)
    value_out[0] = value_rows
    value_t[...] = value_rows.astype(F32).T.astype(BF)

    def pair_step(pair, carry):
        start = pl.multiple_of(pair * 2 * head, 2 * head)
        key_pair = key_out[0, :, pl.ds(start, 2 * head)]
        query_pair = query_t[pl.ds(start, 2 * head), :]
        for which in range(2):
            index = 2 * pair + which
            scores = dot_nn(key_pair, pick_rows(query_pair, which))
            scores = scores - slopes_ref[index] * dist_ref[...] + mask_ref[...]
            peak = jnp.max(scores, axis=0, keepdims=True)
            lifted = jnp.exp(scores - peak)
            total = jnp.sum(lifted, axis=0, keepdims=True)
            shares = (lifted * (1.0 / total)).astype(BF)
            rows = pl.ds(start + which * head, head)
            mixed = dot_nn(value_t[rows, :], shares)
            att_t[rows, :] = mixed
            lse_out[0, pl.ds(index, 1), :] = peak + jnp.log(total)
        return carry

    lax.fori_loop(0, head_count // 2, pair_step, 0)
    attended = att_t[...].T.astype(BF)
    att_out[0] = attended
    need(2)
    total_one = residual + dot_nn(attended, weight_ref[3 * width : 4 * width])
    total_one_out[0] = total_one
    unit, _ = norm_parts(total_one)
    normed = unit * gains_ref[0:1] + gains_ref[1:2]
    normed_low = normed.astype(BF)
    need(3)
    need(4)
    total_two = normed
    for chunk in range(inner // width):
        inner_rows = pl.ds(4 * width + chunk * width, width)
        outer_rows = pl.ds(4 * width + inner + chunk * width, width)
        pre = dot_nt(normed_low, weight_ref[inner_rows, :])
        square = pre * pre
        bend = jnp.tanh(pre * (GELU_COEF + (GELU_COEF * GELU_CUBE) * square))
        half = 0.5 + 0.5 * bend
        hidden = (pre * half).astype(BF)
        steep = half + (0.5 * pre) * (1.0 - bend * bend) * (
            GELU_COEF + (3.0 * GELU_COEF * GELU_CUBE) * square
        )
        columns = pl.ds(chunk * width, width)
        hidden_out[0, :, columns] = hidden
        slope_out[0, :, columns] = steep.astype(BF)
        total_two = total_two + dot_nn(hidden, weight_ref[outer_rows, :])
    total_two_out[0] = total_two
    unit_two, _ = norm_parts(total_two)
    result = unit_two * gains_ref[2:3] + gains_ref[3:4]
    layer_out[0] = result.astype(layer_out.dtype)


def layer_ahead(is_first, x, lengths, slopes, gains, weight_full, out_dtype):
    batch, memory_length, width = x.shape
    queries = memory_length // 2 if is_first else memory_length
    keys = memory_length
    head_count = slopes.shape[0]
    rows = weight_full.shape[0]
    inner = (rows - 4 * width) // 2
    head_rows = -(-head_count // 8) * 8

    def block(length, size):
        return pl.BlockSpec((1, length, size), lambda i, *_: (i, 0, 0))

    def shape(length, size, dtype):
        return jax.ShapeDtypeStruct((batch, length, size), dtype)

    outs = [
        (queries, width, BF),
        (keys, width, BF),
        (keys, width, BF),
        (head_rows, queries, F32),
        (queries, width, BF),
        (queries, width, F32),
        (queries, inner, BF),
        (queries, inner, BF),
        (queries, width, F32),
        (queries, width, out_dtype),
    ]
    flops = 2 * batch * width * (
        2 * queries * width + 2 * keys * width + 2 * queries * inner + 2 * queries * keys
    )
    return pl.pallas_call(
        functools.partial(ahead_kernel, is_first, head_count),
        grid_spec=pltpu.PrefetchScalarGridSpec(
            num_scalar_prefetch=2,
            grid=(batch,),
            in_specs=[
                block(memory_length, width),
                pl.BlockSpec((4, width), lambda i, *_: (0, 0)),
                pl.BlockSpec(memory_space=pl.ANY),
            ],
            out_specs=[block(length, size) for length, size, _ in outs],
            scratch_shapes=[
                pltpu.VMEM((rows, width), BF),
                pltpu.VMEM((keys, queries), F32),
                pltpu.VMEM((keys, queries), F32),
                pltpu.VMEM((width, queries), BF),
                pltpu.VMEM((width, keys), BF),
                pltpu.VMEM((width, queries), F32),
                pltpu.SemaphoreType.DMA((5,)),
            ],
        ),
        out_shape=[shape(*out) for out in outs],
        compiler_params=pltpu.CompilerParams(vmem_limit_bytes=VMEM_LIMIT),
        cost_estimate=pl.CostEstimate(
            flops=flops, bytes_accessed=rows * width * 2 + 30000000, transcendentals=0
        ),
        name="layer_ahead",
    )(lengths, slopes, x, gains, weight_full)


def back_kernel(
    is_first,
    head_count,
    lengths_ref,
    slopes_ref,
    grad_ref,
    total_two_ref,
    total_one_ref,
    slope_ref,
    query_ref,
    key_ref,
    value_ref,
    att_ref,
    lse_ref,
    gains_ref,
    weight_hbm,
    two_out,
    pre_out,
    normed_out,
    one_out,
    query_grad_out,
    key_grad_out,
    value_grad_out,
    input_out,
    gains_out,
    slopes_out,
    weight_ref,
    dist_ref,
    mask_ref,
    query_t,
    key_t,
    mixed_t,
    mixed_rows,
    delta_ref,
    query_grad_t,
    sems,
):
    step = pl.program_id(0)
    width = weight_ref.shape[1]
    inner = (weight_ref.shape[0] - 4 * width) // 2
    queries, keys = query_ref.shape[1], key_ref.shape[1]
    head = width // head_count
    cuts = [0, 3 * width, 4 * width, 4 * width + inner, 4 * width + 2 * inner]
    copies = weight_copies(weight_hbm, weight_ref, sems, cuts)
    key_step = 1 if is_first else 2
    scale = float(head) ** (-0.5)

    @pl.when(step == 0)
    def _():
        for index in (3, 2, 1, 0):
            copies[index].start()
        fill_distance(dist_ref, key_step, 2)
        gains_out[...] = jnp.zeros_like(gains_out)
        slopes_out[...] = jnp.zeros_like(slopes_out)

    def need(index):
        @pl.when(step == 0)
        def _():
            copies[index].wait()

    fill_mask(mask_ref, key_step, lengths_ref[step])
    query_t[...] = (query_ref[0].astype(F32) * scale).T.astype(BF)
    key_t[...] = key_ref[0].astype(F32).T.astype(BF)

    grad = grad_ref[0].astype(F32)
    unit_two, inverse_two = norm_parts(total_two_ref[0])
    gains_out[2:3] += jnp.sum(grad * unit_two, axis=0, keepdims=True)
    gains_out[3:4] += jnp.sum(grad, axis=0, keepdims=True)
    back_two = norm_back(grad, unit_two, inverse_two, gains_ref[2:3])
    two_low = back_two.astype(BF)
    two_out[0] = two_low
    need(3)
    need(2)
    back_normed = back_two
    for chunk in range(inner // width):
        inner_rows = pl.ds(4 * width + chunk * width, width)
        outer_rows = pl.ds(4 * width + inner + chunk * width, width)
        columns = pl.ds(chunk * width, width)
        back_hidden = dot_nt(two_low, weight_ref[outer_rows, :])
        pre_grad = (back_hidden * slope_ref[0, :, columns].astype(F32)).astype(BF)
        pre_out[0, :, columns] = pre_grad
        back_normed = back_normed + dot_nn(pre_grad, weight_ref[inner_rows, :])
    unit_one, inverse_one = norm_parts(total_one_ref[0])
    normed_out[0] = (unit_one * gains_ref[0:1] + gains_ref[1:2]).astype(BF)
    gains_out[0:1] += jnp.sum(back_normed * unit_one, axis=0, keepdims=True)
    gains_out[1:2] += jnp.sum(back_normed, axis=0, keepdims=True)
    back_one = norm_back(back_normed, unit_one, inverse_one, gains_ref[0:1])
    one_low = back_one.astype(BF)
    one_out[0] = one_low
    need(1)
    back_mixed = dot_nt(one_low, weight_ref[3 * width : 4 * width])
    mixed_low = back_mixed.astype(BF)
    mixed_rows[...] = mixed_low
    mixed_wide = mixed_low.astype(F32).T
    mixed_t[...] = mixed_wide.astype(BF)
    product = mixed_wide * att_ref[0].astype(F32).T
    delta_ref[...] = jnp.sum(product.reshape(head_count, head, queries), axis=1)

    def pair_step(pair, carry):
        start = pl.multiple_of(pair * 2 * head, 2 * head)
        lanes = pl.ds(start, 2 * head)
        key_pair = key_ref[0, :, lanes]
        value_pair = value_ref[0, :, lanes]
        query_pair = query_ref[0, :, lanes]
        mixed_pair = mixed_rows[:, lanes]
        query_pair_t = query_t[lanes, :]
        mixed_pair_t = mixed_t[lanes, :]
        key_grad = jnp.zeros((keys, 2 * head), F32)
        value_grad = jnp.zeros((keys, 2 * head), F32)
        for which in range(2):
            index = 2 * pair + which
            half = lane_half(2 * head, which)
            scores = dot_nn(key_pair, pick_rows(query_pair_t, which))
            scores = scores - slopes_ref[index] * dist_ref[...] + mask_ref[...]
            shares = jnp.exp(scores - lse_ref[0, pl.ds(index, 1), :])
            back_shares = dot_nn(value_pair, pick_rows(mixed_pair_t, which))
            back_scores = shares * (back_shares - delta_ref[pl.ds(index, 1), :])
            slopes_out[pl.ds(index, 1), :] += jnp.sum(
                back_scores * dist_ref[...], axis=0, keepdims=True
            )
            scores_low = back_scores.astype(BF)
            value_grad = value_grad + dot_nn(shares.astype(BF), mixed_pair * half)
            key_grad = key_grad + dot_nn(scores_low, query_pair * half)
            rows = pl.ds(start + which * head, head)
            query_grad_t[rows, :] = dot_nn(key_t[rows, :], scores_low)
        key_grad_out[0, :, lanes] = (key_grad * scale).astype(BF)
        value_grad_out[0, :, lanes] = value_grad.astype(BF)
        return carry

    lax.fori_loop(0, head_count // 2, pair_step, 0)
    query_grad = (query_grad_t[...] * scale).T.astype(BF)
    query_grad_out[0] = query_grad
    need(0)
    back_query = back_one + dot_nt(query_grad, weight_ref[0:width])
    back_memory = dot_nt(key_grad_out[0], weight_ref[width : 2 * width]) + dot_nt(
        value_grad_out[0], weight_ref[2 * width : 3 * width]
    )
    if is_first:
        spread = pair_matrix(queries, keys, 1.0, False)
        half_grad = back_query * 0.5
        upper = half_grad.astype(BF)
        lower = (half_grad - upper.astype(F32)).astype(BF)
        back_memory = back_memory + dot_nn(spread, upper) + dot_nn(spread, lower)
        input_out[0] = back_memory
    else:
        input_out[0] = back_query + back_memory


def layer_back(is_first, grad, kept, lengths, slopes, gains, weight_full):
    (query_rows, key_rows, value_rows, lse, attended, total_one, steep, total_two) = kept
    batch, queries, width = query_rows.shape
    keys = key_rows.shape[1]
    head_count = slopes.shape[0]
    rows = weight_full.shape[0]
    inner = (rows - 4 * width) // 2
    head_rows = lse.shape[1]

    def block(length, size):
        return pl.BlockSpec((1, length, size), lambda i, *_: (i, 0, 0))

    def shape(length, size, dtype):
        return jax.ShapeDtypeStruct((batch, length, size), dtype)

    outs = [
        (queries, width, BF),
        (queries, inner, BF),
        (queries, width, BF),
        (queries, width, BF),
        (queries, width, BF),
        (keys, width, BF),
        (keys, width, BF),
        (keys, width, F32),
    ]
    flops = 2 * batch * width * (
        2 * queries * width + 2 * keys * width + 2 * queries * inner + 5 * queries * keys
    )
    return pl.pallas_call(
        functools.partial(back_kernel, is_first, head_count),
        grid_spec=pltpu.PrefetchScalarGridSpec(
            num_scalar_prefetch=2,
            grid=(batch,),
            in_specs=[
                block(queries, width),
                block(queries, width),
                block(queries, width),
                block(queries, inner),
                block(queries, width),
                block(keys, width),
                block(keys, width),
                block(queries, width),
                block(head_rows, queries),
                pl.BlockSpec((4, width), lambda i, *_: (0, 0)),
                pl.BlockSpec(memory_space=pl.ANY),
            ],
            out_specs=[block(length, size) for length, size, _ in outs]
            + [
                pl.BlockSpec((4, width), lambda i, *_: (0, 0)),
                pl.BlockSpec((head_rows, queries), lambda i, *_: (0, 0)),
            ],
            scratch_shapes=[
                pltpu.VMEM((rows, width), BF),
                pltpu.VMEM((keys, queries), F32),
                pltpu.VMEM((keys, queries), F32),
                pltpu.VMEM((width, queries), BF),
                pltpu.VMEM((width, keys), BF),
                pltpu.VMEM((width, queries), BF),
                pltpu.VMEM((queries, width), BF),
                pltpu.VMEM((head_count, queries), F32),
                pltpu.VMEM((width, queries), F32),
                pltpu.SemaphoreType.DMA((4,)),
            ],
        ),
        out_shape=[shape(*out) for out in outs]
        + [
            jax.ShapeDtypeStruct((4, width), F32),
            jax.ShapeDtypeStruct((head_rows, queries), F32),
        ],
        compiler_params=pltpu.CompilerParams(vmem_limit_bytes=VMEM_LIMIT),
        cost_estimate=pl.CostEstimate(
            flops=flops, bytes_accessed=rows * width * 2 + 40000000, transcendentals=0
        ),
        name="layer_back",
    )(
        lengths,
        slopes,
        grad,
        total_two,
        total_one,
        steep,
        query_rows,
        key_rows,
        value_rows,
        attended,
        lse,
        gains,
        weight_full,
    )


def weight_product(left, right):
    return lax.dot_general(
        left, right, (((0, 1), (0, 1)), ((), ())), preferred_element_type=F32
    )


def matrix_gradient(query_low, memory_low, attended, hidden, back):
    (two_low, pre_grad, normed_low, one_low, query_grad, key_grad, value_grad) = back
    return jnp.concatenate(
        [
            weight_product(query_low, query_grad),
            weight_product(memory_low, key_grad),
            weight_product(memory_low, value_grad),
            weight_product(attended, one_low),
            weight_product(pre_grad, normed_low),
            weight_product(hidden, two_low),
        ],
        axis=0,
    )


def adam_step(master, gradient, first_mom, second_mom, rate):
    first_new = BETA_ONE * first_mom + (1.0 - BETA_ONE) * gradient
    second_new = BETA_TWO * second_mom + (1.0 - BETA_TWO) * gradient * gradient
    first_hat = first_new / (1.0 - BETA_ONE**STEP)
    second_hat = second_new / (1.0 - BETA_TWO**STEP)
    inner_move = rate * (first_hat / (jnp.sqrt(second_hat) + ADAM_EPS) + DECAY_RATE * master)
    return (first_new, second_new, inner_move)


def outer_step(master, moves_sum, momentum_old, group_count):
    mean_move = moves_sum / group_count
    momentum_new = MOMENTUM * momentum_old + mean_move
    return (mean_move, momentum_new, master - OUTER_RATE * (mean_move + MOMENTUM * momentum_new))


def shards(
    hidden_in,
    lengths,
    out_grad,
    weights,
    weight_m,
    weight_v,
    outer_mom,
    small,
    small_m,
    small_v,
    small_mom,
):
    width = weights.shape[2]
    part_size = small.shape[0] // 2
    masters_low = weights.astype(BF)

    def fetch(layer_index):
        return lax.all_gather(masters_low[layer_index], "fsdp", axis=0, tiled=True)

    def reduce_layer(grad_rows):
        return lax.psum_scatter(
            grad_rows.astype(BF), "fsdp", scatter_dimension=0, tiled=True
        ).astype(F32)

    gains = []
    slopes = []
    for layer in range(2):
        part = small[layer * part_size : (layer + 1) * part_size]
        gains.append(part[: 4 * width].reshape(4, width))
        slopes.append(part[4 * width :])

    matrix_one = fetch(0)
    matrix_two = fetch(1)
    (q1, k1, v1, lse1, att1, one1, hid1, steep1, two1, first_out) = layer_ahead(
        True, hidden_in, lengths, slopes[0], gains[0], matrix_one, F32
    )
    (q2, k2, v2, lse2, att2, one2, hid2, steep2, two2, block_out) = layer_ahead(
        False, first_out, lengths, slopes[1], gains[1], matrix_two, BF
    )
    back_two = layer_back(
        False,
        out_grad,
        (q2, k2, v2, lse2, att2, one2, steep2, two2),
        lengths,
        slopes[1],
        gains[1],
        matrix_two,
    )
    first_low = first_out.astype(BF)
    shard_two = reduce_layer(matrix_gradient(first_low, first_low, att2, hid2, back_two[:7]))
    back_one = layer_back(
        True,
        back_two[7],
        (q1, k1, v1, lse1, att1, one1, steep1, two1),
        lengths,
        slopes[0],
        gains[0],
        matrix_one,
    )
    input_grad = back_one[7]
    hidden_wide = hidden_in.astype(F32)
    pooled_low = ((hidden_wide[:, 0::2] + hidden_wide[:, 1::2]) * 0.5).astype(BF)
    shard_one = reduce_layer(matrix_gradient(pooled_low, hidden_in, att1, hid1, back_one[:7]))
    grad_shard = jnp.stack([shard_one, shard_two])
    head_count = slopes[0].shape[0]
    small_parts = []
    for back in (back_one, back_two):
        small_parts += [back[8].reshape(-1), -jnp.sum(back[9][:head_count], axis=1)]
    small_grad = lax.psum(jnp.concatenate(small_parts), "fsdp")
    weight_first, weight_second, weight_move = adam_step(
        weights, grad_shard[None], weight_m, weight_v, INNER_RATE
    )
    small_first, small_second, small_move = adam_step(
        small, small_grad[None], small_m, small_v, SMALL_RATE
    )
    weight_sum, small_sum = (
        lax.psum(weight_move[0].astype(BF), "group").astype(F32),
        lax.psum(small_move[0].astype(BF), "group").astype(F32),
    )
    group_count = lax.axis_size("group")
    weight_mean, weight_mom, weight_new = outer_step(weights, weight_sum, outer_mom, group_count)
    small_mean, small_momentum, small_after = outer_step(small, small_sum, small_mom, group_count)
    return (
        block_out,
        input_grad,
        weight_new,
        weight_new.astype(BF),
        weight_first,
        weight_second,
        weight_mean,
        weight_mom,
        small_after,
        small_first,
        small_second,
        small_mean,
        small_momentum,
    )


def solution(mesh):
    in_specs = (
        P(("group", "fsdp"), None, None),
        P(("group", "fsdp")),
        P(("group", "fsdp"), None, None),
        P(None, "fsdp", None),
        P("group", None, "fsdp", None),
        P("group", None, "fsdp", None),
        P(None, "fsdp", None),
        P(),
        P("group", None),
        P("group", None),
        P(),
    )
    out_specs = (
        P(("group", "fsdp"), None, None),
        P(("group", "fsdp"), None, None),
        P(None, "fsdp", None),
        P(None, "fsdp", None),
        P("group", None, "fsdp", None),
        P("group", None, "fsdp", None),
        P(None, "fsdp", None),
        P(None, "fsdp", None),
        P(),
        P("group", None),
        P("group", None),
        P(),
        P(),
    )
    return jax.shard_map(shards, mesh=mesh, in_specs=in_specs, out_specs=out_specs, check_vma=False)
```

time: 865 us -> 877 us (1.014)
  matrix products: 331 us -> 54.6 us
  Pallas kernels: 0 us -> 212 us
  waiting for transfers between devices: 291 us -> 488 us
  other arithmetic: 97.8 us -> 32.4 us
  local copies, waits for them, and re-layouts: 76 us -> 27.3 us
    dot_general x48 -> x12, matrix products: 331 us -> 54.6 us  [weight_product(): lax.dot_general(left, right, (((0, 1), (0, 1)), ((), ())), preferred_elem...]
    pallas_call x0 -> x4, Pallas kernels: none -> 212 us  [the longest x2 107 us: layer_ahead(): pl.pallas_call(functools.partial(ahead_kernel, is_first, head_count), gri...]
    reduce_scatter x2, waiting for transfers between devices: 142 us -> 259 us  [reduce_layer(): lax.psum_scatter(grad_rows.astype(BF), 'fsdp', scatter_dimension=0, tiled...]
    reduce_sum x12 -> x2, other arithmetic: 55.8 us -> 0.22 us  [shards(): small_parts += [back[8].reshape(-1), -jnp.sum(back[9][:head_count], axis=1)]]
    all_gather x2, waiting for transfers between devices: 129 us -> 180 us  [fetch(): return lax.all_gather(masters_low[layer_index], 'fsdp', axis=0, tiled=True)]
    psum x1, waiting for transfers between devices: 19.1 us -> 47.6 us  [shards(): lax.psum(weight_move[0].astype(BF), 'group').astype(F32)]
    convert_element_type x8 -> x0, local copies, waits for them, and re-layouts: 21.7 us -> none  [the longest x2 7.24 us: layer_ahead(): every_value_row = jnp.einsum('zho,og->zhg', memory_rows_reduced, value_we...]
    slice x5, local copies, waits for them, and re-layouts: 32.6 us -> 22.3 us  [the longest x1 9.87 us: shards(): hidden_wide[:, 0::2] + hidden_wide[:, 1::2]]
  transfers between devices with their start and end apart: 5 -> 5, of which waited for: 4 -> 5; matrix products, arithmetic and copies ran while one was open for 37% -> 6% of each run, Pallas kernels for 0% -> 7%
where the time goes in v1:
time: 877 us; the launch traced here: 871 us
  waiting for transfers between devices  488 us (56%)
  Pallas kernels  212 us (24%)
  matrix products  54.6 us (6%)
  blocking collectives  42.3 us (5%)
  other arithmetic  32.4 us (4%)
  local copies, waits for them, and re-layouts  27.3 us (3%)
  between operations  14.5 us (2%)
    reduce_scatter x2, waiting for transfers between devices, reduce_layer(): lax.psum_scatter(grad_rows.astype(BF), 'fsdp', scatter_dimension=0, tiled...  259 us
    all_gather x2, waiting for transfers between devices, fetch(): return lax.all_gather(masters_low[layer_index], 'fsdp', axis=0, tiled=True)  180 us
    pallas_call x2, Pallas kernels, layer_ahead(): pl.pallas_call(functools.partial(ahead_kernel, is_first, head_count), gri...  107 us
    pallas_call x2, Pallas kernels, layer_back(): pl.pallas_call(functools.partial(back_kernel, is_first, head_count), grid...  105 us
    dot_general x12, matrix products, weight_product(): lax.dot_general(left, right, (((0, 1), (0, 1)), ((), ())), preferred_elem...  54.6 us
    psum x1, waiting for transfers between devices, shards(): lax.psum(weight_move[0].astype(BF), 'group').astype(F32)  47.6 us
    psum x1, blocking collectives, shards(): small_grad = lax.psum(jnp.concatenate(small_parts), 'fsdp')  26 us
  transfers between devices with their start and end apart: 5, of which 5 were waited for; matrix products, arithmetic and copies ran while one was open for 6% of the time, Pallas kernels for 7%

profile of v1, /device:TPU:0, one launch (start us, length us, event | category | flops | bytes accessed | tf_op | source)
XLA Modules:
  0.0 870.9 jit_solution(8030854277638563920)
XLA Ops:
  7.2 3.4 convert_element_type.37
  10.6 2.0 fusion.27
  13.4 1.1 copy-done
  14.5 9.9 %slice.42 = f32[4,256,768]{2,1,0:T(8,128)} slice(bf16[4,512,768]{2,1,0:T(8,128)(2,1)S(1)} %copy-done), slice={[0:4:1], [0:512:2], [0:768:1]} | slice | bytes 6291456 | tf_op jit(solution)/shard_map/slice | solution.py:614
  24.4 9.8 %slice.43 = f32[4,256,768]{2,1,0:T(8,128)} slice(bf16[4,512,768]{2,1,0:T(8,128)(2,1)S(1)} %copy-done), slice={[0:4:1], [1:512:2], [0:768:1]} | slice | bytes 6291456 | tf_op jit(solution)/shard_map/slice | solution.py:614
  36.0 109.1 %all-gather.5.cloned.1.call-done = bf16[1,9216,768]{2,1,0:T(8,128)(2,1)} async-done(((bf16[1,1152,768]{2,1,0:T(8,128)(2,1)}), bf16[1,9216,768]{2,1,0:T(8,128)(2,1)}) %all-gather.5.cloned.1.call-update) | async-done | bytes 14155792 | tf_op jit(solution)/shard_map/all_gather | solution.py:570
  145.1 59.1 %layer_ahead.2 = (bf16[4,256,768]{2,1,0:T(8,128)(2,1)}, bf16[4,512,768]{2,1,0:T(8,128)(2,1)}, bf16[4,512,768]{2,1,0:T(8,128)(2,1)}, f32[4,16,256]{2,1,0:T(8,128)...) custom-call(s32[4]{0:T(128)} %lengths_ref.7, ...), custom_call_target="tpu_custom_call" | custom-call | flops 18522046464 | bytes 44155776 | tf_op jit(solution)/shard_map/layer_ahead/pallas_call | solution.py:247
  204.3 71.0 %all-gather.7.cloned.1.call-done = bf16[1,9216,768]{2,1,0:T(8,128)(2,1)} async-done(((bf16[1,1152,768]{2,1,0:T(8,128)(2,1)}), bf16[1,9216,768]{2,1,0:T(8,128)(2,1)}) %all-gather.7.cloned.1.call-update) | async-done | bytes 14155792 | tf_op jit(solution)/shard_map/all_gather | solution.py:570
  275.2 47.4 %layer_ahead.3 = (bf16[4,256,768]{2,1,0:T(8,128)(2,1)}, bf16[4,256,768]{2,1,0:T(8,128)(2,1)}, bf16[4,256,768]{2,1,0:T(8,128)(2,1)}, f32[4,16,256]{2,1,0:T(8,128)...) custom-call(s32[4]{0:T(128)} %lengths_ref.7, ...), custom_call_target="tpu_custom_call" | custom-call | flops 15300820992 | bytes 44155776 | tf_op jit(solution)/shard_map/layer_ahead/pallas_call | solution.py:247
  322.6 45.6 %layer_back.2 = (bf16[4,256,768]{2,1,0:T(8,128)(2,1)}, bf16[4,256,3072]{2,1,0:T(8,128)(2,1)}, bf16[4,256,768]{2,1,0:T(8,128)(2,1)}, bf16[4,256,768]{2,1,0:T(8,12...) custom-call(s32[4]{0:T(128)} %lengths_ref.7, ...), custom_call_target="tpu_custom_call" | custom-call | flops 16508780544 | bytes 54155776 | tf_op jit(solution)/shard_map/layer_back/pallas_call | solution.py:453
  368.3 59.6 %layer_back.3 = (bf16[4,256,768]{2,1,0:T(8,128)(2,1)}, bf16[4,256,3072]{2,1,0:T(8,128)(2,1)}, bf16[4,256,768]{2,1,0:T(8,128)(2,1)}, bf16[4,256,768]{2,1,0:T(8,12...) custom-call(s32[4]{0:T(128)} %lengths_ref.7, ...), custom_call_target="tpu_custom_call" | custom-call | flops 20937965568 | bytes 54155776 | tf_op jit(solution)/shard_map/layer_back/pallas_call | solution.py:453
  428.0 5.0 fusion.10
  433.0 3.7 fusion.17
  436.7 3.7 fusion.19
  440.4 2.4 fusion.11
  442.9 6.9 fusion.4
  449.8 7.1 fusion.5
  457.0 1.8 copy-done.12
  458.9 4.0 fusion.12
  462.9 2.5 fusion.13
  465.4 2.5 fusion.14
  467.9 2.5 fusion.15
  470.5 7.2 fusion.6
  477.7 6.9 fusion.7
  484.7 114.8 %reduce-scatter.3.cloned.1.call-done = bf16[1152,768]{1,0:T(8,128)(2,1)} async-done(((bf16[9216,768]{1,0:T(8,128)(2,1)}), bf16[1152,768]{1,0:T(8,128)(2,1)}) %reduce-scatter.3.cloned.1.call-update) | async-done | bytes 1769488 | tf_op jit(solution)/shard_map/reduce_scatter | solution.py:573
  599.4 144.6 %reduce-scatter.5.cloned.1.call-done = bf16[1152,768]{1,0:T(8,128)(2,1)} async-done(((bf16[9216,768]{1,0:T(8,128)(2,1)}), bf16[1152,768]{1,0:T(8,128)(2,1)}) %reduce-scatter.5.cloned.1.call-update) | async-done | bytes 1769488 | tf_op jit(solution)/shard_map/reduce_scatter | solution.py:573
  744.1 14.4 %fusion.8 = (bf16[2,1152,768]{2,1,0:T(8,128)(2,1)}, f32[1,2,1152,768]{3,2,1,0:T(8,128)}, f32[1,2,1152,768]{3,2,1,0:T(8,128)}) fusion(f32[2,1152,768]{2,1,0:T(8,128)} %param.14, bf16[1,1,1152,768]{3,2,1,0:T(8,128)(2,1)} %bitcast.95, bf16[1,1,1152,768]{3,2,1,0:T(8,128)(2,1)} %bitcast.94, f32[1,2,1152,768]{3,2,1,0:T(8,128)} %param.15, f32[1,2,1152,768]{3,2,1,0:T(8,128)} %param.16), kind=kLoop, calls=%fused_computation.19 | loop fusion | flops 30081024 | bytes 42467328 | tf_op jit(solution)/shard_map/convert_element_type | solution.py:629
  759.6 26.0 %psum.22 = f32[6168]{0:T(1024)S(1)} all-reduce(f32[6168]{0:T(1024)S(1)} %concatenate.34), channel_id=1, replica_groups=mesh['group'=4,'fsdp'=8] {'fsdp'}, use_global_device_ids=true, to_apply=%region_5.0 | all-reduce | flops 6168 | bytes 49344 | tf_op jit(solution)/shard_map/psum | solution.py:621
  785.6 0.8 convert_reduce_fusion
  786.4 16.3 %psum.23 = bf16[6168]{0:T(1024)(128)(2,1)S(1)} all-reduce(bf16[6168]{0:T(1024)(128)(2,1)S(1)} %get-tuple-element.96), channel_id=1, replica_groups=mesh['group'=4,'fsdp'=8] {'group'}, use_global_device_ids=true, to_apply=%region_6.0 | all-reduce | flops 6168 | bytes 24672 | tf_op jit(solution)/shard_map/psum | solution.py:630
  803.3 47.6 %all-reduce.2.cloned.1.call-done = bf16[2,1152,768]{2,1,0:T(8,128)(2,1)} async-done(((bf16[2,1152,768]{2,1,0:T(8,128)(2,1)}), bf16[2,1152,768]{2,1,0:T(8,128)(2,1)}) %all-reduce.2.cloned.1.call-update) | async-done | bytes 3538960 | tf_op jit(solution)/shard_map/psum | solution.py:629
  851.0 13.0 %fusion.24 = (bf16[2,1152,768]{2,1,0:T(8,128)(2,1)}, f32[2,1152,768]{2,1,0:T(8,128)}, f32[2,1152,768]{2,1,0:T(8,128)}, f32[2,1152,768]{2,1,0:T(8,128)}) fusion(f32[2,1152,768]{2,1,0:T(8,128)} %param.14, f32[2,1152,768]{2,1,0:T(8,128)} %param.17, bf16[2,1152,768]{2,1,0:T(8,128)(2,1)} %all-reduce.2.cloned.1.call-done), kind=kLoop, calls=%fused_computation.55 | loop fusion | flops 15925248 | bytes 42467328 | tf_op jit(solution)/shard_map/convert_element_type | solution.py:639
  (92 shorter events, 4.6 us)
Async XLA Ops:
  7.2 137.9 %all-gather.5.cloned.1.call-start = ((), (), s32[]{:S(2)}) async-start(), calls=%async_computation.5 | async-start | bytes 15925248 | tf_op jit(solution)/shard_map/all_gather | solution.py:570
  12.6 1.9 copy-start
  12.6 262.6 %all-gather.7.cloned.1.call-start = ((), (), s32[]{:S(2)}) async-start(), calls=%async_computation.6 | async-start | bytes 15925248 | tf_op jit(solution)/shard_map/all_gather | solution.py:570
  13.4 586.1 %reduce-scatter.3.cloned.1.call-start = ((), (), s32[]{:S(2)}) async-start(), calls=%async_computation.2 | async-start | bytes 15925248 | tf_op jit(solution)/shard_map/reduce_scatter | solution.py:573
  24.4 9.8 %copy-start.3 = (f32[6168]{0:T(1024)S(1)}, f32[6168]{0:T(1024)}, u32[]{:S(2)}) copy-start(f32[6168]{0:T(1024)} %param.18) | copy-start | bytes 74020
  368.3 59.7 %copy-start.2 = (f32[4,256,768]{2,1,0:T(8,128)S(1)}, f32[4,256,768]{2,1,0:T(8,128)}, u32[]{:S(2)}) copy-start(f32[4,256,768]{2,1,0:T(8,128)} %slice.42) | copy-start | bytes 9437188
  427.9 5.0 copy-start.1
  427.9 5.0 copy-start.20
  433.0 3.7 copy-start.19
  433.0 9.9 %slice-start.6 = ((s8[6291456]{0:T(1024)(128)(4,1)}), s8[4194304]{0:T(1024)(128)(4,1)S(1)}, s32[]{:S(2)}) async-start(s8[6291456]{0:T(1024)(128)(4,1)} %bitcast.106), calls=%async_computation.13 | async-start | bytes 8388608
  436.7 3.7 copy-start.17
  436.7 3.7 copy-start.18
  436.7 6.2 slice-start.7
  440.4 2.5 copy-start.24
  440.4 9.4 %slice-start.4 = ((s8[6291456]{0:T(1024)(128)(4,1)}), s8[2097152]{0:T(1024)(128)(4,1)S(1)}, s32[]{:S(2)}) async-start(s8[6291456]{0:T(1024)(128)(4,1)} %bitcast.104), calls=%async_computation.11 | async-start | bytes 4194304
  442.8 7.0 slice-start.5
  442.9 7.0 copy-start.23
  457.0 287.1 %reduce-scatter.5.cloned.1.call-start = ((), (), s32[]{:S(2)}) async-start(), calls=%async_computation.3 | async-start | bytes 15925248 | tf_op jit(solution)/shard_map/reduce_scatter | solution.py:573
  458.9 4.0 copy-start.14
  462.9 2.5 copy-start.13
  462.9 7.6 slice-start.2
  465.4 2.5 copy-start.15
  465.4 2.5 copy-start.16
  465.4 5.1 slice-start.3
  467.9 2.5 copy-start.22
  467.9 9.8 %slice-start = ((s8[6291456]{0:T(1024)(128)(4,1)}), s8[4194304]{0:T(1024)(128)(4,1)S(1)}, s32[]{:S(2)}) async-start(s8[6291456]{0:T(1024)(128)(4,1)} %bitcast.100), calls=%async_computation.7 | async-start | bytes 8388608
  470.5 7.2 slice-start.1
  470.5 7.2 copy-start.21
  484.6 366.3 %all-reduce.2.cloned.1.call-start = ((), (), s32[]{:S(2)}) async-start(), calls=%async_computation.4 | async-start | bytes 7077888 | tf_op jit(solution)/shard_map/psum | solution.py:629
  758.5 27.1 %copy-start.6 = (f32[1,6168]{1,0:T(1,128)S(1)}, f32[1,6168]{1,0:T(1,128)}, u32[]{:S(2)}) copy-start(f32[1,6168]{1,0:T(1,128)} %param.19) | copy-start | bytes 74020
  758.5 27.1 %copy-start.7 = (f32[1,6168]{1,0:T(1,128)S(1)}, f32[1,6168]{1,0:T(1,128)}, u32[]{:S(2)}) copy-start(f32[1,6168]{1,0:T(1,128)} %param.20) | copy-start | bytes 74020
  758.5 44.1 %copy-start.5 = (f32[6168]{0:T(1024)S(1)}, f32[6168]{0:T(1024)}, u32[]{:S(2)}) copy-start(f32[6168]{0:T(1024)} %param.21) | copy-start | bytes 74020
  (6 other events, 5.9 us)
Sparse Core Ops, SparseCore 0:
  12.7 132.3 all-gather.4
  147.3 127.8 all-gather.6
  457.1 142.2 reduce-scatter.2
  601.6 142.4 reduce-scatter.4
  758.7 92.2 all-reduce.1

commit v2 on v1

--- a/solution.py
+++ b/solution.py
@@ -26,6 +26,7 @@
 BF = jnp.bfloat16
 F32 = jnp.float32
 VMEM_LIMIT = 60 * 1024 * 1024
+MESH_ID = pl.DeviceIdType.MESH
 
 
 def dot_nn(left, right):
@@ -85,6 +86,196 @@
     key_index = lax.broadcasted_iota(jnp.int32, shape, 1 if by_query else 0)
     offset = key_index - 2 * query_index
     return jnp.where((offset == 0) | (offset == 1), value, 0.0).astype(BF)
+
+
+def remote(source, target, send_sem, recv_sem, device):
+    return pltpu.make_async_remote_copy(
+        src_ref=source,
+        dst_ref=target,
+        send_sem=send_sem,
+        recv_sem=recv_sem,
+        device_id=device,
+        device_id_type=pl.DeviceIdType.MESH,
+    )
+
+
+class Spot:
+    def __init__(self, chips, group_count):
+        self.chips = chips
+        self.group_count = group_count
+        self.group = lax.axis_index("group")
+        self.member = lax.axis_index("fsdp")
+        self.chip = self.member // 2
+        self.core = self.member % 2
+
+    def line(self, chip):
+        return {"fsdp": 2 * chip + self.core}
+
+    def partner(self):
+        return {"fsdp": 2 * self.chip + 1 - self.core}
+
+    def other(self, turn):
+        return {"group": lax.rem(self.group + turn, self.group_count)}
+
+    def back_group(self, turn):
+        return lax.rem(self.group + self.group_count - turn, self.group_count)
+
+    def ahead_chip(self, hop):
+        return lax.rem(self.chip + hop, self.chips)
+
+    def back_chip(self, hop):
+        return lax.rem(self.chip + self.chips - hop, self.chips)
+
+
+def meet(spot):
+    barrier = pltpu.get_barrier_semaphore()
+    for hop in range(1, spot.chips):
+        pl.semaphore_signal(
+            barrier, inc=1, device_id=spot.line(spot.ahead_chip(hop)), device_id_type=MESH_ID
+        )
+    pl.semaphore_signal(barrier, inc=1, device_id=spot.partner(), device_id_type=MESH_ID)
+    for turn in range(1, spot.group_count):
+        pl.semaphore_signal(barrier, inc=1, device_id=spot.other(turn), device_id_type=MESH_ID)
+    pl.semaphore_wait(barrier, spot.chips - 1 + 1 + spot.group_count - 1)
+
+
+class Gather:
+    def __init__(self, spot, shard_ref, full_ref, sems):
+        self.spot = spot
+        self.shard = shard_ref
+        self.full = full_ref
+        self.line_send, self.line_recv, self.cross_send, self.cross_recv = sems[:4]
+        self.core_send, self.core_recv, self.own_sem = sems[4:]
+        self.rows = shard_ref.shape[0]
+        self.part = self.rows // spot.group_count
+        self.tick_count = 2 * spot.chips
+
+    def piece(self, chip, core, group):
+        start = (2 * chip + core) * self.rows + group * self.part
+        return self.full.at[pl.ds(start, self.part)]
+
+    def whole(self, chip, core):
+        return self.full.at[pl.ds((2 * chip + core) * self.rows, self.rows)]
+
+    def line_copy(self, hop):
+        spot = self.spot
+        return remote(
+            self.shard.at[pl.ds(spot.group * self.part, self.part)],
+            self.piece(spot.chip, spot.core, spot.group),
+            self.line_send.at[hop],
+            self.line_recv.at[hop],
+            spot.line(spot.ahead_chip(hop)),
+        )
+
+    def line_arrival(self, hop):
+        spot = self.spot
+        here = self.piece(spot.back_chip(hop), spot.core, spot.group)
+        return remote(
+            here, here, self.line_send.at[hop], self.line_recv.at[hop], spot.partner()
+        )
+
+    def cross_copy(self, hop, turn):
+        spot = self.spot
+        here = self.piece(spot.back_chip(hop), spot.core, spot.group)
+        slot = hop * spot.group_count + turn
+        return remote(
+            here, here, self.cross_send.at[slot], self.cross_recv.at[slot], spot.other(turn)
+        )
+
+    def cross_arrival(self, hop, turn):
+        spot = self.spot
+        here = self.piece(spot.back_chip(hop), spot.core, spot.back_group(turn))
+        slot = hop * spot.group_count + turn
+        return remote(
+            here, here, self.cross_send.at[slot], self.cross_recv.at[slot], spot.partner()
+        )
+
+    def core_copy(self, hop, turn):
+        spot = self.spot
+        slot = hop * spot.group_count + turn
+        if hop == 0:
+            source, target = self.shard, self.whole(spot.chip, spot.core)
+        else:
+            source = self.piece(spot.back_chip(hop), spot.core, spot.back_group(turn))
+            target = source
+        return remote(
+            source, target, self.core_send.at[slot], self.core_recv.at[slot], spot.partner()
+        )
+
+    def core_arrival(self, hop, turn):
+        spot = self.spot
+        slot = hop * spot.group_count + turn
+        if hop == 0:
+            here = self.whole(spot.chip, 1 - spot.core)
+        else:
+            here = self.piece(spot.back_chip(hop), 1 - spot.core, spot.back_group(turn))
+        return remote(
+            here, here, self.core_send.at[slot], self.core_recv.at[slot], spot.partner()
+        )
+
+    def own_copy(self):
+        return pltpu.make_async_copy(
+            self.shard, self.whole(self.spot.chip, self.spot.core), self.own_sem.at[0]
+        )
+
+    def tick(self, index):
+        chips, groups = self.spot.chips, self.spot.group_count
+        if index == 0:
+            for hop in range(1, chips):
+                self.line_copy(hop).start()
+            self.core_copy(0, 0).start()
+            self.own_copy().start()
+        elif index < chips:
+            hop = index
+            self.line_arrival(hop).wait_recv()
+            for turn in range(1, groups):
+                self.cross_copy(hop, turn).start()
+            self.core_copy(hop, 0).start()
+        elif index < 2 * chips - 1:
+            hop = index - chips + 1
+            for turn in range(1, groups):
+                self.cross_arrival(hop, turn).wait_recv()
+                self.core_copy(hop, turn).start()
+        else:
+            self.own_copy().wait()
+            self.core_copy(0, 0).wait_send()
+            self.core_arrival(0, 0).wait_recv()
+            for hop in range(1, chips):
+                self.line_copy(hop).wait_send()
+                self.core_copy(hop, 0).wait_send()
+                self.core_arrival(hop, 0).wait_recv()
+                for turn in range(1, groups):
+                    self.cross_copy(hop, turn).wait_send()
+                    self.core_copy(hop, turn).wait_send()
+                    self.core_arrival(hop, turn).wait_recv()
+
+
+def gather_sems(chips, group_count):
+    dma = pltpu.SemaphoreType.DMA
+    crossing = (chips * group_count,)
+    return [dma((chips,)), dma((chips,))] + [dma(crossing)] * 4 + [dma((1,))]
+
+
+def gather_kernel(chips, group_count, shard_ref, full_ref, *sems):
+    spot = Spot(chips, group_count)
+    job = Gather(spot, shard_ref, full_ref, sems)
+    meet(spot)
+    for index in range(job.tick_count):
+        job.tick(index)
+
+
+def gather_rows(shard):
+    members, group_count = lax.axis_size("fsdp"), lax.axis_size("group")
+    rows, width = shard.shape
+    return pl.pallas_call(
+        functools.partial(gather_kernel, members // 2, group_count),
+        out_shape=jax.ShapeDtypeStruct((rows * members, width), BF),
+        in_specs=[pl.BlockSpec(memory_space=pl.ANY)],
+        out_specs=pl.BlockSpec(memory_space=pl.ANY),
+        scratch_shapes=gather_sems(members // 2, group_count),
+        compiler_params=pltpu.CompilerParams(collective_id=0, has_side_effects=True),
+        name="gather_rows",
+    )(shard)
 
 
 def weight_copies(weight_hbm, weight_ref, sems, cuts):
@@ -101,12 +292,20 @@
 def ahead_kernel(
     is_first,
     head_count,
+    place,
     lengths_ref,
     slopes_ref,
     x_ref,
     gains_ref,
     weight_hbm,
-    query_out,
+    *rest,
+):
+    if place is not None:
+        shard_ref, rest = rest[0], rest[1:]
+        full_ref, rest = rest[11], rest[:11] + rest[12:]
+        job_sems = rest[18:]
+    (
+        query_out,
     key_out,
     value_out,
     lse_out,
@@ -116,6 +315,7 @@
     slope_out,
     total_two_out,
     layer_out,
+    low_out,
     weight_ref,
     dist_ref,
     mask_ref,
@@ -123,8 +323,26 @@
     value_t,
     att_t,
     sems,
-):
+    ) = rest[:18]
     step = pl.program_id(0)
+    if place is not None:
+        spot = Spot(*place)
+        job = Gather(spot, shard_ref, full_ref, job_sems)
+        spread = [round(index * 7 / (job.tick_count - 1)) for index in range(job.tick_count)]
+
+    def tick(quarter):
+        if place is None:
+            return
+        for index in range(job.tick_count):
+            if spread[index] % 2 == quarter:
+
+                @pl.when(step == spread[index] // 2)
+                def _():
+                    if index == 0:
+                        meet(spot)
+                    job.tick(index)
+
+    tick(0)
     width = weight_ref.shape[1]
     inner = (weight_ref.shape[0] - 4 * width) // 2
     queries, keys = query_out.shape[1], key_out.shape[1]
@@ -153,6 +371,7 @@
         residual = x_ref[0]
         query_low = residual.astype(BF)
         memory_low = query_low
+    low_out[0] = query_low
     need(0)
     query_rows = dot_nn(query_low, weight_ref[0:width]).astype(BF)
     query_out[0] = query_rows
@@ -212,9 +431,10 @@
     unit_two, _ = norm_parts(total_two)
     result = unit_two * gains_ref[2:3] + gains_ref[3:4]
     layer_out[0] = result.astype(layer_out.dtype)
-
-
-def layer_ahead(is_first, x, lengths, slopes, gains, weight_full, out_dtype):
+    tick(1)
+
+
+def layer_ahead(is_first, x, lengths, slopes, gains, weight_full, out_dtype, shard=None):
     batch, memory_length, width = x.shape
     queries = memory_length // 2 if is_first else memory_length
     keys = memory_length
@@ -240,12 +460,19 @@
         (queries, inner, BF),
         (queries, width, F32),
         (queries, width, out_dtype),
+        (queries, width, BF),
     ]
     flops = 2 * batch * width * (
         2 * queries * width + 2 * keys * width + 2 * queries * inner + 2 * queries * keys
     )
+    hosted = shard is not None
+    place = (lax.axis_size("fsdp") // 2, lax.axis_size("group")) if hosted else None
+    anywhere = [pl.BlockSpec(memory_space=pl.ANY)] * hosted
+    full_shape = [jax.ShapeDtypeStruct((rows, width), BF)] * hosted
+    job_sems = gather_sems(*place) if hosted else []
+    params = dict(collective_id=1, has_side_effects=True) if hosted else {}
     return pl.pallas_call(
-        functools.partial(ahead_kernel, is_first, head_count),
+        functools.partial(ahead_kernel, is_first, head_count, place),
         grid_spec=pltpu.PrefetchScalarGridSpec(
             num_scalar_prefetch=2,
             grid=(batch,),
@@ -253,8 +480,9 @@
                 block(memory_length, width),
                 pl.BlockSpec((4, width), lambda i, *_: (0, 0)),
                 pl.BlockSpec(memory_space=pl.ANY),
-            ],
-            out_specs=[block(length, size) for length, size, _ in outs],
+            ]
+            + anywhere,
+            out_specs=[block(length, size) for length, size, _ in outs] + anywhere,
             scratch_shapes=[
                 pltpu.VMEM((rows, width), BF),
                 pltpu.VMEM((keys, queries), F32),
@@ -263,15 +491,16 @@
                 pltpu.VMEM((width, keys), BF),
                 pltpu.VMEM((width, queries), F32),
                 pltpu.SemaphoreType.DMA((5,)),
-            ],
+            ]
+            + job_sems,
         ),
-        out_shape=[shape(*out) for out in outs],
-        compiler_params=pltpu.CompilerParams(vmem_limit_bytes=VMEM_LIMIT),
+        out_shape=[shape(*out) for out in outs] + full_shape,
+        compiler_params=pltpu.CompilerParams(vmem_limit_bytes=VMEM_LIMIT, **params),
         cost_estimate=pl.CostEstimate(
             flops=flops, bytes_accessed=rows * width * 2 + 30000000, transcendentals=0
         ),
         name="layer_ahead",
-    )(lengths, slopes, x, gains, weight_full)
+    )(lengths, slopes, x, gains, weight_full, *([shard] * hosted))
 
 
 def back_kernel(
@@ -566,9 +795,6 @@
     part_size = small.shape[0] // 2
     masters_low = weights.astype(BF)
 
-    def fetch(layer_index):
-        return lax.all_gather(masters_low[layer_index], "fsdp", axis=0, tiled=True)
-
     def reduce_layer(grad_rows):
         return lax.psum_scatter(
             grad_rows.astype(BF), "fsdp", scatter_dimension=0, tiled=True
@@ -581,12 +807,11 @@
         gains.append(part[: 4 * width].reshape(4, width))
         slopes.append(part[4 * width :])
 
-    matrix_one = fetch(0)
-    matrix_two = fetch(1)
-    (q1, k1, v1, lse1, att1, one1, hid1, steep1, two1, first_out) = layer_ahead(
-        True, hidden_in, lengths, slopes[0], gains[0], matrix_one, F32
-    )
-    (q2, k2, v2, lse2, att2, one2, hid2, steep2, two2, block_out) = layer_ahead(
+    matrix_one = gather_rows(masters_low[0])
+    (q1, k1, v1, lse1, att1, one1, hid1, steep1, two1, first_out, low1, matrix_two) = layer_ahead(
+        True, hidden_in, lengths, slopes[0], gains[0], matrix_one, F32, masters_low[1]
+    )
+    (q2, k2, v2, lse2, att2, one2, hid2, steep2, two2, block_out, low2) = layer_ahead(
         False, first_out, lengths, slopes[1], gains[1], matrix_two, BF
     )
     back_two = layer_back(
@@ -598,11 +823,14 @@
         gains[1],
         matrix_two,
     )
-    first_low = first_out.astype(BF)
-    shard_two = reduce_layer(matrix_gradient(first_low, first_low, att2, hid2, back_two[:7]))
+    matrix_grad_two = matrix_gradient(low2, low2, att2, hid2, back_two[:7])
+    first_grad, matrix_grad_two = lax.optimization_barrier(
+        (back_two[7], matrix_grad_two.astype(BF))
+    )
+    shard_two = reduce_layer(matrix_grad_two)
     back_one = layer_back(
         True,
-        back_two[7],
+        first_grad,
         (q1, k1, v1, lse1, att1, one1, steep1, two1),
         lengths,
         slopes[0],
@@ -610,9 +838,7 @@
         matrix_one,
     )
     input_grad = back_one[7]
-    hidden_wide = hidden_in.astype(F32)
-    pooled_low = ((hidden_wide[:, 0::2] + hidden_wide[:, 1::2]) * 0.5).astype(BF)
-    shard_one = reduce_layer(matrix_gradient(pooled_low, hidden_in, att1, hid1, back_one[:7]))
+    shard_one = reduce_layer(matrix_gradient(low1, hidden_in, att1, hid1, back_one[:7]))
     grad_shard = jnp.stack([shard_one, shard_two])
     head_count = slopes[0].shape[0]
     small_parts = []

time: 877 us -> 833 us (0.950)
  waiting for transfers between devices: 488 us -> 342 us
  Pallas kernels: 212 us -> 336 us
  local copies, waits for them, and re-layouts: 27.3 us -> 6.19 us
    all_gather x2 -> x0, waiting for transfers between devices: 180 us -> none  [fetch(): return lax.all_gather(masters_low[layer_index], 'fsdp', axis=0, tiled=True)]
    pallas_call x2 -> x3, Pallas kernels: 107 us -> 230 us  [the longest x2 152 us: layer_ahead(): pl.pallas_call(functools.partial(ahead_kernel, is_first, head_count, plac...]
    reduce_scatter x2, waiting for transfers between devices: 259 us -> 294 us  [reduce_layer(): lax.psum_scatter(grad_rows.astype(BF), 'fsdp', scatter_dimension=0, tiled...]
    slice x3 -> x0, local copies, waits for them, and re-layouts: 21.7 us -> none  [the longest x1 9.87 us: shards(): hidden_wide[:, 0::2] + hidden_wide[:, 1::2]]
  transfers between devices with their start and end apart: 5 -> 3, of which waited for: 5 -> 3; matrix products, arithmetic and copies ran while one was open for 6% -> 0% of each run, Pallas kernels for 7% -> 0%
where the time goes in v2:
time: 833 us; the launch traced here: 826 us
  waiting for transfers between devices  342 us (41%)
  Pallas kernels  336 us (40%)
  matrix products  53.3 us (6%)
  blocking collectives  42.3 us (5%)
  other arithmetic  32.4 us (4%)
  between operations  14.3 us (2%)
    reduce_scatter x2, waiting for transfers between devices, reduce_layer(): lax.psum_scatter(grad_rows.astype(BF), 'fsdp', scatter_dimension=0, tiled...  294 us
    pallas_call x2, Pallas kernels, layer_ahead(): pl.pallas_call(functools.partial(ahead_kernel, is_first, head_count, plac...  152 us
    pallas_call x2, Pallas kernels, layer_back(): pl.pallas_call(functools.partial(back_kernel, is_first, head_count), grid...  105 us
    pallas_call x1, Pallas kernels, gather_rows(): pl.pallas_call(functools.partial(gather_kernel, members // 2, group_count...  78.5 us
    dot_general x12, matrix products, weight_product(): lax.dot_general(left, right, (((0, 1), (0, 1)), ((), ())), preferred_elem...  53.3 us
    psum x1, waiting for transfers between devices, shards(): lax.psum(weight_move[0].astype(BF), 'group').astype(F32)  47.7 us
    psum x1, blocking collectives, shards(): small_grad = lax.psum(jnp.concatenate(small_parts), 'fsdp')  26 us
  transfers between devices with their start and end apart: 3, of which 3 were waited for; matrix products, arithmetic and copies ran while one was open for 0% of the time, Pallas kernels for 0%

profile of v2, /device:TPU:0, one launch (start us, length us, event | category | flops | bytes accessed | tf_op | source)
XLA Modules:
  0.0 826.0 jit_solution(17855034723737537406)
XLA Ops:
  7.2 0.8 fusion.22
  8.0 1.3 fusion.23
  9.3 3.4 convert_element_type.28
  12.7 2.0 slice_bitcast_fusion
  14.7 78.5 %gather_rows.1.weight_hbm = bf16[9216,768]{1,0:T(8,128)(2,1)} custom-call(bf16[1152,768]{1,0:T(8,128)(2,1)} %get-tuple-element.117.shard_ref), custom_call_target="tpu_custom_call" | custom-call | tf_op jit(solution)/shard_map/gather_rows/pallas_call | solution.py:270
  93.2 0.6 reshape.137.gains_ref
  94.4 103.7 %layer_ahead.2 = (bf16[4,256,768]{2,1,0:T(8,128)(2,1)}, bf16[4,512,768]{2,1,0:T(8,128)(2,1)}, bf16[4,512,768]{2,1,0:T(8,128)(2,1)}, f32[4,16,256]{2,1,0:T(8,128)...) custom-call(s32[4]{0:T(128)} %lengths_ref.7, ...), custom_call_target="tpu_custom_call" | custom-call | flops 18522046464 | bytes 44155776 | tf_op jit(solution)/shard_map/layer_ahead/pallas_call | solution.py:474
  198.1 47.9 %layer_ahead.3 = (bf16[4,256,768]{2,1,0:T(8,128)(2,1)}, bf16[4,256,768]{2,1,0:T(8,128)(2,1)}, bf16[4,256,768]{2,1,0:T(8,128)(2,1)}, f32[4,16,256]{2,1,0:T(8,128)...) custom-call(s32[4]{0:T(128)} %lengths_ref.7, ...), custom_call_target="tpu_custom_call" | custom-call | flops 15300820992 | bytes 44155776 | tf_op jit(solution)/shard_map/layer_ahead/pallas_call | solution.py:474
  246.0 45.9 %layer_back.2 = (bf16[4,256,768]{2,1,0:T(8,128)(2,1)}, bf16[4,256,3072]{2,1,0:T(8,128)(2,1)}, bf16[4,256,768]{2,1,0:T(8,128)(2,1)}, bf16[4,256,768]{2,1,0:T(8,12...) custom-call(s32[4]{0:T(128)} %lengths_ref.7, ...), custom_call_target="tpu_custom_call" | custom-call | flops 16508780544 | bytes 54155776 | tf_op jit(solution)/shard_map/layer_back/pallas_call | solution.py:682
  291.9 4.0 fusion.9
  295.9 2.5 fusion.10
  298.4 2.5 fusion.11
  300.9 2.5 fusion.12
  303.4 7.0 fusion.4
  310.4 6.9 fusion.5
  317.3 59.6 %layer_back.3 = (bf16[4,256,768]{2,1,0:T(8,128)(2,1)}, bf16[4,256,3072]{2,1,0:T(8,128)(2,1)}, bf16[4,256,768]{2,1,0:T(8,128)(2,1)}, bf16[4,256,768]{2,1,0:T(8,12...) custom-call(s32[4]{0:T(128)} %lengths_ref.7, ...), custom_call_target="tpu_custom_call" | custom-call | flops 20937965568 | bytes 54155776 | tf_op jit(solution)/shard_map/layer_back/pallas_call | solution.py:682
  377.0 4.0 fusion.13
  381.0 3.7 fusion.16
  384.7 3.7 fusion.18
  388.4 2.5 fusion.14
  390.9 7.0 fusion.6
  397.9 7.2 fusion.7
  405.1 0.7 reduce-scatter.5.cloned.1.call-update
  405.9 148.8 %reduce-scatter.3.cloned.1.call-done = bf16[1152,768]{1,0:T(8,128)(2,1)} async-done(((bf16[9216,768]{1,0:T(8,128)(2,1)}), bf16[1152,768]{1,0:T(8,128)(2,1)}) %reduce-scatter.3.cloned.1.call-update) | async-done | bytes 1769488 | tf_op jit(solution)/shard_map/reduce_scatter | solution.py:799
  554.7 144.7 %reduce-scatter.5.cloned.1.call-done = bf16[1152,768]{1,0:T(8,128)(2,1)} async-done(((bf16[9216,768]{1,0:T(8,128)(2,1)}), bf16[1152,768]{1,0:T(8,128)(2,1)}) %reduce-scatter.5.cloned.1.call-update) | async-done | bytes 1769488 | tf_op jit(solution)/shard_map/reduce_scatter | solution.py:799
  699.4 14.4 %fusion.8 = (bf16[2,1152,768]{2,1,0:T(8,128)(2,1)}, f32[1,2,1152,768]{3,2,1,0:T(8,128)}, f32[1,2,1152,768]{3,2,1,0:T(8,128)}) fusion(f32[2,1152,768]{2,1,0:T(8,128)} %param.14, bf16[1,1,1152,768]{3,2,1,0:T(8,128)(2,1)} %bitcast.101, bf16[1,1,1152,768]{3,2,1,0:T(8,128)(2,1)} %bitcast.100, f32[1,2,1152,768]{3,2,1,0:T(8,128)} %param.15, ...), kind=kLoop, calls=%fused_computation.19 | loop fusion | flops 30081024 | bytes 42467328 | tf_op jit(solution)/shard_map/convert_element_type | solution.py:855
  714.9 26.0 %psum.22 = f32[6168]{0:T(1024)S(1)} all-reduce(f32[6168]{0:T(1024)S(1)} %concatenate.34), channel_id=1, replica_groups=mesh['group'=4,'fsdp'=8] {'fsdp'}, use_global_device_ids=true, to_apply=%region_5.0 | all-reduce | flops 6168 | bytes 49344 | tf_op jit(solution)/shard_map/psum | solution.py:847
  740.9 0.8 convert_reduce_fusion
  741.7 16.3 %psum.23 = bf16[6168]{0:T(1024)(128)(2,1)S(1)} all-reduce(bf16[6168]{0:T(1024)(128)(2,1)S(1)} %get-tuple-element.106), channel_id=1, replica_groups=mesh['group'=4,'fsdp'=8] {'group'}, use_global_device_ids=true, to_apply=%region_6.0 | all-reduce | flops 6168 | bytes 24672 | tf_op jit(solution)/shard_map/psum | solution.py:856
  758.0 0.6 multiply_subtract_fusion.1
  758.7 47.7 %all-reduce.2.cloned.1.call-done = bf16[2,1152,768]{2,1,0:T(8,128)(2,1)} async-done(((bf16[2,1152,768]{2,1,0:T(8,128)(2,1)}), bf16[2,1152,768]{2,1,0:T(8,128)(2,1)}) %all-reduce.2.cloned.1.call-update) | async-done | bytes 3538960 | tf_op jit(solution)/shard_map/psum | solution.py:855
  806.3 13.0 %fusion.19 = (bf16[2,1152,768]{2,1,0:T(8,128)(2,1)}, f32[2,1152,768]{2,1,0:T(8,128)}, f32[2,1152,768]{2,1,0:T(8,128)}, f32[2,1152,768]{2,1,0:T(8,128)}) fusion(f32[2,1152,768]{2,1,0:T(8,128)} %param.14, f32[2,1152,768]{2,1,0:T(8,128)} %param.17, bf16[2,1152,768]{2,1,0:T(8,128)(2,1)} %all-reduce.2.cloned.1.call-done), kind=kLoop, calls=%fused_computation.51 | loop fusion | flops 15925248 | bytes 42467328 | tf_op jit(solution)/shard_map/convert_element_type | solution.py:865
  (81 shorter events, 1.9 us)
Async XLA Ops:
  7.2 547.5 %reduce-scatter.3.cloned.1.call-start = ((), (), s32[]{:S(2)}) async-start(), calls=%async_computation.2 | async-start | bytes 15925248 | tf_op jit(solution)/shard_map/reduce_scatter | solution.py:799
  246.0 45.9 %copy-start.11 = (bf16[4,256,768]{2,1,0:T(8,128)(2,1)S(1)}, bf16[4,256,768]{2,1,0:T(8,128)(2,1)}, u32[]{:S(2)}) copy-start(bf16[4,256,768]{2,1,0:T(8,128)(2,1)} %get-tuple-element.70) | copy-start | bytes 4718596
  291.9 4.0 copy-start.15
  295.9 2.5 copy-start.14
  295.9 7.5 slice-start.6
  298.4 2.5 copy-start.10
  298.4 2.5 copy-start.13
  298.4 5.0 slice-start.7
  300.9 2.5 copy-start.22
  300.9 9.5 %slice-start.2 = ((s8[6291456]{0:T(1024)(128)(4,1)}), s8[4194304]{0:T(1024)(128)(4,1)S(1)}, s32[]{:S(2)}) async-start(s8[6291456]{0:T(1024)(128)(4,1)} %bitcast.104), calls=%async_computation.7 | async-start | bytes 8388608
  303.4 7.0 slice-start.3
  303.4 7.0 copy-start.20
  317.3 59.6 %copy-start.16 = (bf16[4,256,768]{2,1,0:T(8,128)(2,1)S(1)}, bf16[4,256,768]{2,1,0:T(8,128)(2,1)}, u32[]{:S(2)}) copy-start(bf16[4,256,768]{2,1,0:T(8,128)(2,1)} %get-tuple-element.89) | copy-start | bytes 4718596
  376.9 4.1 copy-start.8
  376.9 4.0 copy-start.18
  381.0 3.7 copy-start.17
  381.0 9.9 %slice-start.4 = ((s8[6291456]{0:T(1024)(128)(4,1)}), s8[4194304]{0:T(1024)(128)(4,1)S(1)}, s32[]{:S(2)}) async-start(s8[6291456]{0:T(1024)(128)(4,1)} %bitcast.106), calls=%async_computation.9 | async-start | bytes 8388608
  384.7 3.7 copy-start.9
  384.7 3.7 copy-start.12
  384.7 6.2 slice-start.5
  388.4 2.5 copy-start.21
  388.4 9.5 %slice-start = ((s8[6291456]{0:T(1024)(128)(4,1)}), s8[2097152]{0:T(1024)(128)(4,1)S(1)}, s32[]{:S(2)}) async-start(s8[6291456]{0:T(1024)(128)(4,1)} %bitcast.102), calls=%async_computation.5 | async-start | bytes 4194304
  390.9 7.0 slice-start.1
  390.9 7.0 copy-start.19
  405.1 294.3 %reduce-scatter.5.cloned.1.call-start = ((), (), s32[]{:S(2)}) async-start(), calls=%async_computation.3 | async-start | bytes 15925248 | tf_op jit(solution)/shard_map/reduce_scatter | solution.py:799
  405.8 400.5 %all-reduce.2.cloned.1.call-start = ((), (), s32[]{:S(2)}) async-start(), calls=%async_computation.4 | async-start | bytes 7077888 | tf_op jit(solution)/shard_map/psum | solution.py:855
  713.8 0.8 copy-start.6
  713.8 0.9 copy-start.4
  713.9 27.0 %copy-start = (f32[6168]{0:T(1024)S(1)}, f32[6168]{0:T(1024)}, u32[]{:S(2)}) copy-start(f32[6168]{0:T(1024)} %param.18) | copy-start | bytes 74020
  713.9 27.1 %copy-start.2 = (f32[1,6168]{1,0:T(1,128)S(1)}, f32[1,6168]{1,0:T(1,128)}, u32[]{:S(2)}) copy-start(f32[1,6168]{1,0:T(1,128)} %param.19) | copy-start | bytes 74020
  713.9 27.1 %copy-start.3 = (f32[1,6168]{1,0:T(1,128)S(1)}, f32[1,6168]{1,0:T(1,128)}, u32[]{:S(2)}) copy-start(f32[1,6168]{1,0:T(1,128)} %param.20) | copy-start | bytes 74020
  713.9 44.1 %copy-start.1 = (f32[6168]{0:T(1024)S(1)}, f32[6168]{0:T(1024)}, u32[]{:S(2)}) copy-start(f32[6168]{0:T(1024)} %param.21) | copy-start | bytes 74020
  (2 other events, 1.4 us)
Sparse Core Ops, SparseCore 0:
  405.2 149.4 reduce-scatter.2
  557.0 142.4 reduce-scatter.4
  714.1 92.2 all-reduce.1

commit v3 on v2

--- a/solution.py
+++ b/solution.py
@@ -276,6 +276,598 @@
         compiler_params=pltpu.CompilerParams(collective_id=0, has_side_effects=True),
         name="gather_rows",
     )(shard)
+
+
+def chunk_count(rows):
+    return max(
+        count for count in range(1, 7) if rows % (32 * count) == 0
+    )
+
+
+class Reduce:
+    def __init__(self, spot, count, grad, swap, lands, loads, sends, sems):
+        self.spot = spot
+        self.count = count
+        self.grad = grad
+        self.swap = swap
+        self.lands = lands
+        self.loads = loads
+        self.sends = sends
+        (self.load_sems, self.send_sems, self.recv_sems, self.swap_send, self.swap_recv) = sems
+        self.last = spot.chips - 1
+        self.rows = grad.shape[0] // (2 * spot.chips)
+        self.piece = self.rows // count
+        self.items = self.last * count
+        self.ticks = self.items + self.last
+        self.slots = sends.shape[1]
+
+    def swap_copy(self, chip, part):
+        spot = self.spot
+        start = part * self.piece
+        source = (2 * chip + 1 - spot.core) * self.rows + start
+        return remote(
+            self.grad.at[pl.ds(pl.multiple_of(source, 8), self.piece)],
+            self.swap.at[pl.ds(pl.multiple_of(chip * self.rows + start, 8), self.piece)],
+            self.swap_send.at[chip * self.count + part],
+            self.swap_recv.at[chip * self.count + part],
+            spot.partner(),
+        )
+
+    def start(self):
+        for chip in range(self.last, -1, -1):
+            for part in range(self.count - 1, -1, -1):
+                self.swap_copy(chip, part).start()
+        self.fetch(0)
+
+    def own_rows(self, chip, part):
+        start = (2 * chip + self.spot.core) * self.rows + part * self.piece
+        return self.grad.at[pl.ds(pl.multiple_of(start, 8), self.piece)]
+
+    def swap_rows(self, chip, part):
+        start = chip * self.rows + part * self.piece
+        return self.swap.at[pl.ds(pl.multiple_of(start, 8), self.piece)]
+
+    def land_rows(self, way, item):
+        start = (way * self.items + item) * self.piece
+        return self.lands.at[pl.ds(pl.multiple_of(start, 8), self.piece)]
+
+    def plan(self, way, tick):
+        spot, count, last = self.spot, self.count, self.last
+        distance = spot.chip + way * (last - 2 * spot.chip)
+        item = tick - distance
+        raised = item + count * spot.chips
+        chip = last - way - (lax.div(raised, count) - spot.chips)
+        part = count - 1 - lax.rem(raised, count)
+        inside = (item >= 0) & (item < self.items)
+        ahead = (1 - 2 * way) * (chip - spot.chip)
+        passes = inside & (ahead > 0)
+        takes = distance > 0
+        return item, chip, part, passes, takes
+
+    def near_loads(self, way, tick, chip, part):
+        turn = lax.rem(tick, 2)
+        return [
+            pltpu.make_async_copy(
+                source,
+                self.loads.at[way, 2 * turn + which],
+                self.load_sems.at[way * 5 + 2 * turn + which],
+            )
+            for which, source in enumerate((self.own_rows(chip, part), self.swap_rows(chip, part)))
+        ]
+
+    def land_load(self, way, item):
+        return pltpu.make_async_copy(
+            self.land_rows(way, item), self.loads.at[way, 4], self.load_sems.at[way * 5 + 4]
+        )
+
+    def fetch(self, tick):
+        for way in range(2):
+            item, chip, part, passes, takes = self.plan(way, tick)
+
+            @pl.when(passes)
+            def _():
+                self.swap_copy(chip, part).wait_recv()
+                for copy in self.near_loads(way, tick, chip, part):
+                    copy.start()
+
+    def hop(self, way, item):
+        spot = self.spot
+        return remote(
+            self.sends.at[way, lax.rem(item, self.slots)],
+            self.land_rows(way, item),
+            self.send_sems.at[way * self.items + item],
+            self.recv_sems.at[way * self.items + item],
+            spot.line(spot.chip + 1 - 2 * way),
+        )
+
+    def arrival(self, way, item):
+        here = self.land_rows(way, item)
+        sem = way * self.items + item
+        return remote(
+            here, here, self.send_sems.at[sem], self.recv_sems.at[sem], self.spot.partner()
+        )
+
+    def tick(self, tick):
+        spot = self.spot
+        nearer = jnp.where(2 * spot.chip > self.last, 1, 0)
+        for turn in range(2):
+            way = nearer if turn == 0 else 1 - nearer
+            item, chip, part, passes, takes = self.plan(way, tick)
+
+            @pl.when(passes)
+            def _():
+                @pl.when(takes)
+                def _():
+                    self.arrival(way, item).wait_recv()
+                    self.land_load(way, item).start()
+
+                slot = lax.rem(item, self.slots)
+                first = way * (self.last - spot.chip) * self.count
+
+                @pl.when(item - first >= self.slots)
+                def _():
+                    self.hop(way, item - self.slots).wait_send()
+
+                for copy in self.near_loads(way, tick, chip, part):
+                    copy.wait()
+
+                @pl.when(takes)
+                def _():
+                    self.land_load(way, item).wait()
+                    self.add(way, tick, slot, True)
+
+                @pl.when(jnp.logical_not(takes))
+                def _():
+                    self.add(way, tick, slot, False)
+
+                self.hop(way, item).start()
+
+        self.fetch(tick + 1)
+
+    def settle(self, order):
+        spot = self.spot
+
+        @pl.when(spot.chip > 0)
+        def _():
+            self.arrival(0, (self.last - spot.chip) * self.count + order).wait_recv()
+
+        @pl.when(spot.chip < self.last)
+        def _():
+            self.arrival(1, (self.last - 1 - spot.chip) * self.count + order).wait_recv()
+
+    def add(self, way, tick, slot, landed):
+        block = 32
+        near = 2 * lax.rem(tick, 2)
+
+        def step(index, carry):
+            rows = pl.ds(pl.multiple_of(index * block, block), block)
+            total = self.loads[way, near, rows, :].astype(F32)
+            total = total + self.loads[way, near + 1, rows, :].astype(F32)
+            if landed:
+                total = total + self.loads[way, 4, rows, :].astype(F32)
+            self.sends[way, slot, rows, :] = total.astype(BF)
+            return carry
+
+        lax.fori_loop(0, self.piece // block, step, 0)
+
+    def drain(self):
+        spot = self.spot
+        for way in range(2):
+            begin = 0 if way == 0 else (self.last - spot.chip) * self.count
+            end = (self.last - spot.chip) * self.count if way == 0 else self.items
+            for back in range(1, self.slots + 1):
+
+                @pl.when(end - back >= begin)
+                def _():
+                    self.hop(way, end - back).wait_send()
+
+        for chip in range(spot.chips):
+            for part in range(self.count):
+                self.swap_copy(chip, part).wait_send()
+
+
+def reduce_scratch(chips, rows, width):
+    count = chunk_count(rows)
+    dma = pltpu.SemaphoreType.DMA
+    items = (chips - 1) * count
+    return [
+        pltpu.VMEM((2, 5, rows // count, width), BF),
+        pltpu.VMEM((2, 4, rows // count, width), BF),
+        dma((10,)),
+        dma((2 * items,)),
+        dma((2 * items,)),
+        dma((chips * count,)),
+        dma((chips * count,)),
+    ]
+
+
+def reduce_lands(chips, rows, width):
+    return [
+        jax.ShapeDtypeStruct((chips * rows, width), BF),
+        jax.ShapeDtypeStruct((2 * (chips - 1) * rows, width), BF),
+    ]
+
+
+def move_of(master, gradient, first_mom, second_mom, rate):
+    return adam_step(master, gradient, first_mom, second_mom, rate)[2]
+
+
+def finish_kernel(
+    chips,
+    group_count,
+    grad_zero,
+    grad_one,
+    swap_one,
+    lands_one,
+    weight_hbm,
+    first_hbm,
+    second_hbm,
+    small_grad,
+    small_ref,
+    small_first,
+    small_second,
+    grad_out,
+    sum_out,
+    small_grad_out,
+    small_sum_out,
+    swap_zero,
+    lands_zero,
+    parts,
+    states,
+    grads,
+    moves,
+    quarters,
+    sums,
+    small_land,
+    small_moves,
+    small_move,
+    part_sems,
+    state_sems,
+    grad_sems,
+    cross_send,
+    cross_recv,
+    share_send,
+    share_recv,
+    share_own,
+    small_send,
+    small_recv,
+    small_cross_send,
+    small_cross_recv,
+    *engine_scratch,
+):
+    tick = pl.program_id(0)
+    spot = Spot(chips, group_count)
+    rows = sum_out.shape[1]
+    count = moves.shape[1]
+    piece = rows // count
+    quarter = piece // group_count
+    engine = Reduce(
+        spot,
+        count,
+        grad_zero,
+        swap_zero,
+        lands_zero,
+        engine_scratch[0],
+        engine_scratch[1],
+        engine_scratch[2:],
+    )
+    members = 2 * chips
+    last = chips - 1
+    tops = ((grad_zero, swap_zero, lands_zero), (grad_one, swap_one, lands_one))
+
+    def small_send_copy(hop):
+        target = lax.rem(spot.member + hop, members)
+        return remote(
+            small_grad,
+            small_land.at[spot.member],
+            small_send.at[hop],
+            small_recv.at[hop],
+            {"fsdp": target},
+        )
+
+    def small_cross_copy(turn):
+        return remote(
+            small_move,
+            small_moves.at[spot.group],
+            small_cross_send.at[turn],
+            small_cross_recv.at[turn],
+            spot.other(turn),
+        )
+
+    @pl.when(tick == 0)
+    def _():
+        barrier = pltpu.get_barrier_semaphore()
+        for hop in range(1, members):
+            pl.semaphore_signal(
+                barrier,
+                inc=1,
+                device_id={"fsdp": lax.rem(spot.member + hop, members)},
+                device_id_type=MESH_ID,
+            )
+        for turn in range(1, group_count):
+            pl.semaphore_signal(barrier, inc=1, device_id=spot.other(turn), device_id_type=MESH_ID)
+        pl.semaphore_wait(barrier, members - 1 + group_count - 1)
+        engine.start()
+        for hop in range(1, members):
+            small_send_copy(hop).start()
+        parts[...] = jnp.zeros_like(parts)
+
+    bases = (engine.ticks - count, 1)
+
+    def part_loads(layer, order):
+        top = tops[layer]
+        part, slot = count - 1 - order, lax.rem(order, 2)
+        here = pl.multiple_of(part * piece, 8)
+        start = (2 * spot.chip + spot.core) * rows + here
+        sources = (
+            top[0].at[pl.ds(pl.multiple_of(start, 8), piece)],
+            top[1].at[pl.ds(pl.multiple_of(spot.chip * rows + here, 8), piece)],
+            top[2].at[
+                pl.ds(pl.multiple_of(((last - spot.chip) * count + order) * piece, 8), piece)
+            ],
+            top[2].at[
+                pl.ds(
+                    pl.multiple_of(
+                        ((2 * last - 1 - spot.chip) * count + order) * piece, 8
+                    ),
+                    piece,
+                )
+            ],
+        )
+        return [
+            pltpu.make_async_copy(
+                source,
+                parts.at[layer, slot, which],
+                part_sems.at[(2 * layer + slot) * 4 + which],
+            )
+            for which, source in enumerate(sources)
+        ]
+
+    def state_loads(layer, order):
+        part, slot = count - 1 - order, lax.rem(order, 2)
+        window = pl.ds(pl.multiple_of(part * piece, 8), piece)
+        sources = (
+            weight_hbm.at[layer, window],
+            first_hbm.at[0, layer, window],
+            second_hbm.at[0, layer, window],
+        )
+        return [
+            pltpu.make_async_copy(
+                source,
+                states.at[layer, slot, which],
+                state_sems.at[(2 * layer + slot) * 3 + which],
+            )
+            for which, source in enumerate(sources)
+        ]
+
+    def each_near(layer, order, act):
+        copies = part_loads(layer, order)
+        act(copies[0])
+        act(copies[1])
+
+    def each_landed(layer, order, act):
+        copies = part_loads(layer, order)
+
+        @pl.when(spot.chip > 0)
+        def _():
+            act(copies[2])
+
+        @pl.when(spot.chip < last)
+        def _():
+            act(copies[3])
+
+    def grad_store(layer, order):
+        part = count - 1 - order
+        return pltpu.make_async_copy(
+            grads.at[layer, part],
+            grad_out.at[layer, pl.ds(pl.multiple_of(part * piece, 8), piece)],
+            grad_sems.at[layer * count + part],
+        )
+
+    def cross_copy(layer, order, turn):
+        part = count - 1 - order
+        target = lax.rem(spot.group + turn, group_count)
+        sem = (layer * count + part) * group_count + turn
+        return remote(
+            moves.at[layer, part, pl.ds(pl.multiple_of(target * quarter, 8), quarter)],
+            quarters.at[layer, part, turn],
+            cross_send.at[sem],
+            cross_recv.at[sem],
+            spot.other(turn),
+        )
+
+    def share_rows(layer, part, group):
+        start = pl.multiple_of(part * piece + group * quarter, 8)
+        return sum_out.at[layer, pl.ds(start, quarter)]
+
+    def share_copy(layer, order, turn):
+        part = count - 1 - order
+        sem = (layer * count + part) * group_count + turn
+        return remote(
+            sums.at[layer, part],
+            share_rows(layer, part, spot.group),
+            share_send.at[sem],
+            share_recv.at[sem],
+            spot.other(turn),
+        )
+
+    def share_local(layer, order):
+        part = count - 1 - order
+        return pltpu.make_async_copy(
+            sums.at[layer, part],
+            share_rows(layer, part, spot.group),
+            share_own.at[layer * count + part],
+        )
+
+    def prepare(tick):
+        for layer in range(2):
+            order = tick - bases[layer]
+
+            @pl.when((order >= 0) & (order < count))
+            def _():
+                if layer == 0:
+                    engine.swap_copy(spot.chip, count - 1 - order).wait_recv()
+                else:
+                    each_landed(layer, order, lambda copy: copy.start())
+                each_near(layer, order, lambda copy: copy.start())
+                for copy in state_loads(layer, order):
+                    copy.start()
+
+    engine.tick(tick)
+    prepare(tick + 1)
+    landed = tick - bases[0]
+
+    @pl.when((landed >= 0) & (landed < count))
+    def _():
+        engine.settle(landed)
+        each_landed(0, landed, lambda copy: copy.start())
+
+    for layer in range(2):
+        later = tick - bases[layer] - 1
+
+        @pl.when((later >= 0) & (later < count))
+        def _():
+            part = count - 1 - later
+            for turn in range(1, group_count):
+                cross_copy(layer, later, turn).wait_recv()
+            total = moves[
+                layer, part, pl.ds(pl.multiple_of(spot.group * quarter, 8), quarter), :
+            ].astype(F32)
+            for turn in range(1, group_count):
+                total = total + quarters[layer, part, turn].astype(F32)
+            sums[layer, part] = total.astype(sums.dtype)
+            for turn in range(1, group_count):
+                share_copy(layer, later, turn).start()
+            share_local(layer, later).start()
+
+        order = tick - bases[layer]
+
+        @pl.when((order >= 0) & (order < count))
+        def _():
+            part, slot = count - 1 - order, lax.rem(order, 2)
+            each_near(layer, order, lambda copy: copy.wait())
+            each_landed(layer, order, lambda copy: copy.wait())
+            for copy in state_loads(layer, order):
+                copy.wait()
+
+            def step(index, carry):
+                window = pl.ds(pl.multiple_of(index * 32, 32), 32)
+                total = parts[layer, slot, 0, window, :].astype(F32)
+                for which in range(1, 4):
+                    total = total + parts[layer, slot, which, window, :].astype(F32)
+                low = total.astype(BF)
+                grads[layer, part, window, :] = low
+                move = move_of(
+                    states[layer, slot, 0, window, :],
+                    low.astype(F32),
+                    states[layer, slot, 1, window, :],
+                    states[layer, slot, 2, window, :],
+                    INNER_RATE,
+                )
+                moves[layer, part, window, :] = move.astype(moves.dtype)
+                return carry
+
+            lax.fori_loop(0, piece // 32, step, 0)
+            for turn in range(1, group_count):
+                cross_copy(layer, order, turn).start()
+            grad_store(layer, order).start()
+
+    @pl.when(tick == 2)
+    def _():
+        small_land[spot.member] = small_grad[...]
+        for hop in range(1, members):
+            small_send_copy(hop).wait_recv()
+        total = small_land[0]
+        for member in range(1, members):
+            total = total + small_land[member]
+        small_grad_out[...] = total
+        move = move_of(small_ref[...], total, small_first[...], small_second[...], SMALL_RATE)
+        small_move[...] = move
+        small_moves[spot.group] = move
+        for turn in range(1, group_count):
+            small_cross_copy(turn).start()
+
+    @pl.when(tick == 4)
+    def _():
+        for turn in range(1, group_count):
+            small_cross_copy(turn).wait_recv()
+        total = small_moves[0]
+        for group in range(1, group_count):
+            total = total + small_moves[group]
+        small_sum_out[...] = total
+
+    @pl.when(tick == pl.num_programs(0) - 1)
+    def _():
+        engine.drain()
+        for hop in range(1, members):
+            small_send_copy(hop).wait_send()
+        for turn in range(1, group_count):
+            small_cross_copy(turn).wait_send()
+        for layer in range(2):
+            for order in range(count):
+                grad_store(layer, order).wait()
+                share_local(layer, order).wait()
+                for turn in range(1, group_count):
+                    cross_copy(layer, order, turn).wait_send()
+                    share_copy(layer, order, turn).wait_send()
+                    share_copy(layer, order, turn).wait_recv()
+
+
+def finish(grad_zero, one, weights, weight_m, weight_v, small_grad, small, small_m, small_v):
+    members, group_count = lax.axis_size("fsdp"), lax.axis_size("group")
+    chips = members // 2
+    layers, rows, width = weights.shape
+    count = chunk_count(rows)
+    piece = rows // count
+    quarter = piece // group_count
+    wire = BF if quarter % 16 == 0 else F32
+    small_size = small.shape[1]
+    dma = pltpu.SemaphoreType.DMA
+    ticks = (chips - 1) * count + chips - 1 + 1
+    anywhere = pl.BlockSpec(memory_space=pl.ANY)
+    local = pl.BlockSpec(memory_space=pltpu.VMEM)
+    crossing = dma((layers * count * group_count,))
+    return pl.pallas_call(
+        functools.partial(finish_kernel, chips, group_count),
+        grid=(ticks,),
+        in_specs=[anywhere] * 7 + [local] * 4,
+        out_specs=[anywhere, anywhere, local, local] + [anywhere] * 2,
+        out_shape=[
+            jax.ShapeDtypeStruct((layers, rows, width), BF),
+            jax.ShapeDtypeStruct((layers, rows, width), wire),
+            jax.ShapeDtypeStruct((1, small_size), F32),
+            jax.ShapeDtypeStruct((1, small_size), F32),
+        ]
+        + reduce_lands(chips, rows, width),
+        scratch_shapes=[
+            pltpu.VMEM((layers, 2, 4, piece, width), BF),
+            pltpu.VMEM((layers, 2, 3, piece, width), F32),
+            pltpu.VMEM((layers, count, piece, width), BF),
+            pltpu.VMEM((layers, count, piece, width), wire),
+            pltpu.VMEM((layers, count, group_count, quarter, width), wire),
+            pltpu.VMEM((layers, count, quarter, width), wire),
+            pltpu.VMEM((members, 1, small_size), F32),
+            pltpu.VMEM((group_count, 1, small_size), F32),
+            pltpu.VMEM((1, small_size), F32),
+            dma((8 * layers,)),
+            dma((6 * layers,)),
+            dma((layers * count,)),
+            crossing,
+            crossing,
+            crossing,
+            crossing,
+            dma((layers * count,)),
+            dma((members,)),
+            dma((members,)),
+            dma((group_count,)),
+            dma((group_count,)),
+        ]
+        + reduce_scratch(chips, rows, width),
+        compiler_params=pltpu.CompilerParams(
+            vmem_limit_bytes=VMEM_LIMIT, collective_id=3, has_side_effects=True
+        ),
+        name="finish",
+    )(grad_zero, *one, weights, weight_m, weight_v, small_grad, small, small_m, small_v)
 
 
 def weight_copies(weight_hbm, weight_ref, sems, cuts):
@@ -506,6 +1098,8 @@
 def back_kernel(
     is_first,
     head_count,
+    place,
+    query_steps,
     lengths_ref,
     slopes_ref,
     grad_ref,
@@ -519,28 +1113,70 @@
     lse_ref,
     gains_ref,
     weight_hbm,
-    two_out,
-    pre_out,
-    normed_out,
-    one_out,
-    query_grad_out,
-    key_grad_out,
-    value_grad_out,
-    input_out,
-    gains_out,
-    slopes_out,
-    weight_ref,
-    dist_ref,
-    mask_ref,
-    query_t,
-    key_t,
-    mixed_t,
-    mixed_rows,
-    delta_ref,
-    query_grad_t,
-    sems,
+    *rest,
 ):
+    if place is not None:
+        grad_rows, rest = rest[0], rest[1:]
+        landing, rest = rest[10:12], rest[:10] + rest[12:]
+        job = rest[20:]
+    (
+        two_out,
+        pre_out,
+        normed_out,
+        one_out,
+        query_grad_out,
+        key_grad_out,
+        value_grad_out,
+        input_out,
+        gains_out,
+        slopes_out,
+        weight_ref,
+        dist_ref,
+        mask_ref,
+        query_t,
+        key_t,
+        mixed_t,
+        mixed_rows,
+        delta_ref,
+        query_grad_t,
+        sems,
+    ) = rest[:20]
     step = pl.program_id(0)
+    if place is not None:
+        spot = Spot(*place)
+        engine = Reduce(
+            spot,
+            chunk_count(grad_rows.shape[0] // (2 * spot.chips)),
+            grad_rows,
+            landing[0],
+            landing[1],
+            job[0],
+            job[1],
+            job[2:],
+        )
+
+        early_ticks = engine.items - 2
+
+        @pl.when(step == 0)
+        def _():
+            meet(spot)
+            engine.start()
+
+    pairs = head_count // 2
+    sites = pairs + 2
+
+    def reduce_ticks(site):
+        if place is None:
+            return
+        total = sites * query_steps
+        here = step * sites + site
+        for index in range(-(-early_ticks // total)):
+            tick = lax.div(here * early_ticks, total) + index
+
+            @pl.when(tick < lax.div((here + 1) * early_ticks, total))
+            def _():
+                engine.tick(tick)
+
     width = weight_ref.shape[1]
     inner = (weight_ref.shape[0] - 4 * width) // 2
     queries, keys = query_ref.shape[1], key_ref.shape[1]
@@ -585,6 +1221,8 @@
         pre_grad = (back_hidden * slope_ref[0, :, columns].astype(F32)).astype(BF)
         pre_out[0, :, columns] = pre_grad
         back_normed = back_normed + dot_nn(pre_grad, weight_ref[inner_rows, :])
+        if chunk % 2 == 1 and chunk < 4:
+            reduce_ticks(chunk // 2)
     unit_one, inverse_one = norm_parts(total_one_ref[0])
     normed_out[0] = (unit_one * gains_ref[0:1] + gains_ref[1:2]).astype(BF)
     gains_out[0:1] += jnp.sum(back_normed * unit_one, axis=0, keepdims=True)
@@ -628,6 +1266,7 @@
             key_grad = key_grad + dot_nn(scores_low, query_pair * half)
             rows = pl.ds(start + which * head, head)
             query_grad_t[rows, :] = dot_nn(key_t[rows, :], scores_low)
+        reduce_ticks(pair + 2)
         key_grad_out[0, :, lanes] = (key_grad * scale).astype(BF)
         value_grad_out[0, :, lanes] = value_grad.astype(BF)
         return carry
@@ -649,9 +1288,22 @@
         input_out[0] = back_memory
     else:
         input_out[0] = back_query + back_memory
-
-
-def layer_back(is_first, grad, kept, lengths, slopes, gains, weight_full):
+    if place is not None:
+
+        @pl.when(step == pl.num_programs(0) - 1)
+        def _():
+            def late_tick(tick, carry):
+                engine.tick(tick)
+                return carry
+
+            lax.fori_loop(early_ticks, engine.ticks, late_tick, 0)
+            for part in range(engine.count):
+                engine.swap_copy(spot.chip, part).wait_recv()
+                engine.settle(part)
+            engine.drain()
+
+
+def layer_back(is_first, grad, kept, lengths, slopes, gains, weight_full, grad_rows=None):
     (query_rows, key_rows, value_rows, lse, attended, total_one, steep, total_two) = kept
     batch, queries, width = query_rows.shape
     keys = key_rows.shape[1]
@@ -679,8 +1331,17 @@
     flops = 2 * batch * width * (
         2 * queries * width + 2 * keys * width + 2 * queries * inner + 5 * queries * keys
     )
+    hosted = grad_rows is not None
+    place, job_scratch, lands, params = None, [], [], {}
+    if hosted:
+        place = (lax.axis_size("fsdp") // 2, lax.axis_size("group"))
+        shard_rows = rows // (2 * place[0])
+        job_scratch = reduce_scratch(place[0], shard_rows, width)
+        lands = reduce_lands(place[0], shard_rows, width)
+        params = dict(collective_id=2, has_side_effects=True)
+    anywhere = pl.BlockSpec(memory_space=pl.ANY)
     return pl.pallas_call(
-        functools.partial(back_kernel, is_first, head_count),
+        functools.partial(back_kernel, is_first, head_count, place, batch),
         grid_spec=pltpu.PrefetchScalarGridSpec(
             num_scalar_prefetch=2,
             grid=(batch,),
@@ -695,13 +1356,15 @@
                 block(queries, width),
                 block(head_rows, queries),
                 pl.BlockSpec((4, width), lambda i, *_: (0, 0)),
-                pl.BlockSpec(memory_space=pl.ANY),
-            ],
+                anywhere,
+            ]
+            + [anywhere] * hosted,
             out_specs=[block(length, size) for length, size, _ in outs]
             + [
                 pl.BlockSpec((4, width), lambda i, *_: (0, 0)),
                 pl.BlockSpec((head_rows, queries), lambda i, *_: (0, 0)),
-            ],
+            ]
+            + [anywhere] * len(lands),
             scratch_shapes=[
                 pltpu.VMEM((rows, width), BF),
                 pltpu.VMEM((keys, queries), F32),
@@ -713,14 +1376,16 @@
                 pltpu.VMEM((head_count, queries), F32),
                 pltpu.VMEM((width, queries), F32),
                 pltpu.SemaphoreType.DMA((4,)),
-            ],
+            ]
+            + job_scratch,
         ),
         out_shape=[shape(*out) for out in outs]
         + [
             jax.ShapeDtypeStruct((4, width), F32),
             jax.ShapeDtypeStruct((head_rows, queries), F32),
-        ],
-        compiler_params=pltpu.CompilerParams(vmem_limit_bytes=VMEM_LIMIT),
+        ]
+        + lands,
+        compiler_params=pltpu.CompilerParams(vmem_limit_bytes=VMEM_LIMIT, **params),
         cost_estimate=pl.CostEstimate(
             flops=flops, bytes_accessed=rows * width * 2 + 40000000, transcendentals=0
         ),
@@ -739,6 +1404,7 @@
         lse,
         gains,
         weight_full,
+        *([grad_rows] * hosted),
     )
 
 
@@ -795,11 +1461,6 @@
     part_size = small.shape[0] // 2
     masters_low = weights.astype(BF)
 
-    def reduce_layer(grad_rows):
-        return lax.psum_scatter(
-            grad_rows.astype(BF), "fsdp", scatter_dimension=0, tiled=True
-        ).astype(F32)
-
     gains = []
     slopes = []
     for layer in range(2):
@@ -823,38 +1484,39 @@
         gains[1],
         matrix_two,
     )
-    matrix_grad_two = matrix_gradient(low2, low2, att2, hid2, back_two[:7])
-    first_grad, matrix_grad_two = lax.optimization_barrier(
-        (back_two[7], matrix_grad_two.astype(BF))
-    )
-    shard_two = reduce_layer(matrix_grad_two)
+    matrix_grad_two = matrix_gradient(low2, low2, att2, hid2, back_two[:7]).astype(BF)
     back_one = layer_back(
         True,
-        first_grad,
+        back_two[7],
         (q1, k1, v1, lse1, att1, one1, steep1, two1),
         lengths,
         slopes[0],
         gains[0],
         matrix_one,
+        matrix_grad_two,
     )
     input_grad = back_one[7]
-    shard_one = reduce_layer(matrix_gradient(low1, hidden_in, att1, hid1, back_one[:7]))
-    grad_shard = jnp.stack([shard_one, shard_two])
+    matrix_grad_one = matrix_gradient(low1, hidden_in, att1, hid1, back_one[:7]).astype(BF)
     head_count = slopes[0].shape[0]
     small_parts = []
     for back in (back_one, back_two):
         small_parts += [back[8].reshape(-1), -jnp.sum(back[9][:head_count], axis=1)]
-    small_grad = lax.psum(jnp.concatenate(small_parts), "fsdp")
-    weight_first, weight_second, weight_move = adam_step(
-        weights, grad_shard[None], weight_m, weight_v, INNER_RATE
-    )
-    small_first, small_second, small_move = adam_step(
-        small, small_grad[None], small_m, small_v, SMALL_RATE
-    )
-    weight_sum, small_sum = (
-        lax.psum(weight_move[0].astype(BF), "group").astype(F32),
-        lax.psum(small_move[0].astype(BF), "group").astype(F32),
-    )
+    grad_shard, weight_sum, small_grad, small_sum = finish(
+        matrix_grad_one,
+        (matrix_grad_two, *back_one[10:12]),
+        weights,
+        weight_m,
+        weight_v,
+        jnp.concatenate(small_parts)[None],
+        small[None],
+        small_m,
+        small_v,
+    )[:4]
+    weight_first, weight_second, _ = adam_step(
+        weights, grad_shard[None].astype(F32), weight_m, weight_v, INNER_RATE
+    )
+    small_first, small_second, _ = adam_step(small, small_grad, small_m, small_v, SMALL_RATE)
+    weight_sum, small_sum = weight_sum.astype(F32), small_sum[0]
     group_count = lax.axis_size("group")
     weight_mean, weight_mom, weight_new = outer_step(weights, weight_sum, outer_mom, group_count)
     small_mean, small_momentum, small_after = outer_step(small, small_sum, small_mom, group_count)

time: 833 us -> 717 us (0.86)
  waiting for transfers between devices: 342 us -> 0 us
  Pallas kernels: 336 us -> 613 us
  blocking collectives: 42.3 us -> 0 us
  between operations: 14.3 us -> 1.46 us
    reduce_scatter x2 -> x0, waiting for transfers between devices: 294 us -> none  [reduce_layer(): lax.psum_scatter(grad_rows.astype(BF), 'fsdp', scatter_dimension=0, tiled...]
    pallas_call x2 -> x3, Pallas kernels: 105 us -> 383 us  [the longest x2 212 us: layer_back(): pl.pallas_call(functools.partial(back_kernel, is_first, head_count, place...]
    psum x1 -> x0, waiting for transfers between devices: 47.7 us -> none  [shards(): lax.psum(weight_move[0].astype(BF), 'group').astype(F32)]
    psum x2 -> x0, blocking collectives: 42.3 us -> none  [the longest x1 26 us: shards(): small_grad = lax.psum(jnp.concatenate(small_parts), 'fsdp')]
    convert_element_type x2 -> x0, other arithmetic: 15.2 us -> none  [the longest x1 14.4 us: shards(): weight_move[0].astype(BF)]
    add x0 -> x2, other arithmetic: none -> 8.65 us  [adam_step(): second_new = BETA_TWO * second_mom + (1.0 - BETA_TWO) * gradient * gradient]
  transfers between devices with their start and end apart: 3 -> 0, of which waited for: 3 -> 0; matrix products, arithmetic and copies ran while one was open for 0% -> 0% of each run, Pallas kernels for 0% -> 0%
where the time goes in v3:
time: 717 us; the launch traced here: 709 us
  Pallas kernels  613 us (85%)
  matrix products  53.4 us (7%)
  other arithmetic  29.5 us (4%)
  local copies, waits for them, and re-layouts  11.6 us (2%)
    pallas_call x2, Pallas kernels, layer_back(): pl.pallas_call(functools.partial(back_kernel, is_first, head_count, place...  212 us
    pallas_call x1, Pallas kernels, finish(): pl.pallas_call(functools.partial(finish_kernel, chips, group_count), grid...  171 us
    pallas_call x2, Pallas kernels, layer_ahead(): pl.pallas_call(functools.partial(ahead_kernel, is_first, head_count, plac...  152 us
    pallas_call x1, Pallas kernels, gather_rows(): pl.pallas_call(functools.partial(gather_kernel, members // 2, group_count...  78.5 us
    dot_general x12, matrix products, weight_product(): lax.dot_general(left, right, (((0, 1), (0, 1)), ((), ())), preferred_elem...  53.4 us
    convert_element_type x1, other arithmetic, shards(): weight_new.astype(BF)  16.6 us

profile of v3, /device:TPU:0, one launch (start us, length us, event | category | flops | bytes accessed | tf_op | source)
XLA Modules:
  0.0 709.2 jit_solution(7289762551618789838)
XLA Ops:
  0.6 1.3 fusion.21
  2.0 0.8 fusion.20
  2.8 0.6 reshape.44.gains_ref
  3.4 3.4 convert_element_type.15
  6.7 2.0 slice_bitcast_fusion
  8.7 78.5 %gather_rows.1.weight_hbm = bf16[9216,768]{1,0:T(8,128)(2,1)} custom-call(bf16[1152,768]{1,0:T(8,128)(2,1)} %get-tuple-element.120.shard_ref), custom_call_target="tpu_custom_call" | custom-call | tf_op jit(solution)/shard_map/gather_rows/pallas_call | solution.py:270
  87.2 103.8 %layer_ahead.2 = (bf16[4,256,768]{2,1,0:T(8,128)(2,1)}, bf16[4,512,768]{2,1,0:T(8,128)(2,1)}, bf16[4,512,768]{2,1,0:T(8,128)(2,1)}, f32[4,16,256]{2,1,0:T(8,128)...) custom-call(s32[4]{0:T(128)} %lengths_ref.7, ...), custom_call_target="tpu_custom_call" | custom-call | flops 18522046464 | bytes 44155776 | tf_op jit(solution)/shard_map/layer_ahead/pallas_call | solution.py:1066
  191.7 47.9 %layer_ahead.3 = (bf16[4,256,768]{2,1,0:T(8,128)(2,1)}, bf16[4,256,768]{2,1,0:T(8,128)(2,1)}, bf16[4,256,768]{2,1,0:T(8,128)(2,1)}, f32[4,16,256]{2,1,0:T(8,128)...) custom-call(s32[4]{0:T(128)} %lengths_ref.7, ...), custom_call_target="tpu_custom_call" | custom-call | flops 15300820992 | bytes 44155776 | tf_op jit(solution)/shard_map/layer_ahead/pallas_call | solution.py:1066
  239.6 46.2 %layer_back.2 = (bf16[4,256,768]{2,1,0:T(8,128)(2,1)}, bf16[4,256,3072]{2,1,0:T(8,128)(2,1)}, bf16[4,256,768]{2,1,0:T(8,128)(2,1)}, bf16[4,256,768]{2,1,0:T(8,12...) custom-call(s32[4]{0:T(128)} %lengths_ref.7, ...), custom_call_target="tpu_custom_call" | custom-call | flops 16508780544 | bytes 54155776 | tf_op jit(solution)/shard_map/layer_back/pallas_call | solution.py:1343
  285.8 4.0 fusion.8
  289.8 2.6 fusion.9
  292.3 2.5 fusion.10
  294.8 2.5 fusion.11
  297.4 6.9 fusion.4
  304.3 6.9 fusion.5.rest_0_.grad_one
  311.2 166.3 %layer_back.3 = (bf16[4,256,768]{2,1,0:T(8,128)(2,1)}, bf16[4,256,3072]{2,1,0:T(8,128)(2,1)}, bf16[4,256,768]{2,1,0:T(8,128)(2,1)}, bf16[4,256,768]{2,1,0:T(8,12...) custom-call(s32[4]{0:T(128)} %lengths_ref.7, ...), custom_call_target="tpu_custom_call" | custom-call | flops 20937965568 | bytes 54155776 | tf_op jit(solution)/shard_map/layer_back/pallas_call | solution.py:1343
  477.5 4.0 fusion.12
  481.6 3.7 fusion.15
  485.3 3.8 fusion.17
  489.1 2.5 fusion.13
  491.6 6.9 fusion.6
  498.5 7.2 %fusion.7.grad_zero = bf16[9216,768]{1,0:T(8,128)(2,1)} fusion(bf16[9216,768]{1,0:T(8,128)(2,1)} %fusion.6, bf16[4,256,3072]{2,1,0:T(8,128)(2,1)S(1)} %bitcast.103, bf16[4,256,768]{2,1,0:T(8,128)(2,1)S(1)} %copy-done.22), kind=kOutput, calls=%fused_computation.16 | convolution fusion | flops 4834197504 | bytes 12582912 | tf_op jit(solution)/shard_map/dot_general | solution.py:1412
  506.1 0.6 broadcast_in_dim.7.small_grad
  506.7 0.6 broadcast_in_dim.8.small_ref
  507.4 170.7 %finish.1 = (bf16[2,1152,768]{2,1,0:T(8,128)(2,1)}, bf16[2,1152,768]{2,1,0:T(8,128)(2,1)}, f32[1,6168]{1,0:T(1,128)}, f32[1,6168]{1,0:T(1,128)}, bf16[4608,768]{1,0:T(8,128)(2,1)}, /*index=5*/bf16[6912,768]{1,0:T(8,128)(2,1)}) custom-call(bf16[9216,768]{1,0:T(8,128)(2,1)} %fusion.7.grad_zero, bf16[9216,768]{1,0:T(8,128)(2,1)} %fusion.5.rest_0_.grad_one, ...), custom_call_target="tpu_custom_call" | custom-call | tf_op jit(solution)/shard_map/finish/pallas_call | solution.py:830
  678.1 16.6 %fusion.19 = (bf16[2,1152,768]{2,1,0:T(8,128)(2,1)}, f32[2,1152,768]{2,1,0:T(8,128)}, f32[2,1152,768]{2,1,0:T(8,128)}, f32[2,1152,768]{2,1,0:T(8,128)}) fusion(f32[2,1152,768]{2,1,0:T(8,128)} %weight_hbm.1, f32[2,1152,768]{2,1,0:T(8,128)} %param.17, bf16[2,1152,768]{2,1,0:T(8,128)(2,1)} %get-tuple-element.107), kind=kLoop, calls=%fused_computation.45 | loop fusion | flops 15925248 | bytes 42467328 | tf_op jit(solution)/shard_map/convert_element_type | solution.py:1527
  694.7 1.2 slice-done.1
  695.8 0.8 slice-done.3
  696.7 7.9 %fusion.3 = (f32[1,2,1152,768]{3,2,1,0:T(8,128)}, f32[1,2,1152,768]{3,2,1,0:T(8,128)}) fusion(bf16[2,1152,768]{2,1,0:T(8,128)(2,1)} %get-tuple-element.108, f32[1,2,1152,768]{3,2,1,0:T(8,128)S(1)} %bitcast.99, f32[1,2,1152,768]{3,2,1,0:T(8,128)S(1)} %bitcast.97), kind=kLoop, calls=%fused_computation.9 | loop fusion | flops 14155776 | bytes 31850496 | tf_op jit(solution)/shard_map/add | solution.py:1434
  704.7 0.7 fusion.18
  705.4 0.6 multiply_subtract_fusion.1
  706.0 2.7 copy.59
  (93 shorter events, 1.1 us)
Async XLA Ops:
  239.6 46.2 %copy-start.14 = (bf16[4,256,768]{2,1,0:T(8,128)(2,1)S(1)}, bf16[4,256,768]{2,1,0:T(8,128)(2,1)}, u32[]{:S(2)}) copy-start(bf16[4,256,768]{2,1,0:T(8,128)(2,1)} %get-tuple-element.82) | copy-start | bytes 4718596
  285.8 4.0 copy-start.18
  289.8 7.6 %slice-start.12 = ((s8[6291456]{0:T(1024)(128)(4,1)}), s8[4194304]{0:T(1024)(128)(4,1)S(1)}, s32[]{:S(2)}) async-start(s8[6291456]{0:T(1024)(128)(4,1)} %bitcast.108), calls=%async_computation.12 | async-start | bytes 8388608
  292.3 5.0 slice-start.13
  294.8 9.5 %slice-start.8 = ((s8[6291456]{0:T(1024)(128)(4,1)}), s8[4194304]{0:T(1024)(128)(4,1)S(1)}, s32[]{:S(2)}) async-start(s8[6291456]{0:T(1024)(128)(4,1)} %bitcast.104), calls=%async_computation.8 | async-start | bytes 8388608
  297.4 6.9 slice-start.9
  297.4 6.9 copy-start.23
  311.2 166.3 %copy-start.19 = (bf16[4,256,768]{2,1,0:T(8,128)(2,1)S(1)}, bf16[4,256,768]{2,1,0:T(8,128)(2,1)}, u32[]{:S(2)}) copy-start(bf16[4,256,768]{2,1,0:T(8,128)(2,1)} %get-tuple-element.92) | copy-start | bytes 4718596
  477.5 4.1 copy-start.11
  477.5 4.1 copy-start.21
  481.5 10.0 %slice-start.10 = ((s8[6291456]{0:T(1024)(128)(4,1)}), s8[4194304]{0:T(1024)(128)(4,1)S(1)}, s32[]{:S(2)}) async-start(s8[6291456]{0:T(1024)(128)(4,1)} %bitcast.106), calls=%async_computation.10 | async-start | bytes 8388608
  485.3 3.8 copy-start.15
  485.3 6.2 slice-start.11
  489.0 9.4 %slice-start.6 = ((s8[6291456]{0:T(1024)(128)(4,1)}), s8[2097152]{0:T(1024)(128)(4,1)S(1)}, s32[]{:S(2)}) async-start(s8[6291456]{0:T(1024)(128)(4,1)} %bitcast.102), calls=%async_computation.6 | async-start | bytes 4194304
  491.5 6.9 slice-start.7
  491.5 6.9 copy-start.22
  498.5 7.3 %copy-start.10 = (f32[4,768]{1,0:T(4,128)S(1)}, f32[4,768]{1,0:T(4,128)}, u32[]{:S(2)}) copy-start(f32[4,768]{1,0:T(4,128)} %get-tuple-element.103) | copy-start | bytes 36868
  498.5 7.3 %copy-start.8 = (f32[16,256]{1,0:T(8,128)S(1)}, f32[16,256]{1,0:T(8,128)}, u32[]{:S(2)}) copy-start(f32[16,256]{1,0:T(8,128)} %get-tuple-element.104) | copy-start | bytes 49156
  498.5 7.4 %copy-start.9 = (f32[4,768]{1,0:T(4,128)S(1)}, f32[4,768]{1,0:T(4,128)}, u32[]{:S(2)}) copy-start(f32[4,768]{1,0:T(4,128)} %get-tuple-element.105) | copy-start | bytes 36868
  498.5 7.4 %copy-start.7 = (f32[16,256]{1,0:T(8,128)S(1)}, f32[16,256]{1,0:T(8,128)}, u32[]{:S(2)}) copy-start(f32[16,256]{1,0:T(8,128)} %get-tuple-element.106) | copy-start | bytes 49156
  498.5 8.2 %copy-start = (f32[6168]{0:T(1024)S(1)}, f32[6168]{0:T(1024)}, u32[]{:S(2)}) copy-start(f32[6168]{0:T(1024)} %param.18) | copy-start | bytes 74020
  678.0 16.6 %slice-start = ((s8[7077888]{0:T(1024)(128)(4,1)}), s8[4194304]{0:T(1024)(128)(4,1)S(1)}, s32[]{:S(2)}) async-start(s8[7077888]{0:T(1024)(128)(4,1)} %bitcast.96), calls=%async_computation | async-start | bytes 8388608
  678.0 16.6 %slice-start.2 = ((s8[7077888]{0:T(1024)(128)(4,1)}), s8[4194304]{0:T(1024)(128)(4,1)S(1)}, s32[]{:S(2)}) async-start(s8[7077888]{0:T(1024)(128)(4,1)} %bitcast.98), calls=%async_computation.2 | async-start | bytes 8388608
  678.0 17.8 %slice-start.1 = ((s8[7077888]{0:T(1024)(128)(4,1)}), s8[2883584]{0:T(1024)(128)(4,1)S(1)}, s32[]{:S(2)}) async-start(s8[7077888]{0:T(1024)(128)(4,1)} %bitcast.96), calls=%async_computation.1 | async-start | bytes 5767168
  678.1 18.6 %slice-start.3 = ((s8[7077888]{0:T(1024)(128)(4,1)}), s8[2883584]{0:T(1024)(128)(4,1)S(1)}, s32[]{:S(2)}) async-start(s8[7077888]{0:T(1024)(128)(4,1)} %bitcast.98), calls=%async_computation.3 | async-start | bytes 5767168
  694.7 11.4 %slice-start.4 = ((s8[6291456]{0:T(1024)(128)(4,1)}), s8[4194304]{0:T(1024)(128)(4,1)S(1)}, s32[]{:S(2)}) async-start(s8[6291456]{0:T(1024)(128)(4,1)} %bitcast.100), calls=%async_computation.4 | async-start | bytes 8388608
  696.7 8.0 %copy-start.2 = (f32[1,6168]{1,0:T(1,128)S(1)}, f32[1,6168]{1,0:T(1,128)}, u32[]{:S(2)}) copy-start(f32[1,6168]{1,0:T(1,128)} %small_first.1) | copy-start | bytes 74020
  696.7 8.0 %copy-start.3 = (f32[1,6168]{1,0:T(1,128)S(1)}, f32[1,6168]{1,0:T(1,128)}, u32[]{:S(2)}) copy-start(f32[1,6168]{1,0:T(1,128)} %small_second.1) | copy-start | bytes 74020
  696.7 8.0 %copy-start.5 = (f32[1,6168]{1,0:T(1,128)S(1)}, f32[1,6168]{1,0:T(1,128)}, u32[]{:S(2)}) copy-start(f32[1,6168]{1,0:T(1,128)} %get-tuple-element.110) | copy-start | bytes 74020
  696.7 8.0 %copy-start.6 = (f32[1,6168]{1,0:T(1,128)S(1)}, f32[1,6168]{1,0:T(1,128)}, u32[]{:S(2)}) copy-start(f32[1,6168]{1,0:T(1,128)} %get-tuple-element.109) | copy-start | bytes 74020
  696.7 8.7 %copy-start.4 = (f32[6168]{0:T(1024)S(1)}, f32[6168]{0:T(1024)}, u32[]{:S(2)}) copy-start(f32[6168]{0:T(1024)} %param.21) | copy-start | bytes 74020
  696.7 9.3 %slice-start.5 = ((s8[6291456]{0:T(1024)(128)(4,1)}), s8[2097152]{0:T(1024)(128)(4,1)S(1)}, s32[]{:S(2)}) async-start(s8[6291456]{0:T(1024)(128)(4,1)} %bitcast.100), calls=%async_computation.5 | async-start | bytes 4194304
  (8 other events, 23.4 us)

commit v4 on v3

--- a/solution.py
+++ b/solution.py
@@ -496,9 +496,7 @@
     chips,
     group_count,
     grad_zero,
-    grad_one,
-    swap_one,
-    lands_one,
+    shard_one,
     weight_hbm,
     first_hbm,
     second_hbm,
@@ -553,7 +551,6 @@
     )
     members = 2 * chips
     last = chips - 1
-    tops = ((grad_zero, swap_zero, lands_zero), (grad_one, swap_one, lands_one))
 
     def small_send_copy(hop):
         target = lax.rem(spot.member + hop, members)
@@ -595,17 +592,16 @@
     bases = (engine.ticks - count, 1)
 
     def part_loads(layer, order):
-        top = tops[layer]
         part, slot = count - 1 - order, lax.rem(order, 2)
         here = pl.multiple_of(part * piece, 8)
         start = (2 * spot.chip + spot.core) * rows + here
-        sources = (
-            top[0].at[pl.ds(pl.multiple_of(start, 8), piece)],
-            top[1].at[pl.ds(pl.multiple_of(spot.chip * rows + here, 8), piece)],
-            top[2].at[
+        sources = (shard_one.at[pl.ds(here, piece)],) if layer == 1 else (
+            grad_zero.at[pl.ds(pl.multiple_of(start, 8), piece)],
+            swap_zero.at[pl.ds(pl.multiple_of(spot.chip * rows + here, 8), piece)],
+            lands_zero.at[
                 pl.ds(pl.multiple_of(((last - spot.chip) * count + order) * piece, 8), piece)
             ],
-            top[2].at[
+            lands_zero.at[
                 pl.ds(
                     pl.multiple_of(
                         ((2 * last - 1 - spot.chip) * count + order) * piece, 8
@@ -642,10 +638,12 @@
 
     def each_near(layer, order, act):
         copies = part_loads(layer, order)
-        act(copies[0])
-        act(copies[1])
+        for copy in copies[:2]:
+            act(copy)
 
     def each_landed(layer, order, act):
+        if layer == 1:
+            return
         copies = part_loads(layer, order)
 
         @pl.when(spot.chip > 0)
@@ -707,8 +705,6 @@
             def _():
                 if layer == 0:
                     engine.swap_copy(spot.chip, count - 1 - order).wait_recv()
-                else:
-                    each_landed(layer, order, lambda copy: copy.start())
                 each_near(layer, order, lambda copy: copy.start())
                 for copy in state_loads(layer, order):
                     copy.start()
@@ -813,7 +809,7 @@
                     share_copy(layer, order, turn).wait_recv()
 
 
-def finish(grad_zero, one, weights, weight_m, weight_v, small_grad, small, small_m, small_v):
+def finish(grad_zero, shard_one, weights, weight_m, weight_v, small_grad, small, small_m, small_v):
     members, group_count = lax.axis_size("fsdp"), lax.axis_size("group")
     chips = members // 2
     layers, rows, width = weights.shape
@@ -830,7 +826,7 @@
     return pl.pallas_call(
         functools.partial(finish_kernel, chips, group_count),
         grid=(ticks,),
-        in_specs=[anywhere] * 7 + [local] * 4,
+        in_specs=[anywhere] * 5 + [local] * 4,
         out_specs=[anywhere, anywhere, local, local] + [anywhere] * 2,
         out_shape=[
             jax.ShapeDtypeStruct((layers, rows, width), BF),
@@ -867,7 +863,7 @@
             vmem_limit_bytes=VMEM_LIMIT, collective_id=3, has_side_effects=True
         ),
         name="finish",
-    )(grad_zero, *one, weights, weight_m, weight_v, small_grad, small, small_m, small_v)
+    )(grad_zero, shard_one, weights, weight_m, weight_v, small_grad, small, small_m, small_v)
 
 
 def weight_copies(weight_hbm, weight_ref, sems, cuts):
@@ -1155,12 +1151,13 @@
             job[2:],
         )
 
-        early_ticks = engine.items - 2
+        early_ticks = engine.ticks - 1
 
         @pl.when(step == 0)
         def _():
             meet(spot)
             engine.start()
+            engine.tick(0)
 
     pairs = head_count // 2
     sites = pairs + 2
@@ -1171,9 +1168,9 @@
         total = sites * query_steps
         here = step * sites + site
         for index in range(-(-early_ticks // total)):
-            tick = lax.div(here * early_ticks, total) + index
-
-            @pl.when(tick < lax.div((here + 1) * early_ticks, total))
+            tick = lax.div(here * early_ticks, total) + index + 1
+
+            @pl.when(tick <= lax.div((here + 1) * early_ticks, total))
             def _():
                 engine.tick(tick)
 
@@ -1296,7 +1293,7 @@
                 engine.tick(tick)
                 return carry
 
-            lax.fori_loop(early_ticks, engine.ticks, late_tick, 0)
+            lax.fori_loop(early_ticks + 1, engine.ticks, late_tick, 0)
             for part in range(engine.count):
                 engine.swap_copy(spot.chip, part).wait_recv()
                 engine.settle(part)
@@ -1459,7 +1456,7 @@
 ):
     width = weights.shape[2]
     part_size = small.shape[0] // 2
-    masters_low = weights.astype(BF)
+    masters_low = [weights[layer].astype(BF) for layer in range(2)]
 
     gains = []
     slopes = []
@@ -1468,9 +1465,10 @@
         gains.append(part[: 4 * width].reshape(4, width))
         slopes.append(part[4 * width :])
 
+    matrix_two = lax.all_gather(masters_low[1], "fsdp", axis=0, tiled=True)
     matrix_one = gather_rows(masters_low[0])
-    (q1, k1, v1, lse1, att1, one1, hid1, steep1, two1, first_out, low1, matrix_two) = layer_ahead(
-        True, hidden_in, lengths, slopes[0], gains[0], matrix_one, F32, masters_low[1]
+    (q1, k1, v1, lse1, att1, one1, hid1, steep1, two1, first_out, low1) = layer_ahead(
+        True, hidden_in, lengths, slopes[0], gains[0], matrix_one, F32
     )
     (q2, k2, v2, lse2, att2, one2, hid2, steep2, two2, block_out, low2) = layer_ahead(
         False, first_out, lengths, slopes[1], gains[1], matrix_two, BF
@@ -1485,15 +1483,16 @@
         matrix_two,
     )
     matrix_grad_two = matrix_gradient(low2, low2, att2, hid2, back_two[:7]).astype(BF)
+    first_grad, matrix_grad_two = lax.optimization_barrier((back_two[7], matrix_grad_two))
+    shard_two = lax.psum_scatter(matrix_grad_two, "fsdp", scatter_dimension=0, tiled=True)
     back_one = layer_back(
         True,
-        back_two[7],
+        first_grad,
         (q1, k1, v1, lse1, att1, one1, steep1, two1),
         lengths,
         slopes[0],
         gains[0],
         matrix_one,
-        matrix_grad_two,
     )
     input_grad = back_one[7]
     matrix_grad_one = matrix_gradient(low1, hidden_in, att1, hid1, back_one[:7]).astype(BF)
@@ -1503,7 +1502,7 @@
         small_parts += [back[8].reshape(-1), -jnp.sum(back[9][:head_count], axis=1)]
     grad_shard, weight_sum, small_grad, small_sum = finish(
         matrix_grad_one,
-        (matrix_grad_two, *back_one[10:12]),
+        shard_two,
         weights,
         weight_m,
         weight_v,

time: 717 us -> 654 us (0.912)
  Pallas kernels: 613 us -> 468 us
  waiting for transfers between devices: 0 us -> 72.5 us
  between operations: 1.46 us -> 14.6 us
    pallas_call x2, Pallas kernels: 212 us -> 106 us  [layer_back(): pl.pallas_call(functools.partial(back_kernel, is_first, head_count, place...]
    reduce_scatter x0 -> x1, waiting for transfers between devices: none -> 67.1 us  [shards(): lax.psum_scatter(matrix_grad_two, 'fsdp', scatter_dimension=0, tiled=True)]
    pallas_call x2, Pallas kernels: 152 us -> 107 us  [layer_ahead(): pl.pallas_call(functools.partial(ahead_kernel, is_first, head_count, plac...]
    pallas_call x1, Pallas kernels: 78.5 us -> 94.5 us  [gather_rows(): pl.pallas_call(functools.partial(gather_kernel, members // 2, group_count...]
    pallas_call x1, Pallas kernels: 171 us -> 161 us  [finish(): pl.pallas_call(functools.partial(finish_kernel, chips, group_count), grid...]
  transfers between devices with their start and end apart: 0 -> 2, of which waited for: 0 -> 2; matrix products, arithmetic and copies ran while one was open for 0% -> 5% of each run, Pallas kernels for 0% -> 33%
where the time goes in v4:
time: 654 us; the launch traced here: 645 us
  Pallas kernels  468 us (72%)
  waiting for transfers between devices  72.5 us (11%)
  matrix products  53.5 us (8%)
  other arithmetic  28.5 us (4%)
  between operations  14.6 us (2%)
  local copies, waits for them, and re-layouts  7.93 us (1%)
    pallas_call x1, Pallas kernels, finish(): pl.pallas_call(functools.partial(finish_kernel, chips, group_count), grid...  161 us
    pallas_call x2, Pallas kernels, layer_ahead(): pl.pallas_call(functools.partial(ahead_kernel, is_first, head_count, plac...  107 us
    pallas_call x2, Pallas kernels, layer_back(): pl.pallas_call(functools.partial(back_kernel, is_first, head_count, place...  106 us
    pallas_call x1, Pallas kernels, gather_rows(): pl.pallas_call(functools.partial(gather_kernel, members // 2, group_count...  94.5 us
    reduce_scatter x1, waiting for transfers between devices, shards(): lax.psum_scatter(matrix_grad_two, 'fsdp', scatter_dimension=0, tiled=True)  67.1 us
    dot_general x12, matrix products, weight_product(): lax.dot_general(left, right, (((0, 1), (0, 1)), ((), ())), preferred_elem...  53.5 us
  transfers between devices with their start and end apart: 2, of which 2 were waited for; matrix products, arithmetic and copies ran while one was open for 5% of the time, Pallas kernels for 33%

profile of v4, /device:TPU:0, one launch (start us, length us, event | category | flops | bytes accessed | tf_op | source)
XLA Modules:
  0.0 645.2 jit_solution(2741011455780579839)
XLA Ops:
  7.2 3.4 convert.42
  10.6 2.0 fusion.20
  12.7 94.5 %gather_rows.1.weight_hbm = bf16[9216,768]{1,0:T(8,128)(2,1)} custom-call(bf16[1152,768]{1,0:T(8,128)(2,1)} %get-tuple-element.118.shard_ref), custom_call_target="tpu_custom_call" | custom-call | tf_op jit(solution)/shard_map/gather_rows/pallas_call | solution.py:270
  109.1 59.1 %layer_ahead.2 = (bf16[4,256,768]{2,1,0:T(8,128)(2,1)}, bf16[4,512,768]{2,1,0:T(8,128)(2,1)}, bf16[4,512,768]{2,1,0:T(8,128)(2,1)}, f32[4,16,256]{2,1,0:T(8,128)...) custom-call(s32[4]{0:T(128)} %lengths_ref.7, ...), custom_call_target="tpu_custom_call" | custom-call | flops 18522046464 | bytes 44155776 | tf_op jit(solution)/shard_map/layer_ahead/pallas_call | solution.py:1062
  168.2 5.4 all-gather.3.cloned.1.call-done
  173.5 47.8 %layer_ahead.3 = (bf16[4,256,768]{2,1,0:T(8,128)(2,1)}, bf16[4,256,768]{2,1,0:T(8,128)(2,1)}, bf16[4,256,768]{2,1,0:T(8,128)(2,1)}, f32[4,16,256]{2,1,0:T(8,128)...) custom-call(s32[4]{0:T(128)} %lengths_ref.7, ...), custom_call_target="tpu_custom_call" | custom-call | flops 15300820992 | bytes 44155776 | tf_op jit(solution)/shard_map/layer_ahead/pallas_call | solution.py:1062
  221.4 45.9 %layer_back.2 = (bf16[4,256,768]{2,1,0:T(8,128)(2,1)}, bf16[4,256,3072]{2,1,0:T(8,128)(2,1)}, bf16[4,256,768]{2,1,0:T(8,128)(2,1)}, bf16[4,256,768]{2,1,0:T(8,12...) custom-call(s32[4]{0:T(128)} %lengths_ref.7, ...), custom_call_target="tpu_custom_call" | custom-call | flops 16508780544 | bytes 54155776 | tf_op jit(solution)/shard_map/layer_back/pallas_call | solution.py:1340
  267.3 4.0 fusion.8
  271.4 2.5 fusion.9
  273.8 2.5 fusion.10
  276.4 2.5 fusion.11
  278.9 7.0 %fusion.4 = bf16[9216,768]{1,0:T(8,128)(2,1)} fusion(bf16[9216,768]{1,0:T(8,128)(2,1)} %fusion.11, bf16[4,256,3072]{2,1,0:T(8,128)(2,1)S(1)} %bitcast.108, bf16[4,256,768]{2,1,0:T(8,128)(2,1)S(1)} %copy-done.23), kind=kOutput, calls=%fused_computation.13 | convolution fusion | flops 4834197504 | bytes 12582912 | tf_op jit(solution)/shard_map/dot_general | solution.py:1409
  285.8 6.9 %fusion.5 = bf16[9216,768]{1,0:T(8,128)(2,1)} fusion(bf16[9216,768]{1,0:T(8,128)(2,1)} %fusion.4, bf16[4,256,3072]{2,1,0:T(8,128)(2,1)S(1)} %bitcast.106, bf16[4,256,768]{2,1,0:T(8,128)(2,1)S(1)} %copy-done.22), kind=kOutput, calls=%fused_computation.14 | convolution fusion | flops 4834197504 | bytes 12582912 | tf_op jit(solution)/shard_map/dot_general | solution.py:1409
  292.7 0.6 broadcast_in_dim.8.small_ref
  293.4 59.6 %layer_back.3 = (bf16[4,256,768]{2,1,0:T(8,128)(2,1)}, bf16[4,256,3072]{2,1,0:T(8,128)(2,1)}, bf16[4,256,768]{2,1,0:T(8,128)(2,1)}, bf16[4,256,768]{2,1,0:T(8,12...) custom-call(s32[4]{0:T(128)} %lengths_ref.7, ...), custom_call_target="tpu_custom_call" | custom-call | flops 20937965568 | bytes 54155776 | tf_op jit(solution)/shard_map/layer_back/pallas_call | solution.py:1340
  353.0 0.7 reshape.48
  353.7 0.8 slice_reduce_fusion.1
  354.8 0.6 broadcast_in_dim.7.small_grad
  355.4 4.2 fusion.12
  359.6 3.7 fusion.15
  363.3 3.7 fusion.17
  367.0 2.5 fusion.13
  369.5 7.0 %fusion.6 = bf16[9216,768]{1,0:T(8,128)(2,1)} fusion(bf16[9216,768]{1,0:T(8,128)(2,1)} %fusion.13, bf16[4,256,3072]{2,1,0:T(8,128)(2,1)S(1)} %bitcast.104, bf16[4,256,768]{2,1,0:T(8,128)(2,1)S(1)} %copy-done.21), kind=kOutput, calls=%fused_computation.15 | convolution fusion | flops 4834197504 | bytes 12582912 | tf_op jit(solution)/shard_map/dot_general | solution.py:1409
  376.5 7.1 %fusion.7.grad_zero = bf16[9216,768]{1,0:T(8,128)(2,1)} fusion(bf16[9216,768]{1,0:T(8,128)(2,1)} %fusion.6, bf16[4,256,3072]{2,1,0:T(8,128)(2,1)S(1)} %bitcast.102, bf16[4,256,768]{2,1,0:T(8,128)(2,1)S(1)} %copy-done.20), kind=kOutput, calls=%fused_computation.16 | convolution fusion | flops 4834197504 | bytes 12582912 | tf_op jit(solution)/shard_map/dot_general | solution.py:1409
  383.7 67.1 %reduce-scatter.2.cloned.1.call-done.shard_one = bf16[1152,768]{1,0:T(8,128)(2,1)} async-done(((bf16[9216,768]{1,0:T(8,128)(2,1)}), bf16[1152,768]{1,0:T(8,128)(2,1)}) %reduce-scatter.2.cloned.1.call-update) | async-done | bytes 1769488 | tf_op jit(solution)/shard_map/reduce_scatter | solution.py:1487
  450.8 161.1 %finish.1 = (bf16[2,1152,768]{2,1,0:T(8,128)(2,1)}, bf16[2,1152,768]{2,1,0:T(8,128)(2,1)}, f32[1,6168]{1,0:T(1,128)}, f32[1,6168]{1,0:T(1,128)}, bf16[4608,768]{1,0:T(8,128)(2,1)}, /*index=5*/bf16[6912,768]{1,0:T(8,128)(2,1)}) custom-call(bf16[9216,768]{1,0:T(8,128)(2,1)} %fusion.7.grad_zero, bf16[1152,768]{1,0:T(8,128)(2,1)} %reduce-scatter.2.cloned.1.call-done.shard_one, ...), custom_call_target="tpu_custom_call" | custom-call | tf_op jit(solution)/shard_map/finish/pallas_call | solution.py:826
  612.0 12.2 %fusion.3 = (f32[1,2,1152,768]{3,2,1,0:T(8,128)}, f32[1,2,1152,768]{3,2,1,0:T(8,128)}) fusion(bf16[2,1152,768]{2,1,0:T(8,128)(2,1)} %get-tuple-element.106, f32[1,2,1152,768]{3,2,1,0:T(8,128)} %second_hbm.1, f32[1,2,1152,768]{3,2,1,0:T(8,128)} %first_hbm.1), kind=kLoop, calls=%fused_computation.9 | loop fusion | flops 14155776 | bytes 31850496 | tf_op jit(solution)/shard_map/add | solution.py:1431
  624.2 0.7 fusion.18
  624.9 0.6 multiply_subtract_fusion.1
  625.7 0.8 slice-done.1
  626.6 0.8 slice-done.3
  627.4 10.7 %fusion.19 = (bf16[2,1152,768]{2,1,0:T(8,128)(2,1)}, f32[2,1152,768]{2,1,0:T(8,128)}, f32[2,1152,768]{2,1,0:T(8,128)}, f32[2,1152,768]{2,1,0:T(8,128)}) fusion(f32[2,1152,768]{2,1,0:T(8,128)S(1)} %bitcast.96, f32[2,1152,768]{2,1,0:T(8,128)S(1)} %bitcast.98, bf16[2,1152,768]{2,1,0:T(8,128)(2,1)} %get-tuple-element.105), kind=kLoop, calls=%fused_computation.44 | loop fusion | flops 15925248 | bytes 42467328 | tf_op jit(solution)/shard_map/convert_element_type | solution.py:1526
  (89 shorter events, 2.5 us)
Async XLA Ops:
  7.2 166.4 %all-gather.3.cloned.1.call-start = ((), (), s32[]{:S(2)}) async-start(), calls=%async_computation.2 | async-start | bytes 15925248 | tf_op jit(solution)/shard_map/all_gather | solution.py:1468
  12.6 438.2 %reduce-scatter.2.cloned.1.call-start = ((), (), s32[]{:S(2)}) async-start(), calls=%async_computation.1 | async-start | bytes 15925248 | tf_op jit(solution)/shard_map/reduce_scatter | solution.py:1487
  12.7 94.6 %copy-start = (f32[6168]{0:T(1024)S(1)}, f32[6168]{0:T(1024)}, u32[]{:S(2)}) copy-start(f32[6168]{0:T(1024)} %param.18) | copy-start | bytes 74020
  221.4 45.9 %copy-start.13 = (bf16[4,256,768]{2,1,0:T(8,128)(2,1)S(1)}, bf16[4,256,768]{2,1,0:T(8,128)(2,1)}, u32[]{:S(2)}) copy-start(bf16[4,256,768]{2,1,0:T(8,128)(2,1)} %get-tuple-element.72) | copy-start | bytes 4718596
  267.3 4.0 copy-start.16
  271.4 7.5 %slice-start.10 = ((s8[6291456]{0:T(1024)(128)(4,1)}), s8[4194304]{0:T(1024)(128)(4,1)S(1)}, s32[]{:S(2)}) async-start(s8[6291456]{0:T(1024)(128)(4,1)} %bitcast.107), calls=%async_computation.13 | async-start | bytes 8388608
  273.8 5.0 slice-start.11
  276.4 9.5 %slice-start.8 = ((s8[6291456]{0:T(1024)(128)(4,1)}), s8[4194304]{0:T(1024)(128)(4,1)S(1)}, s32[]{:S(2)}) async-start(s8[6291456]{0:T(1024)(128)(4,1)} %bitcast.105), calls=%async_computation.11 | async-start | bytes 8388608
  278.8 7.0 %slice-start.9 = ((s8[6291456]{0:T(1024)(128)(4,1)}), s8[2097152]{0:T(1024)(128)(4,1)S(1)}, s32[]{:S(2)}) async-start(s8[6291456]{0:T(1024)(128)(4,1)} %bitcast.105), calls=%async_computation.12 | async-start | bytes 4194304
  278.9 7.0 %copy-start.22 = (bf16[4,256,768]{2,1,0:T(8,128)(2,1)S(1)}, bf16[4,256,768]{2,1,0:T(8,128)(2,1)}, u32[]{:S(2)}) copy-start(bf16[4,256,768]{2,1,0:T(8,128)(2,1)} %get-tuple-element.80) | copy-start | bytes 4718596
  293.4 61.2 %copy-start.8 = (f32[4,768]{1,0:T(4,128)S(1)}, f32[4,768]{1,0:T(4,128)}, u32[]{:S(2)}) copy-start(f32[4,768]{1,0:T(4,128)} %get-tuple-element.103) | copy-start | bytes 36868
  293.4 61.2 %copy-start.7 = (f32[16,256]{1,0:T(8,128)S(1)}, f32[16,256]{1,0:T(8,128)}, u32[]{:S(2)}) copy-start(f32[16,256]{1,0:T(8,128)} %get-tuple-element.104) | copy-start | bytes 49156
  293.4 62.1 %copy-start.17 = (bf16[4,256,768]{2,1,0:T(8,128)(2,1)S(1)}, bf16[4,256,768]{2,1,0:T(8,128)(2,1)}, u32[]{:S(2)}) copy-start(bf16[4,256,768]{2,1,0:T(8,128)(2,1)} %get-tuple-element.91) | copy-start | bytes 4718596
  355.4 4.2 copy-start.9
  355.4 4.2 copy-start.19
  359.6 3.7 copy-start.18
  359.6 9.9 %slice-start.6 = ((s8[6291456]{0:T(1024)(128)(4,1)}), s8[4194304]{0:T(1024)(128)(4,1)S(1)}, s32[]{:S(2)}) async-start(s8[6291456]{0:T(1024)(128)(4,1)} %bitcast.103), calls=%async_computation.9 | async-start | bytes 8388608
  363.3 3.7 copy-start.11
  363.3 6.2 slice-start.7
  367.0 9.5 %slice-start.4 = ((s8[6291456]{0:T(1024)(128)(4,1)}), s8[2097152]{0:T(1024)(128)(4,1)S(1)}, s32[]{:S(2)}) async-start(s8[6291456]{0:T(1024)(128)(4,1)} %bitcast.101), calls=%async_computation.7 | async-start | bytes 4194304
  369.5 7.0 %slice-start.5 = ((s8[6291456]{0:T(1024)(128)(4,1)}), s8[4194304]{0:T(1024)(128)(4,1)S(1)}, s32[]{:S(2)}) async-start(s8[6291456]{0:T(1024)(128)(4,1)} %bitcast.101), calls=%async_computation.8 | async-start | bytes 8388608
  369.5 7.0 %copy-start.20 = (bf16[4,256,768]{2,1,0:T(8,128)(2,1)S(1)}, bf16[4,256,768]{2,1,0:T(8,128)(2,1)}, u32[]{:S(2)}) copy-start(bf16[4,256,768]{2,1,0:T(8,128)(2,1)} %get-tuple-element.99) | copy-start | bytes 4718596
  611.9 13.6 %slice-start = ((s8[7077888]{0:T(1024)(128)(4,1)}), s8[4194304]{0:T(1024)(128)(4,1)S(1)}, s32[]{:S(2)}) async-start(s8[7077888]{0:T(1024)(128)(4,1)} %bitcast.95), calls=%async_computation.3 | async-start | bytes 8388608
  611.9 13.8 %slice-start.2 = ((s8[7077888]{0:T(1024)(128)(4,1)}), s8[4194304]{0:T(1024)(128)(4,1)S(1)}, s32[]{:S(2)}) async-start(s8[7077888]{0:T(1024)(128)(4,1)} %bitcast.97), calls=%async_computation.5 | async-start | bytes 8388608
  611.9 12.2 %copy-start.2 = (f32[1,6168]{1,0:T(1,128)S(1)}, f32[1,6168]{1,0:T(1,128)}, u32[]{:S(2)}) copy-start(f32[1,6168]{1,0:T(1,128)} %small_first.1) | copy-start | bytes 74020
  612.0 12.2 %copy-start.3 = (f32[1,6168]{1,0:T(1,128)S(1)}, f32[1,6168]{1,0:T(1,128)}, u32[]{:S(2)}) copy-start(f32[1,6168]{1,0:T(1,128)} %small_second.1) | copy-start | bytes 74020
  612.0 12.2 %copy-start.5 = (f32[1,6168]{1,0:T(1,128)S(1)}, f32[1,6168]{1,0:T(1,128)}, u32[]{:S(2)}) copy-start(f32[1,6168]{1,0:T(1,128)} %get-tuple-element.108) | copy-start | bytes 74020
  612.0 12.2 %copy-start.6 = (f32[1,6168]{1,0:T(1,128)S(1)}, f32[1,6168]{1,0:T(1,128)}, u32[]{:S(2)}) copy-start(f32[1,6168]{1,0:T(1,128)} %get-tuple-element.107) | copy-start | bytes 74020
  612.0 12.9 %copy-start.4 = (f32[6168]{0:T(1024)S(1)}, f32[6168]{0:T(1024)}, u32[]{:S(2)}) copy-start(f32[6168]{0:T(1024)} %param.21) | copy-start | bytes 74020
  612.0 14.6 %slice-start.1 = ((s8[7077888]{0:T(1024)(128)(4,1)}), s8[2883584]{0:T(1024)(128)(4,1)S(1)}, s32[]{:S(2)}) async-start(s8[7077888]{0:T(1024)(128)(4,1)} %bitcast.95), calls=%async_computation.4 | async-start | bytes 5767168
  612.0 15.4 %slice-start.3 = ((s8[7077888]{0:T(1024)(128)(4,1)}), s8[2883584]{0:T(1024)(128)(4,1)S(1)}, s32[]{:S(2)}) async-start(s8[7077888]{0:T(1024)(128)(4,1)} %bitcast.97), calls=%async_computation.6 | async-start | bytes 5767168
  624.9 13.2 %copy-start.1 = (f32[6168]{0:T(1024)}, f32[6168]{0:T(1024)S(1)}, u32[]{:S(2)}) copy-start(f32[6168]{0:T(1024)S(1)} %get-tuple-element.125) | copy-start | bytes 74020
  (6 other events, 16.2 us)
Sparse Core Ops, SparseCore 0:
  12.7 160.7 all-gather.2
  292.9 157.8 reduce-scatter.1

commit v5 on v4

--- a/solution.py
+++ b/solution.py
@@ -866,15 +866,36 @@
     )(grad_zero, shard_one, weights, weight_m, weight_v, small_grad, small, small_m, small_v)
 
 
-def weight_copies(weight_hbm, weight_ref, sems, cuts):
+def weight_copies(weight_hbm, weight_ref, sems, ranges):
     return [
         pltpu.make_async_copy(
-            weight_hbm.at[pl.ds(cuts[index], cuts[index + 1] - cuts[index])],
-            weight_ref.at[pl.ds(cuts[index], cuts[index + 1] - cuts[index])],
-            sems.at[index],
-        )
-        for index in range(len(cuts) - 1)
+            weight_hbm.at[pl.ds(start, size)], weight_ref.at[pl.ds(start, size)], sems.at[index]
+        )
+        for index, (start, size) in enumerate(ranges)
     ]
+
+
+class Rolling:
+    def __init__(self, copies, active, depth=2):
+        self.copies = copies
+        self.active = active
+        self.depth = depth
+
+    def start(self):
+        for copy in self.copies[: self.depth]:
+            copy.start()
+
+    def need(self, index):
+        @pl.when(self.active)
+        def _():
+            self.copies[index].wait()
+            if index + self.depth < len(self.copies):
+                self.copies[index + self.depth].start()
+
+
+def feed_cuts(width, inner):
+    ranges = [(0, width), (width, 2 * width), (3 * width, width)]
+    return ranges + [(4 * width, inner), (4 * width + inner, inner)]
 
 
 def ahead_kernel(
@@ -935,20 +956,14 @@
     inner = (weight_ref.shape[0] - 4 * width) // 2
     queries, keys = query_out.shape[1], key_out.shape[1]
     head = width // head_count
-    cuts = [0, width, 3 * width, 4 * width, 4 * width + inner, 4 * width + 2 * inner]
-    copies = weight_copies(weight_hbm, weight_ref, sems, cuts)
+    copies = weight_copies(weight_hbm, weight_ref, sems, feed_cuts(width, inner))
+    rolling = Rolling(copies, step == 0)
     key_step = 1 if is_first else 2
 
     @pl.when(step == 0)
     def _():
-        for copy in copies:
-            copy.start()
+        rolling.start()
         fill_distance(dist_ref, key_step, 2)
-
-    def need(index):
-        @pl.when(step == 0)
-        def _():
-            copies[index].wait()
 
     fill_mask(mask_ref, key_step, lengths_ref[step])
     if is_first:
@@ -960,11 +975,11 @@
         query_low = residual.astype(BF)
         memory_low = query_low
     low_out[0] = query_low
-    need(0)
+    rolling.need(0)
     query_rows = dot_nn(query_low, weight_ref[0:width]).astype(BF)
     query_out[0] = query_rows
     query_t[...] = (query_rows.astype(F32) * float(head) ** (-0.5)).T.astype(BF)
-    need(1)
+    rolling.need(1)
     key_out[0] = dot_nn(memory_low, weight_ref[width : 2 * width]).astype(BF)
     value_rows = dot_nn(memory_low, weight_ref[2 * width : 3 * width]).astype(BF)
     value_out[0] = value_rows
@@ -981,24 +996,24 @@
             peak = jnp.max(scores, axis=0, keepdims=True)
             lifted = jnp.exp(scores - peak)
             total = jnp.sum(lifted, axis=0, keepdims=True)
-            shares = (lifted * (1.0 / total)).astype(BF)
+            shares = lifted.astype(BF)
             rows = pl.ds(start + which * head, head)
             mixed = dot_nn(value_t[rows, :], shares)
-            att_t[rows, :] = mixed
+            att_t[rows, :] = mixed * (1.0 / total)
             lse_out[0, pl.ds(index, 1), :] = peak + jnp.log(total)
         return carry
 
-    lax.fori_loop(0, head_count // 2, pair_step, 0)
+    lax.fori_loop(0, head_count // 2, pair_step, 0, unroll=True)
     attended = att_t[...].T.astype(BF)
     att_out[0] = attended
-    need(2)
+    rolling.need(2)
     total_one = residual + dot_nn(attended, weight_ref[3 * width : 4 * width])
     total_one_out[0] = total_one
     unit, _ = norm_parts(total_one)
     normed = unit * gains_ref[0:1] + gains_ref[1:2]
     normed_low = normed.astype(BF)
-    need(3)
-    need(4)
+    rolling.need(3)
+    rolling.need(4)
     total_two = normed
     for chunk in range(inner // width):
         inner_rows = pl.ds(4 * width + chunk * width, width)
@@ -1178,8 +1193,13 @@
     inner = (weight_ref.shape[0] - 4 * width) // 2
     queries, keys = query_ref.shape[1], key_ref.shape[1]
     head = width // head_count
-    cuts = [0, 3 * width, 4 * width, 4 * width + inner, 4 * width + 2 * inner]
-    copies = weight_copies(weight_hbm, weight_ref, sems, cuts)
+    ranges = [
+        (0, 3 * width),
+        (3 * width, width),
+        (4 * width, inner),
+        (4 * width + inner, inner),
+    ]
+    copies = weight_copies(weight_hbm, weight_ref, sems, ranges)
     key_step = 1 if is_first else 2
     scale = float(head) ** (-0.5)
 
@@ -1268,7 +1288,7 @@
         value_grad_out[0, :, lanes] = value_grad.astype(BF)
         return carry
 
-    lax.fori_loop(0, head_count // 2, pair_step, 0)
+    lax.fori_loop(0, head_count // 2, pair_step, 0, unroll=True)
     query_grad = (query_grad_t[...] * scale).T.astype(BF)
     query_grad_out[0] = query_grad
     need(0)
@@ -1405,6 +1425,244 @@
     )
 
 
+def last_kernel(
+    head_count,
+    lengths_ref,
+    slopes_ref,
+    x_ref,
+    grad_ref,
+    gains_ref,
+    weight_hbm,
+    layer_out,
+    low_out,
+    att_out,
+    hidden_out,
+    two_out,
+    pre_out,
+    normed_out,
+    one_out,
+    query_grad_out,
+    key_grad_out,
+    value_grad_out,
+    back_out,
+    gains_out,
+    slopes_out,
+    weight_ref,
+    dist_ref,
+    mask_ref,
+    query_rows,
+    key_rows,
+    value_rows,
+    query_t,
+    key_t,
+    value_t,
+    att_t,
+    shares_ref,
+    steep_ref,
+    mixed_rows,
+    mixed_t,
+    delta_ref,
+    query_grad_t,
+    sems,
+):
+    step = pl.program_id(0)
+    width = weight_ref.shape[1]
+    inner = (weight_ref.shape[0] - 4 * width) // 2
+    chunks = inner // width
+    length = low_out.shape[1]
+    head = width // head_count
+    scale = float(head) ** (-0.5)
+    rolling = Rolling(
+        weight_copies(weight_hbm, weight_ref, sems, feed_cuts(width, inner)), step == 0
+    )
+
+    @pl.when(step == 0)
+    def _():
+        rolling.start()
+        fill_distance(dist_ref, 2, 2)
+        gains_out[...] = jnp.zeros_like(gains_out)
+        slopes_out[...] = jnp.zeros_like(slopes_out)
+
+    fill_mask(mask_ref, 2, lengths_ref[step])
+    residual = x_ref[0]
+    low = residual.astype(BF)
+    low_out[0] = low
+    rolling.need(0)
+    queries = dot_nn(low, weight_ref[0:width]).astype(BF)
+    query_rows[...] = queries
+    query_t[...] = (queries.astype(F32) * scale).T.astype(BF)
+    rolling.need(1)
+    keys = dot_nn(low, weight_ref[width : 2 * width]).astype(BF)
+    key_rows[...] = keys
+    key_t[...] = keys.astype(F32).T.astype(BF)
+    values = dot_nn(low, weight_ref[2 * width : 3 * width]).astype(BF)
+    value_rows[...] = values
+    value_t[...] = values.astype(F32).T.astype(BF)
+
+    def ahead_pair(pair, carry):
+        start = pl.multiple_of(pair * 2 * head, 2 * head)
+        key_pair = key_rows[:, pl.ds(start, 2 * head)]
+        query_pair = query_t[pl.ds(start, 2 * head), :]
+        for which in range(2):
+            index = 2 * pair + which
+            scores = dot_nn(key_pair, pick_rows(query_pair, which))
+            scores = scores - slopes_ref[index] * dist_ref[...] + mask_ref[...]
+            peak = jnp.max(scores, axis=0, keepdims=True)
+            lifted = jnp.exp(scores - peak)
+            total = jnp.sum(lifted, axis=0, keepdims=True)
+            shares = lifted * (1.0 / total)
+            shares_ref[index] = shares
+            rows = pl.ds(start + which * head, head)
+            att_t[rows, :] = dot_nn(value_t[rows, :], shares.astype(BF))
+        return carry
+
+    lax.fori_loop(0, head_count // 2, ahead_pair, 0, unroll=True)
+    attended = att_t[...].T.astype(BF)
+    att_out[0] = attended
+    rolling.need(2)
+    total_one = residual + dot_nn(attended, weight_ref[3 * width : 4 * width])
+    unit_one, inverse_one = norm_parts(total_one)
+    normed = unit_one * gains_ref[0:1] + gains_ref[1:2]
+    normed_low = normed.astype(BF)
+    normed_out[0] = normed_low
+    rolling.need(3)
+    rolling.need(4)
+    total_two = normed
+    for chunk in range(chunks):
+        inner_rows = pl.ds(4 * width + chunk * width, width)
+        outer_rows = pl.ds(4 * width + inner + chunk * width, width)
+        pre = dot_nt(normed_low, weight_ref[inner_rows, :])
+        square = pre * pre
+        bend = jnp.tanh(pre * (GELU_COEF + (GELU_COEF * GELU_CUBE) * square))
+        half = 0.5 + 0.5 * bend
+        hidden = (pre * half).astype(BF)
+        steep = half + (0.5 * pre) * (1.0 - bend * bend) * (
+            GELU_COEF + (3.0 * GELU_COEF * GELU_CUBE) * square
+        )
+        columns = pl.ds(chunk * width, width)
+        hidden_out[0, :, columns] = hidden
+        steep_ref[:, columns] = steep.astype(BF)
+        total_two = total_two + dot_nn(hidden, weight_ref[outer_rows, :])
+    unit_two, inverse_two = norm_parts(total_two)
+    layer_out[0] = (unit_two * gains_ref[2:3] + gains_ref[3:4]).astype(layer_out.dtype)
+
+    grad = grad_ref[0].astype(F32)
+    gains_out[2:3] += jnp.sum(grad * unit_two, axis=0, keepdims=True)
+    gains_out[3:4] += jnp.sum(grad, axis=0, keepdims=True)
+    back_two = norm_back(grad, unit_two, inverse_two, gains_ref[2:3])
+    two_low = back_two.astype(BF)
+    two_out[0] = two_low
+    back_normed = back_two
+    for chunk in range(chunks):
+        inner_rows = pl.ds(4 * width + chunk * width, width)
+        outer_rows = pl.ds(4 * width + inner + chunk * width, width)
+        columns = pl.ds(chunk * width, width)
+        back_hidden = dot_nt(two_low, weight_ref[outer_rows, :])
+        pre_grad = (back_hidden * steep_ref[:, columns].astype(F32)).astype(BF)
+        pre_out[0, :, columns] = pre_grad
+        back_normed = back_normed + dot_nn(pre_grad, weight_ref[inner_rows, :])
+    gains_out[0:1] += jnp.sum(back_normed * unit_one, axis=0, keepdims=True)
+    gains_out[1:2] += jnp.sum(back_normed, axis=0, keepdims=True)
+    back_one = norm_back(back_normed, unit_one, inverse_one, gains_ref[0:1])
+    back_out[0] = back_one
+    one_low = back_one.astype(BF)
+    one_out[0] = one_low
+    mixed_low = dot_nt(one_low, weight_ref[3 * width : 4 * width]).astype(BF)
+    mixed_rows[...] = mixed_low
+    mixed_wide = mixed_low.astype(F32).T
+    mixed_t[...] = mixed_wide.astype(BF)
+    delta_ref[...] = jnp.sum((mixed_wide * att_t[...]).reshape(head_count, head, length), axis=1)
+
+    def back_pair(pair, carry):
+        start = pl.multiple_of(pair * 2 * head, 2 * head)
+        lanes = pl.ds(start, 2 * head)
+        value_pair = value_rows[:, lanes]
+        query_pair = query_rows[:, lanes]
+        mixed_pair = mixed_rows[:, lanes]
+        mixed_pair_t = mixed_t[lanes, :]
+        key_grad = jnp.zeros((length, 2 * head), F32)
+        value_grad = jnp.zeros((length, 2 * head), F32)
+        for which in range(2):
+            index = 2 * pair + which
+            half = lane_half(2 * head, which)
+            shares = shares_ref[index]
+            back_shares = dot_nn(value_pair, pick_rows(mixed_pair_t, which))
+            back_scores = shares * (back_shares - delta_ref[pl.ds(index, 1), :])
+            slopes_out[pl.ds(index, 1), :] += jnp.sum(
+                back_scores * dist_ref[...], axis=0, keepdims=True
+            )
+            scores_low = back_scores.astype(BF)
+            value_grad = value_grad + dot_nn(shares.astype(BF), mixed_pair * half)
+            key_grad = key_grad + dot_nn(scores_low, query_pair * half)
+            rows = pl.ds(start + which * head, head)
+            query_grad_t[rows, :] = dot_nn(key_t[rows, :], scores_low)
+        key_grad_out[0, :, lanes] = (key_grad * scale).astype(BF)
+        value_grad_out[0, :, lanes] = value_grad.astype(BF)
+        return carry
+
+    lax.fori_loop(0, head_count // 2, back_pair, 0, unroll=True)
+    query_grad_out[0] = (query_grad_t[...] * scale).T.astype(BF)
+
+
+def layer_last(x, grad, lengths, slopes, gains, weight_full):
+    batch, length, width = x.shape
+    head_count = slopes.shape[0]
+    rows = weight_full.shape[0]
+    inner = (rows - 4 * width) // 2
+    head_rows = -(-head_count // 8) * 8
+
+    def block(size):
+        return pl.BlockSpec((1, length, size), lambda i, *_: (i, 0, 0))
+
+    def shape(size, dtype):
+        return jax.ShapeDtypeStruct((batch, length, size), dtype)
+
+    outs = [(width, BF)] * 3 + [(inner, BF), (width, BF), (inner, BF)] + [(width, BF)] * 5
+    outs = outs + [(width, F32)]
+    fixed = [
+        pl.BlockSpec((4, width), lambda i, *_: (0, 0)),
+        pl.BlockSpec((head_rows, length), lambda i, *_: (0, 0)),
+    ]
+    return pl.pallas_call(
+        functools.partial(last_kernel, head_count),
+        grid_spec=pltpu.PrefetchScalarGridSpec(
+            num_scalar_prefetch=2,
+            grid=(batch,),
+            in_specs=[block(width), block(width), fixed[0], pl.BlockSpec(memory_space=pl.ANY)],
+            out_specs=[block(size) for size, _ in outs] + fixed,
+            scratch_shapes=[
+                pltpu.VMEM((rows, width), BF),
+                pltpu.VMEM((length, length), F32),
+                pltpu.VMEM((length, length), F32),
+                pltpu.VMEM((length, width), BF),
+                pltpu.VMEM((length, width), BF),
+                pltpu.VMEM((length, width), BF),
+                pltpu.VMEM((width, length), BF),
+                pltpu.VMEM((width, length), BF),
+                pltpu.VMEM((width, length), BF),
+                pltpu.VMEM((width, length), F32),
+                pltpu.VMEM((head_count, length, length), F32),
+                pltpu.VMEM((length, inner), BF),
+                pltpu.VMEM((length, width), BF),
+                pltpu.VMEM((width, length), BF),
+                pltpu.VMEM((head_count, length), F32),
+                pltpu.VMEM((width, length), F32),
+                pltpu.SemaphoreType.DMA((5,)),
+            ],
+        ),
+        out_shape=[shape(size, dtype) for size, dtype in outs]
+        + [
+            jax.ShapeDtypeStruct((4, width), F32),
+            jax.ShapeDtypeStruct((head_rows, length), F32),
+        ],
+        compiler_params=pltpu.CompilerParams(vmem_limit_bytes=VMEM_LIMIT),
+        cost_estimate=pl.CostEstimate(
+            flops=60000000000, bytes_accessed=80000000, transcendentals=0
+        ),
+        name="layer_last",
+    )(lengths, slopes, x, grad, gains, weight_full)
+
+
 def weight_product(left, right):
     return lax.dot_general(
         left, right, (((0, 1), (0, 1)), ((), ())), preferred_element_type=F32
@@ -1470,20 +1728,21 @@
     (q1, k1, v1, lse1, att1, one1, hid1, steep1, two1, first_out, low1) = layer_ahead(
         True, hidden_in, lengths, slopes[0], gains[0], matrix_one, F32
     )
-    (q2, k2, v2, lse2, att2, one2, hid2, steep2, two2, block_out, low2) = layer_ahead(
-        False, first_out, lengths, slopes[1], gains[1], matrix_two, BF
-    )
-    back_two = layer_back(
-        False,
-        out_grad,
-        (q2, k2, v2, lse2, att2, one2, steep2, two2),
-        lengths,
-        slopes[1],
-        gains[1],
-        matrix_two,
+    (block_out, low2, att2, hid2, *back_two) = layer_last(
+        first_out, out_grad, lengths, slopes[1], gains[1], matrix_two
     )
     matrix_grad_two = matrix_gradient(low2, low2, att2, hid2, back_two[:7]).astype(BF)
-    first_grad, matrix_grad_two = lax.optimization_barrier((back_two[7], matrix_grad_two))
+    rest_two, matrix_grad_two = lax.optimization_barrier(
+        ((back_two[4], back_two[5], back_two[6], back_two[7]), matrix_grad_two)
+    )
+    first_grad = rest_two[3]
+    for index in range(3):
+        first_grad = first_grad + jnp.einsum(
+            "btn,an->bta",
+            rest_two[index],
+            matrix_two[index * width : (index + 1) * width],
+            preferred_element_type=F32,
+        )
     shard_two = lax.psum_scatter(matrix_grad_two, "fsdp", scatter_dimension=0, tiled=True)
     back_one = layer_back(
         True,

time: 654 us -> 629 us (0.962)
  Pallas kernels: 468 us -> 441 us
  matrix products: 53.5 us -> 64.6 us
  waiting for transfers between devices: 72.5 us -> 61.5 us
    pallas_call x0 -> x1, Pallas kernels: none -> 71.7 us  [layer_last(): pl.pallas_call(functools.partial(last_kernel, head_count), grid_spec=pltp...]
    pallas_call x2 -> x1, Pallas kernels: 107 us -> 53.6 us  [layer_ahead(): pl.pallas_call(functools.partial(ahead_kernel, is_first, head_count, plac...]
    pallas_call x2 -> x1, Pallas kernels: 106 us -> 60.1 us  [layer_back(): pl.pallas_call(functools.partial(back_kernel, is_first, head_count, place...]
    reduce_scatter x1, waiting for transfers between devices: 67.1 us -> 50.7 us  [shards(): lax.psum_scatter(matrix_grad_two, 'fsdp', scatter_dimension=0, tiled=True)]
    dot_general x0 -> x3, matrix products: none -> 10.5 us  [shards(): jnp.einsum('btn,an->bta', rest_two[index], matrix_two[index * width:(inde...]
  transfers between devices with their start and end apart: 2 -> 2, of which waited for: 2 -> 2; matrix products, arithmetic and copies ran while one was open for 5% -> 7% of each run, Pallas kernels for 33% -> 34%
where the time goes in v5:
time: 629 us; the launch traced here: 619 us
  Pallas kernels  441 us (70%)
  matrix products  64.6 us (10%)
  waiting for transfers between devices  61.5 us (10%)
  other arithmetic  28.5 us (5%)
  between operations  14.8 us (2%)
  local copies, waits for them, and re-layouts  7.95 us (1%)
    pallas_call x1, Pallas kernels, finish(): pl.pallas_call(functools.partial(finish_kernel, chips, group_count), grid...  161 us
    pallas_call x1, Pallas kernels, gather_rows(): pl.pallas_call(functools.partial(gather_kernel, members // 2, group_count...  94.5 us
    pallas_call x1, Pallas kernels, layer_last(): pl.pallas_call(functools.partial(last_kernel, head_count), grid_spec=pltp...  71.7 us
    pallas_call x1, Pallas kernels, layer_back(): pl.pallas_call(functools.partial(back_kernel, is_first, head_count, place...  60.1 us
    dot_general x12, matrix products, weight_product(): lax.dot_general(left, right, (((0, 1), (0, 1)), ((), ())), preferred_elem...  54.2 us
    pallas_call x1, Pallas kernels, layer_ahead(): pl.pallas_call(functools.partial(ahead_kernel, is_first, head_count, plac...  53.6 us
    reduce_scatter x1, waiting for transfers between devices, shards(): lax.psum_scatter(matrix_grad_two, 'fsdp', scatter_dimension=0, tiled=True)  50.7 us
    add x2, other arithmetic, adam_step(): second_new = BETA_TWO * second_mom + (1.0 - BETA_TWO) * gradient * gradient  12.9 us
  transfers between devices with their start and end apart: 2, of which 2 were waited for; matrix products, arithmetic and copies ran while one was open for 7% of the time, Pallas kernels for 34%

profile of v5, /device:TPU:0, one launch (start us, length us, event | category | flops | bytes accessed | tf_op | source)
XLA Modules:
  0.0 618.6 jit_solution(4646887512574528754)
XLA Ops:
  7.2 3.4 convert.42
  10.6 2.0 fusion.22
  12.7 94.5 %gather_rows.1.weight_hbm = bf16[9216,768]{1,0:T(8,128)(2,1)} custom-call(bf16[1152,768]{1,0:T(8,128)(2,1)} %get-tuple-element.110.shard_ref), custom_call_target="tpu_custom_call" | custom-call | tf_op jit(solution)/shard_map/gather_rows/pallas_call | solution.py:270
  109.1 53.6 %layer_ahead.1 = (bf16[4,256,768]{2,1,0:T(8,128)(2,1)}, bf16[4,512,768]{2,1,0:T(8,128)(2,1)}, bf16[4,512,768]{2,1,0:T(8,128)(2,1)}, f32[4,16,256]{2,1,0:T(8,128)...) custom-call(s32[4]{0:T(128)} %lengths_ref.5, ...), custom_call_target="tpu_custom_call" | custom-call | flops 18522046464 | bytes 44155776 | tf_op jit(solution)/shard_map/layer_ahead/pallas_call | solution.py:1077
  162.8 10.8 %all-gather.3.cloned.1.call-done = bf16[1,9216,768]{2,1,0:T(8,128)(2,1)} async-done(((bf16[1,1152,768]{2,1,0:T(8,128)(2,1)}), bf16[1,9216,768]{2,1,0:T(8,128)(2,1)}) %all-gather.3.cloned.1.call-update) | async-done | bytes 14155792 | tf_op jit(solution)/shard_map/all_gather | solution.py:1726
  173.5 71.7 %layer_last.1 = (bf16[4,256,768]{2,1,0:T(8,128)(2,1)}, bf16[4,256,768]{2,1,0:T(8,128)(2,1)}, bf16[4,256,768]{2,1,0:T(8,128)(2,1)}, bf16[4,256,3072]{2,1,0:T(8,12...) custom-call(s32[4]{0:T(128)} %lengths_ref.5, ...), custom_call_target="tpu_custom_call" | custom-call | flops 60000002048 | bytes 80000000 | tf_op jit(solution)/shard_map/layer_last/pallas_call | solution.py:1626
  245.2 4.6 fusion.8
  249.8 2.5 fusion.9
  252.3 2.5 fusion.10
  254.8 2.5 fusion.11
  257.4 7.0 %fusion.4 = bf16[9216,768]{1,0:T(8,128)(2,1)} fusion(bf16[9216,768]{1,0:T(8,128)(2,1)} %fusion.11, bf16[4,256,3072]{2,1,0:T(8,128)(2,1)S(1)} %bitcast.122, bf16[4,256,768]{2,1,0:T(8,128)(2,1)S(1)} %copy-done.25), kind=kOutput, calls=%fused_computation.13 | convolution fusion | flops 4834197504 | bytes 12582912 | tf_op jit(solution)/shard_map/dot_general | solution.py:1667
  264.3 7.1 %fusion.5 = bf16[9216,768]{1,0:T(8,128)(2,1)} fusion(bf16[9216,768]{1,0:T(8,128)(2,1)} %fusion.4, bf16[4,256,3072]{2,1,0:T(8,128)(2,1)S(1)} %bitcast.120, bf16[4,256,768]{2,1,0:T(8,128)(2,1)S(1)} %copy-done.24), kind=kOutput, calls=%fused_computation.14 | convolution fusion | flops 4834197504 | bytes 12582912 | tf_op jit(solution)/shard_map/dot_general | solution.py:1667
  272.1 3.3 fusion.19
  275.4 2.8 fusion.18
  278.2 4.3 add_add_fusion.grad_ref
  282.6 60.1 %layer_back.1 = (bf16[4,256,768]{2,1,0:T(8,128)(2,1)}, bf16[4,256,3072]{2,1,0:T(8,128)(2,1)}, bf16[4,256,768]{2,1,0:T(8,128)(2,1)}, bf16[4,256,768]{2,1,0:T(8,12...) custom-call(s32[4]{0:T(128)} %lengths_ref.5, ...), custom_call_target="tpu_custom_call" | custom-call | flops 20937965568 | bytes 54155776 | tf_op jit(solution)/shard_map/layer_back/pallas_call | solution.py:1360
  342.7 0.7 reshape.48
  343.4 0.8 slice_reduce_fusion.1
  344.5 0.6 broadcast_in_dim.7.small_grad
  345.1 4.1 fusion.12
  349.2 3.7 fusion.15
  352.9 3.7 fusion.17
  356.7 2.5 fusion.13
  359.2 7.0 %fusion.6 = bf16[9216,768]{1,0:T(8,128)(2,1)} fusion(bf16[9216,768]{1,0:T(8,128)(2,1)} %fusion.13, bf16[4,256,3072]{2,1,0:T(8,128)(2,1)S(1)} %bitcast.118, bf16[4,256,768]{2,1,0:T(8,128)(2,1)S(1)} %copy-done.23), kind=kOutput, calls=%fused_computation.15 | convolution fusion | flops 4834197504 | bytes 12582912 | tf_op jit(solution)/shard_map/dot_general | solution.py:1667
  366.2 7.2 %fusion.7.grad_zero = bf16[9216,768]{1,0:T(8,128)(2,1)} fusion(bf16[9216,768]{1,0:T(8,128)(2,1)} %fusion.6, bf16[4,256,3072]{2,1,0:T(8,128)(2,1)S(1)} %bitcast.116, bf16[4,256,768]{2,1,0:T(8,128)(2,1)S(1)} %copy-done.22), kind=kOutput, calls=%fused_computation.16 | convolution fusion | flops 4834197504 | bytes 12582912 | tf_op jit(solution)/shard_map/dot_general | solution.py:1667
  373.3 50.7 %reduce-scatter.2.cloned.1.call-done.shard_one = bf16[1152,768]{1,0:T(8,128)(2,1)} async-done(((bf16[9216,768]{1,0:T(8,128)(2,1)}), bf16[1152,768]{1,0:T(8,128)(2,1)}) %reduce-scatter.2.cloned.1.call-update) | async-done | bytes 1769488 | tf_op jit(solution)/shard_map/reduce_scatter | solution.py:1746
  424.0 161.1 %finish.1 = (bf16[2,1152,768]{2,1,0:T(8,128)(2,1)}, bf16[2,1152,768]{2,1,0:T(8,128)(2,1)}, f32[1,6168]{1,0:T(1,128)}, f32[1,6168]{1,0:T(1,128)}, bf16[4608,768]{1,0:T(8,128)(2,1)}, /*index=5*/bf16[6912,768]{1,0:T(8,128)(2,1)}) custom-call(bf16[9216,768]{1,0:T(8,128)(2,1)} %fusion.7.grad_zero, bf16[1152,768]{1,0:T(8,128)(2,1)} %reduce-scatter.2.cloned.1.call-done.shard_one, ...), custom_call_target="tpu_custom_call" | custom-call | tf_op jit(solution)/shard_map/finish/pallas_call | solution.py:826
  585.3 12.2 %fusion.3 = (f32[1,2,1152,768]{3,2,1,0:T(8,128)}, f32[1,2,1152,768]{3,2,1,0:T(8,128)}) fusion(bf16[2,1152,768]{2,1,0:T(8,128)(2,1)} %get-tuple-element.98, f32[1,2,1152,768]{3,2,1,0:T(8,128)} %second_hbm.1, f32[1,2,1152,768]{3,2,1,0:T(8,128)} %first_hbm.1), kind=kLoop, calls=%fused_computation.9 | loop fusion | flops 14155776 | bytes 31850496 | tf_op jit(solution)/shard_map/add | solution.py:1689
  597.4 0.7 fusion.20
  599.0 0.8 slice-done.1
  599.8 0.8 slice-done.3
  600.6 10.7 %fusion.21 = (bf16[2,1152,768]{2,1,0:T(8,128)(2,1)}, f32[2,1152,768]{2,1,0:T(8,128)}, f32[2,1152,768]{2,1,0:T(8,128)}, f32[2,1152,768]{2,1,0:T(8,128)}) fusion(f32[2,1152,768]{2,1,0:T(8,128)S(1)} %bitcast.111, f32[2,1152,768]{2,1,0:T(8,128)S(1)} %bitcast.113, bf16[2,1152,768]{2,1,0:T(8,128)(2,1)} %get-tuple-element.97), kind=kLoop, calls=%fused_computation.50 | loop fusion | flops 15925248 | bytes 42467328 | tf_op jit(solution)/shard_map/convert_element_type | solution.py:1785
  (95 shorter events, 3.8 us)
Async XLA Ops:
  7.2 166.4 %all-gather.3.cloned.1.call-start = ((), (), s32[]{:S(2)}) async-start(), calls=%async_computation.2 | async-start | bytes 15925248 | tf_op jit(solution)/shard_map/all_gather | solution.py:1726
  12.6 411.4 %reduce-scatter.2.cloned.1.call-start = ((), (), s32[]{:S(2)}) async-start(), calls=%async_computation.1 | async-start | bytes 15925248 | tf_op jit(solution)/shard_map/reduce_scatter | solution.py:1746
  12.7 94.6 %copy-start.2 = (f32[6168]{0:T(1024)S(1)}, f32[6168]{0:T(1024)}, u32[]{:S(2)}) copy-start(f32[6168]{0:T(1024)} %param.18) | copy-start | bytes 74020
  245.2 4.6 copy-start.12
  245.2 4.6 copy-start.18
  249.8 7.5 %slice-start.10 = ((s8[6291456]{0:T(1024)(128)(4,1)}), s8[4194304]{0:T(1024)(128)(4,1)S(1)}, s32[]{:S(2)}) async-start(s8[6291456]{0:T(1024)(128)(4,1)} %bitcast.121), calls=%async_computation.13 | async-start | bytes 8388608
  252.3 5.0 slice-start.11
  254.8 9.5 %slice-start.8 = ((s8[6291456]{0:T(1024)(128)(4,1)}), s8[4194304]{0:T(1024)(128)(4,1)S(1)}, s32[]{:S(2)}) async-start(s8[6291456]{0:T(1024)(128)(4,1)} %bitcast.119), calls=%async_computation.11 | async-start | bytes 8388608
  257.3 7.0 %slice-start.9 = ((s8[6291456]{0:T(1024)(128)(4,1)}), s8[2097152]{0:T(1024)(128)(4,1)S(1)}, s32[]{:S(2)}) async-start(s8[6291456]{0:T(1024)(128)(4,1)} %bitcast.119), calls=%async_computation.12 | async-start | bytes 4194304
  257.3 7.0 %copy-start.24 = (bf16[4,256,768]{2,1,0:T(8,128)(2,1)S(1)}, bf16[4,256,768]{2,1,0:T(8,128)(2,1)}, u32[]{:S(2)}) copy-start(bf16[4,256,768]{2,1,0:T(8,128)(2,1)} %get-tuple-element.69) | copy-start | bytes 4718596
  282.5 61.7 %copy-start.10 = (f32[4,768]{1,0:T(4,128)S(1)}, f32[4,768]{1,0:T(4,128)}, u32[]{:S(2)}) copy-start(f32[4,768]{1,0:T(4,128)} %get-tuple-element.95) | copy-start | bytes 36868
  282.6 61.7 %copy-start.9 = (f32[16,256]{1,0:T(8,128)S(1)}, f32[16,256]{1,0:T(8,128)}, u32[]{:S(2)}) copy-start(f32[16,256]{1,0:T(8,128)} %get-tuple-element.96) | copy-start | bytes 49156
  282.6 62.6 %copy-start.19 = (bf16[4,256,768]{2,1,0:T(8,128)(2,1)S(1)}, bf16[4,256,768]{2,1,0:T(8,128)(2,1)}, u32[]{:S(2)}) copy-start(bf16[4,256,768]{2,1,0:T(8,128)(2,1)} %get-tuple-element.83) | copy-start | bytes 4718596
  345.1 4.1 copy-start.11
  345.1 4.1 copy-start.21
  349.2 9.9 %slice-start.6 = ((s8[6291456]{0:T(1024)(128)(4,1)}), s8[4194304]{0:T(1024)(128)(4,1)S(1)}, s32[]{:S(2)}) async-start(s8[6291456]{0:T(1024)(128)(4,1)} %bitcast.117), calls=%async_computation.9 | async-start | bytes 8388608
  352.9 3.7 copy-start.14
  352.9 3.7 copy-start.15
  352.9 6.2 %slice-start.7 = ((s8[6291456]{0:T(1024)(128)(4,1)}), s8[2097152]{0:T(1024)(128)(4,1)S(1)}, s32[]{:S(2)}) async-start(s8[6291456]{0:T(1024)(128)(4,1)} %bitcast.117), calls=%async_computation.10 | async-start | bytes 4194304
  356.7 9.5 %slice-start.4 = ((s8[6291456]{0:T(1024)(128)(4,1)}), s8[2097152]{0:T(1024)(128)(4,1)S(1)}, s32[]{:S(2)}) async-start(s8[6291456]{0:T(1024)(128)(4,1)} %bitcast.115), calls=%async_computation.7 | async-start | bytes 4194304
  359.1 7.0 %slice-start.5 = ((s8[6291456]{0:T(1024)(128)(4,1)}), s8[4194304]{0:T(1024)(128)(4,1)S(1)}, s32[]{:S(2)}) async-start(s8[6291456]{0:T(1024)(128)(4,1)} %bitcast.115), calls=%async_computation.8 | async-start | bytes 8388608
  359.2 7.0 %copy-start.22 = (bf16[4,256,768]{2,1,0:T(8,128)(2,1)S(1)}, bf16[4,256,768]{2,1,0:T(8,128)(2,1)}, u32[]{:S(2)}) copy-start(bf16[4,256,768]{2,1,0:T(8,128)(2,1)} %get-tuple-element.91) | copy-start | bytes 4718596
  585.2 13.6 %slice-start = ((s8[7077888]{0:T(1024)(128)(4,1)}), s8[4194304]{0:T(1024)(128)(4,1)S(1)}, s32[]{:S(2)}) async-start(s8[7077888]{0:T(1024)(128)(4,1)} %bitcast.110), calls=%async_computation.3 | async-start | bytes 8388608
  585.2 13.8 %slice-start.2 = ((s8[7077888]{0:T(1024)(128)(4,1)}), s8[4194304]{0:T(1024)(128)(4,1)S(1)}, s32[]{:S(2)}) async-start(s8[7077888]{0:T(1024)(128)(4,1)} %bitcast.112), calls=%async_computation.5 | async-start | bytes 8388608
  585.2 12.2 %copy-start.4 = (f32[1,6168]{1,0:T(1,128)S(1)}, f32[1,6168]{1,0:T(1,128)}, u32[]{:S(2)}) copy-start(f32[1,6168]{1,0:T(1,128)} %small_first.1) | copy-start | bytes 74020
  585.2 12.2 %copy-start.5 = (f32[1,6168]{1,0:T(1,128)S(1)}, f32[1,6168]{1,0:T(1,128)}, u32[]{:S(2)}) copy-start(f32[1,6168]{1,0:T(1,128)} %small_second.1) | copy-start | bytes 74020
  585.2 12.2 %copy-start.7 = (f32[1,6168]{1,0:T(1,128)S(1)}, f32[1,6168]{1,0:T(1,128)}, u32[]{:S(2)}) copy-start(f32[1,6168]{1,0:T(1,128)} %get-tuple-element.100) | copy-start | bytes 74020
  585.2 12.2 %copy-start.8 = (f32[1,6168]{1,0:T(1,128)S(1)}, f32[1,6168]{1,0:T(1,128)}, u32[]{:S(2)}) copy-start(f32[1,6168]{1,0:T(1,128)} %get-tuple-element.99) | copy-start | bytes 74020
  585.2 12.9 %copy-start.6 = (f32[6168]{0:T(1024)S(1)}, f32[6168]{0:T(1024)}, u32[]{:S(2)}) copy-start(f32[6168]{0:T(1024)} %param.21) | copy-start | bytes 74020
  585.2 14.6 %slice-start.1 = ((s8[7077888]{0:T(1024)(128)(4,1)}), s8[2883584]{0:T(1024)(128)(4,1)S(1)}, s32[]{:S(2)}) async-start(s8[7077888]{0:T(1024)(128)(4,1)} %bitcast.110), calls=%async_computation.4 | async-start | bytes 5767168
  585.3 15.4 %slice-start.3 = ((s8[7077888]{0:T(1024)(128)(4,1)}), s8[2883584]{0:T(1024)(128)(4,1)S(1)}, s32[]{:S(2)}) async-start(s8[7077888]{0:T(1024)(128)(4,1)} %bitcast.112), calls=%async_computation.6 | async-start | bytes 5767168
  598.2 13.2 %copy-start.3 = (f32[6168]{0:T(1024)}, f32[6168]{0:T(1024)S(1)}, u32[]{:S(2)}) copy-start(f32[6168]{0:T(1024)S(1)} %get-tuple-element.117) | copy-start | bytes 74020
  (8 other events, 22.4 us)
Sparse Core Ops, SparseCore 0:
  12.7 160.7 all-gather.2
  271.5 152.4 reduce-scatter.1

commit v6 on v5

--- a/solution.py
+++ b/solution.py
@@ -148,7 +148,7 @@
         self.core_send, self.core_recv, self.own_sem = sems[4:]
         self.rows = shard_ref.shape[0]
         self.part = self.rows // spot.group_count
-        self.tick_count = 2 * spot.chips
+        self.last = spot.chips - 1
 
     def piece(self, chip, core, group):
         start = (2 * chip + core) * self.rows + group * self.part
@@ -157,60 +157,65 @@
     def whole(self, chip, core):
         return self.full.at[pl.ds((2 * chip + core) * self.rows, self.rows)]
 
-    def line_copy(self, hop):
+    def line_own(self, side):
         spot = self.spot
         return remote(
             self.shard.at[pl.ds(spot.group * self.part, self.part)],
             self.piece(spot.chip, spot.core, spot.group),
-            self.line_send.at[hop],
-            self.line_recv.at[hop],
-            spot.line(spot.ahead_chip(hop)),
-        )
-
-    def line_arrival(self, hop):
-        spot = self.spot
-        here = self.piece(spot.back_chip(hop), spot.core, spot.group)
+            self.line_send.at[spot.chips + side],
+            self.line_recv.at[spot.chip],
+            spot.line(spot.chip + 1 - 2 * side),
+        )
+
+    def line_pass(self, source, chip):
+        here = self.piece(source, self.spot.core, self.spot.group)
         return remote(
-            here, here, self.line_send.at[hop], self.line_recv.at[hop], spot.partner()
-        )
-
-    def cross_copy(self, hop, turn):
-        spot = self.spot
-        here = self.piece(spot.back_chip(hop), spot.core, spot.group)
-        slot = hop * spot.group_count + turn
+            here, here, self.line_send.at[source], self.line_recv.at[source], self.spot.line(chip)
+        )
+
+    def cross_copy(self, source, turn):
+        here = self.piece(source, self.spot.core, self.spot.group)
+        slot = source * self.spot.group_count + turn
         return remote(
-            here, here, self.cross_send.at[slot], self.cross_recv.at[slot], spot.other(turn)
-        )
-
-    def cross_arrival(self, hop, turn):
-        spot = self.spot
-        here = self.piece(spot.back_chip(hop), spot.core, spot.back_group(turn))
-        slot = hop * spot.group_count + turn
+            here, here, self.cross_send.at[slot], self.cross_recv.at[slot], self.spot.other(turn)
+        )
+
+    def cross_arrival(self, source, turn):
+        here = self.piece(source, self.spot.core, self.spot.back_group(turn))
+        slot = source * self.spot.group_count + turn
         return remote(
-            here, here, self.cross_send.at[slot], self.cross_recv.at[slot], spot.partner()
-        )
-
-    def core_copy(self, hop, turn):
-        spot = self.spot
-        slot = hop * spot.group_count + turn
-        if hop == 0:
-            source, target = self.shard, self.whole(spot.chip, spot.core)
-        else:
-            source = self.piece(spot.back_chip(hop), spot.core, spot.back_group(turn))
-            target = source
+            here, here, self.cross_send.at[slot], self.cross_recv.at[slot], self.spot.partner()
+        )
+
+    def core_copy(self, source, turn):
+        here = self.piece(source, self.spot.core, self.spot.back_group(turn))
+        slot = source * self.spot.group_count + turn
         return remote(
-            source, target, self.core_send.at[slot], self.core_recv.at[slot], spot.partner()
-        )
-
-    def core_arrival(self, hop, turn):
-        spot = self.spot
-        slot = hop * spot.group_count + turn
-        if hop == 0:
-            here = self.whole(spot.chip, 1 - spot.core)
-        else:
-            here = self.piece(spot.back_chip(hop), 1 - spot.core, spot.back_group(turn))
+            here, here, self.core_send.at[slot], self.core_recv.at[slot], self.spot.partner()
+        )
+
+    def core_arrival(self, source, turn):
+        here = self.piece(source, 1 - self.spot.core, self.spot.back_group(turn))
+        slot = source * self.spot.group_count + turn
         return remote(
-            here, here, self.core_send.at[slot], self.core_recv.at[slot], spot.partner()
+            here, here, self.core_send.at[slot], self.core_recv.at[slot], self.spot.partner()
+        )
+
+    def core_own(self):
+        slot = self.spot.chip * self.spot.group_count
+        return remote(
+            self.shard,
+            self.whole(self.spot.chip, self.spot.core),
+            self.core_send.at[slot],
+            self.core_recv.at[slot],
+            self.spot.partner(),
+        )
+
+    def core_own_arrival(self):
+        slot = self.spot.chip * self.spot.group_count
+        here = self.whole(self.spot.chip, 1 - self.spot.core)
+        return remote(
+            here, here, self.core_send.at[slot], self.core_recv.at[slot], self.spot.partner()
         )
 
     def own_copy(self):
@@ -218,50 +223,90 @@
             self.shard, self.whole(self.spot.chip, self.spot.core), self.own_sem.at[0]
         )
 
-    def tick(self, index):
-        chips, groups = self.spot.chips, self.spot.group_count
-        if index == 0:
-            for hop in range(1, chips):
-                self.line_copy(hop).start()
-            self.core_copy(0, 0).start()
-            self.own_copy().start()
-        elif index < chips:
-            hop = index
-            self.line_arrival(hop).wait_recv()
-            for turn in range(1, groups):
-                self.cross_copy(hop, turn).start()
-            self.core_copy(hop, 0).start()
-        elif index < 2 * chips - 1:
-            hop = index - chips + 1
-            for turn in range(1, groups):
-                self.cross_arrival(hop, turn).wait_recv()
-                self.core_copy(hop, turn).start()
-        else:
-            self.own_copy().wait()
-            self.core_copy(0, 0).wait_send()
-            self.core_arrival(0, 0).wait_recv()
-            for hop in range(1, chips):
-                self.line_copy(hop).wait_send()
-                self.core_copy(hop, 0).wait_send()
-                self.core_arrival(hop, 0).wait_recv()
-                for turn in range(1, groups):
-                    self.cross_copy(hop, turn).wait_send()
-                    self.core_copy(hop, turn).wait_send()
-                    self.core_arrival(hop, turn).wait_recv()
+    def each_side(self, distance, act):
+        spot = self.spot
+        for side in range(2):
+            source = spot.chip - distance if side == 0 else spot.chip + distance
+            target = spot.chip + 1 - 2 * side
+
+            @pl.when((source >= 0) & (source <= self.last))
+            def _():
+                act(source, target, (target >= 0) & (target <= self.last))
+
+    def start(self):
+        spot = self.spot
+
+        @pl.when(spot.chip < self.last)
+        def _():
+            self.line_own(0).start()
+
+        @pl.when(spot.chip > 0)
+        def _():
+            self.line_own(1).start()
+
+        self.core_own().start()
+        self.own_copy().start()
+
+    def line_stage(self, source, target, inside):
+        self.line_pass(source, self.spot.chip).wait_recv()
+
+        @pl.when(inside)
+        def _():
+            self.line_pass(source, target).start()
+
+        for turn in range(1, self.spot.group_count):
+            self.cross_copy(source, turn).start()
+        self.core_copy(source, 0).start()
+
+    def cross_stage(self, source, target, inside):
+        for turn in range(1, self.spot.group_count):
+            self.cross_arrival(source, turn).wait_recv()
+            self.core_copy(source, turn).start()
+
+    def end_stage(self, source, target, inside):
+        @pl.when(inside)
+        def _():
+            self.line_pass(source, target).wait_send()
+
+        for turn in range(self.spot.group_count):
+            if turn > 0:
+                self.cross_copy(source, turn).wait_send()
+            self.core_copy(source, turn).wait_send()
+            self.core_arrival(source, turn).wait_recv()
+
+    def run(self):
+        spot = self.spot
+        self.start()
+        for distance in range(1, spot.chips):
+            self.each_side(distance, self.line_stage)
+            if distance > 1:
+                self.each_side(distance - 1, self.cross_stage)
+        self.each_side(spot.chips - 1, self.cross_stage)
+        for distance in range(1, spot.chips):
+            self.each_side(distance, self.end_stage)
+        self.own_copy().wait()
+        self.core_own().wait_send()
+        self.core_own_arrival().wait_recv()
+
+        @pl.when(spot.chip < self.last)
+        def _():
+            self.line_own(0).wait_send()
+
+        @pl.when(spot.chip > 0)
+        def _():
+            self.line_own(1).wait_send()
 
 
 def gather_sems(chips, group_count):
     dma = pltpu.SemaphoreType.DMA
     crossing = (chips * group_count,)
-    return [dma((chips,)), dma((chips,))] + [dma(crossing)] * 4 + [dma((1,))]
+    return [dma((chips + 2,)), dma((chips,))] + [dma(crossing)] * 4 + [dma((1,))]
 
 
 def gather_kernel(chips, group_count, shard_ref, full_ref, *sems):
     spot = Spot(chips, group_count)
-    job = Gather(spot, shard_ref, full_ref, sems)
     meet(spot)
-    for index in range(job.tick_count):
-        job.tick(index)
+    Gather(spot, shard_ref, full_ref, sems).run()
 
 
 def gather_rows(shard):

time: 629 us -> 627 us (level)
  waiting for transfers between devices: 61.5 us -> 42.7 us
  Pallas kernels: 441 us -> 457 us
    pallas_call x1, Pallas kernels: 94.5 us -> 112 us  [gather_rows(): pl.pallas_call(functools.partial(gather_kernel, members // 2, group_count...]
    all_gather x1, waiting for transfers between devices: 10.8 us -> 0.02 us  [shards(): matrix_two = lax.all_gather(masters_low[1], 'fsdp', axis=0, tiled=True)]
    reduce_scatter x1, waiting for transfers between devices: 50.7 us -> 42.6 us  [shards(): lax.psum_scatter(matrix_grad_two, 'fsdp', scatter_dimension=0, tiled=True)]
  transfers between devices with their start and end apart: 2 -> 2, of which waited for: 2 -> 1; matrix products, arithmetic and copies ran while one was open for 7% -> 7% of each run, Pallas kernels for 34% -> 36%
where the time goes in v6:
time: 627 us; the launch traced here: 616 us
  Pallas kernels  457 us (73%)
  matrix products  64.9 us (10%)
  waiting for transfers between devices  42.7 us (7%)
  other arithmetic  28.5 us (5%)
  between operations  14.6 us (2%)
  local copies, waits for them, and re-layouts  8.09 us (1%)
    pallas_call x1, Pallas kernels, finish(): pl.pallas_call(functools.partial(finish_kernel, chips, group_count), grid...  161 us
    pallas_call x1, Pallas kernels, gather_rows(): pl.pallas_call(functools.partial(gather_kernel, members // 2, group_count...  112 us
    pallas_call x1, Pallas kernels, layer_last(): pl.pallas_call(functools.partial(last_kernel, head_count), grid_spec=pltp...  71.5 us
    pallas_call x1, Pallas kernels, layer_back(): pl.pallas_call(functools.partial(back_kernel, is_first, head_count, place...  59 us
    dot_general x12, matrix products, weight_product(): lax.dot_general(left, right, (((0, 1), (0, 1)), ((), ())), preferred_elem...  54.4 us
    pallas_call x1, Pallas kernels, layer_ahead(): pl.pallas_call(functools.partial(ahead_kernel, is_first, head_count, plac...  53.6 us
    reduce_scatter x1, waiting for transfers between devices, shards(): lax.psum_scatter(matrix_grad_two, 'fsdp', scatter_dimension=0, tiled=True)  42.6 us
    add x2, other arithmetic, adam_step(): second_new = BETA_TWO * second_mom + (1.0 - BETA_TWO) * gradient * gradient  12.9 us
  transfers between devices with their start and end apart: 2, of which 1 were waited for; matrix products, arithmetic and copies ran while one was open for 7% of the time, Pallas kernels for 36%

profile of v6, /device:TPU:0, one launch (start us, length us, event | category | flops | bytes accessed | tf_op | source)
XLA Modules:
  0.0 615.9 jit_solution(3813316171812902209)
XLA Ops:
  7.2 3.4 convert.42
  10.6 2.0 fusion.22
  12.7 111.9 %gather_rows.1.weight_hbm = bf16[9216,768]{1,0:T(8,128)(2,1)} custom-call(bf16[1152,768]{1,0:T(8,128)(2,1)} %get-tuple-element.110.shard_ref), custom_call_target="tpu_custom_call" | custom-call | tf_op jit(solution)/shard_map/gather_rows/pallas_call | solution.py:315
  126.4 53.6 %layer_ahead.1 = (bf16[4,256,768]{2,1,0:T(8,128)(2,1)}, bf16[4,512,768]{2,1,0:T(8,128)(2,1)}, bf16[4,512,768]{2,1,0:T(8,128)(2,1)}, f32[4,16,256]{2,1,0:T(8,128)...) custom-call(s32[4]{0:T(128)} %lengths_ref.5, ...), custom_call_target="tpu_custom_call" | custom-call | flops 18522046464 | bytes 44155776 | tf_op jit(solution)/shard_map/layer_ahead/pallas_call | solution.py:1122
  180.1 71.5 %layer_last.1 = (bf16[4,256,768]{2,1,0:T(8,128)(2,1)}, bf16[4,256,768]{2,1,0:T(8,128)(2,1)}, bf16[4,256,768]{2,1,0:T(8,128)(2,1)}, bf16[4,256,3072]{2,1,0:T(8,12...) custom-call(s32[4]{0:T(128)} %lengths_ref.5, ...), custom_call_target="tpu_custom_call" | custom-call | flops 60000002048 | bytes 80000000 | tf_op jit(solution)/shard_map/layer_last/pallas_call | solution.py:1671
  251.7 4.6 fusion.8
  256.2 2.5 fusion.9
  258.7 2.5 fusion.10
  261.2 2.5 fusion.11
  263.8 7.0 %fusion.4 = bf16[9216,768]{1,0:T(8,128)(2,1)} fusion(bf16[9216,768]{1,0:T(8,128)(2,1)} %fusion.11, bf16[4,256,3072]{2,1,0:T(8,128)(2,1)S(1)} %bitcast.122, bf16[4,256,768]{2,1,0:T(8,128)(2,1)S(1)} %copy-done.25), kind=kOutput, calls=%fused_computation.13 | convolution fusion | flops 4834197504 | bytes 12582912 | tf_op jit(solution)/shard_map/dot_general | solution.py:1712
  270.8 7.3 %fusion.5 = bf16[9216,768]{1,0:T(8,128)(2,1)} fusion(bf16[9216,768]{1,0:T(8,128)(2,1)} %fusion.4, bf16[4,256,3072]{2,1,0:T(8,128)(2,1)S(1)} %bitcast.120, bf16[4,256,768]{2,1,0:T(8,128)(2,1)S(1)} %copy-done.24), kind=kOutput, calls=%fused_computation.14 | convolution fusion | flops 4834197504 | bytes 12582912 | tf_op jit(solution)/shard_map/dot_general | solution.py:1712
  278.1 0.6 broadcast_in_dim.8.small_ref
  278.7 3.3 fusion.19
  282.0 2.9 fusion.18
  285.1 4.4 add_add_fusion.grad_ref
  289.5 59.0 %layer_back.1 = (bf16[4,256,768]{2,1,0:T(8,128)(2,1)}, bf16[4,256,3072]{2,1,0:T(8,128)(2,1)}, bf16[4,256,768]{2,1,0:T(8,128)(2,1)}, bf16[4,256,768]{2,1,0:T(8,12...) custom-call(s32[4]{0:T(128)} %lengths_ref.5, ...), custom_call_target="tpu_custom_call" | custom-call | flops 20937965568 | bytes 54155776 | tf_op jit(solution)/shard_map/layer_back/pallas_call | solution.py:1405
  348.4 0.7 reshape.48
  349.1 0.8 slice_reduce_fusion.1
  350.2 0.6 broadcast_in_dim.7.small_grad
  350.9 4.1 fusion.12
  355.0 3.7 fusion.15
  358.7 3.7 fusion.17
  362.4 2.5 fusion.13
  364.9 7.0 %fusion.6 = bf16[9216,768]{1,0:T(8,128)(2,1)} fusion(bf16[9216,768]{1,0:T(8,128)(2,1)} %fusion.13, bf16[4,256,3072]{2,1,0:T(8,128)(2,1)S(1)} %bitcast.118, bf16[4,256,768]{2,1,0:T(8,128)(2,1)S(1)} %copy-done.23), kind=kOutput, calls=%fused_computation.15 | convolution fusion | flops 4834197504 | bytes 12582912 | tf_op jit(solution)/shard_map/dot_general | solution.py:1712
  371.9 7.1 %fusion.7.grad_zero = bf16[9216,768]{1,0:T(8,128)(2,1)} fusion(bf16[9216,768]{1,0:T(8,128)(2,1)} %fusion.6, bf16[4,256,3072]{2,1,0:T(8,128)(2,1)S(1)} %bitcast.116, bf16[4,256,768]{2,1,0:T(8,128)(2,1)S(1)} %copy-done.22), kind=kOutput, calls=%fused_computation.16 | convolution fusion | flops 4834197504 | bytes 12582912 | tf_op jit(solution)/shard_map/dot_general | solution.py:1712
  379.0 42.6 %reduce-scatter.2.cloned.1.call-done.shard_one = bf16[1152,768]{1,0:T(8,128)(2,1)} async-done(((bf16[9216,768]{1,0:T(8,128)(2,1)}), bf16[1152,768]{1,0:T(8,128)(2,1)}) %reduce-scatter.2.cloned.1.call-update) | async-done | bytes 1769488 | tf_op jit(solution)/shard_map/reduce_scatter | solution.py:1791
  421.7 161.0 %finish.1 = (bf16[2,1152,768]{2,1,0:T(8,128)(2,1)}, bf16[2,1152,768]{2,1,0:T(8,128)(2,1)}, f32[1,6168]{1,0:T(1,128)}, f32[1,6168]{1,0:T(1,128)}, bf16[4608,768]{1,0:T(8,128)(2,1)}, /*index=5*/bf16[6912,768]{1,0:T(8,128)(2,1)}) custom-call(bf16[9216,768]{1,0:T(8,128)(2,1)} %fusion.7.grad_zero, bf16[1152,768]{1,0:T(8,128)(2,1)} %reduce-scatter.2.cloned.1.call-done.shard_one, ...), custom_call_target="tpu_custom_call" | custom-call | tf_op jit(solution)/shard_map/finish/pallas_call | solution.py:871
  582.8 12.2 %fusion.3 = (f32[1,2,1152,768]{3,2,1,0:T(8,128)}, f32[1,2,1152,768]{3,2,1,0:T(8,128)}) fusion(bf16[2,1152,768]{2,1,0:T(8,128)(2,1)} %get-tuple-element.98, f32[1,2,1152,768]{3,2,1,0:T(8,128)} %second_hbm.1, f32[1,2,1152,768]{3,2,1,0:T(8,128)} %first_hbm.1), kind=kLoop, calls=%fused_computation.9 | loop fusion | flops 14155776 | bytes 31850496 | tf_op jit(solution)/shard_map/add | solution.py:1734
  595.0 0.7 fusion.20
  596.5 0.8 slice-done.1
  597.3 0.8 slice-done.3
  598.1 10.7 %fusion.21 = (bf16[2,1152,768]{2,1,0:T(8,128)(2,1)}, f32[2,1152,768]{2,1,0:T(8,128)}, f32[2,1152,768]{2,1,0:T(8,128)}, f32[2,1152,768]{2,1,0:T(8,128)}) fusion(f32[2,1152,768]{2,1,0:T(8,128)S(1)} %bitcast.111, f32[2,1152,768]{2,1,0:T(8,128)S(1)} %bitcast.113, bf16[2,1152,768]{2,1,0:T(8,128)(2,1)} %get-tuple-element.97), kind=kLoop, calls=%fused_computation.50 | loop fusion | flops 15925248 | bytes 42467328 | tf_op jit(solution)/shard_map/convert_element_type | solution.py:1830
  (95 shorter events, 3.3 us)
Async XLA Ops:
  7.2 172.9 %all-gather.3.cloned.1.call-start = ((), (), s32[]{:S(2)}) async-start(), calls=%async_computation.2 | async-start | bytes 15925248 | tf_op jit(solution)/shard_map/all_gather | solution.py:1771
  12.6 409.0 %reduce-scatter.2.cloned.1.call-start = ((), (), s32[]{:S(2)}) async-start(), calls=%async_computation.1 | async-start | bytes 15925248 | tf_op jit(solution)/shard_map/reduce_scatter | solution.py:1791
  12.7 111.9 %copy-start.2 = (f32[6168]{0:T(1024)S(1)}, f32[6168]{0:T(1024)}, u32[]{:S(2)}) copy-start(f32[6168]{0:T(1024)} %param.18) | copy-start | bytes 74020
  251.6 4.6 copy-start.12
  251.6 4.6 copy-start.18
  256.2 7.5 %slice-start.10 = ((s8[6291456]{0:T(1024)(128)(4,1)}), s8[4194304]{0:T(1024)(128)(4,1)S(1)}, s32[]{:S(2)}) async-start(s8[6291456]{0:T(1024)(128)(4,1)} %bitcast.121), calls=%async_computation.13 | async-start | bytes 8388608
  258.7 5.0 slice-start.11
  261.2 9.5 %slice-start.8 = ((s8[6291456]{0:T(1024)(128)(4,1)}), s8[4194304]{0:T(1024)(128)(4,1)S(1)}, s32[]{:S(2)}) async-start(s8[6291456]{0:T(1024)(128)(4,1)} %bitcast.119), calls=%async_computation.11 | async-start | bytes 8388608
  263.8 7.0 %slice-start.9 = ((s8[6291456]{0:T(1024)(128)(4,1)}), s8[2097152]{0:T(1024)(128)(4,1)S(1)}, s32[]{:S(2)}) async-start(s8[6291456]{0:T(1024)(128)(4,1)} %bitcast.119), calls=%async_computation.12 | async-start | bytes 4194304
  263.8 7.0 %copy-start.24 = (bf16[4,256,768]{2,1,0:T(8,128)(2,1)S(1)}, bf16[4,256,768]{2,1,0:T(8,128)(2,1)}, u32[]{:S(2)}) copy-start(bf16[4,256,768]{2,1,0:T(8,128)(2,1)} %get-tuple-element.69) | copy-start | bytes 4718596
  289.5 60.5 %copy-start.10 = (f32[4,768]{1,0:T(4,128)S(1)}, f32[4,768]{1,0:T(4,128)}, u32[]{:S(2)}) copy-start(f32[4,768]{1,0:T(4,128)} %get-tuple-element.95) | copy-start | bytes 36868
  289.5 60.6 %copy-start.9 = (f32[16,256]{1,0:T(8,128)S(1)}, f32[16,256]{1,0:T(8,128)}, u32[]{:S(2)}) copy-start(f32[16,256]{1,0:T(8,128)} %get-tuple-element.96) | copy-start | bytes 49156
  289.5 61.4 %copy-start.19 = (bf16[4,256,768]{2,1,0:T(8,128)(2,1)S(1)}, bf16[4,256,768]{2,1,0:T(8,128)(2,1)}, u32[]{:S(2)}) copy-start(bf16[4,256,768]{2,1,0:T(8,128)(2,1)} %get-tuple-element.83) | copy-start | bytes 4718596
  350.9 4.1 copy-start.11
  350.9 4.1 copy-start.21
  355.0 3.7 copy-start.20
  355.0 9.9 %slice-start.6 = ((s8[6291456]{0:T(1024)(128)(4,1)}), s8[4194304]{0:T(1024)(128)(4,1)S(1)}, s32[]{:S(2)}) async-start(s8[6291456]{0:T(1024)(128)(4,1)} %bitcast.117), calls=%async_computation.9 | async-start | bytes 8388608
  358.7 3.7 copy-start.15
  358.7 6.2 %slice-start.7 = ((s8[6291456]{0:T(1024)(128)(4,1)}), s8[2097152]{0:T(1024)(128)(4,1)S(1)}, s32[]{:S(2)}) async-start(s8[6291456]{0:T(1024)(128)(4,1)} %bitcast.117), calls=%async_computation.10 | async-start | bytes 4194304
  362.4 9.5 %slice-start.4 = ((s8[6291456]{0:T(1024)(128)(4,1)}), s8[2097152]{0:T(1024)(128)(4,1)S(1)}, s32[]{:S(2)}) async-start(s8[6291456]{0:T(1024)(128)(4,1)} %bitcast.115), calls=%async_computation.7 | async-start | bytes 4194304
  364.9 7.0 %slice-start.5 = ((s8[6291456]{0:T(1024)(128)(4,1)}), s8[4194304]{0:T(1024)(128)(4,1)S(1)}, s32[]{:S(2)}) async-start(s8[6291456]{0:T(1024)(128)(4,1)} %bitcast.115), calls=%async_computation.8 | async-start | bytes 8388608
  364.9 7.0 %copy-start.22 = (bf16[4,256,768]{2,1,0:T(8,128)(2,1)S(1)}, bf16[4,256,768]{2,1,0:T(8,128)(2,1)}, u32[]{:S(2)}) copy-start(bf16[4,256,768]{2,1,0:T(8,128)(2,1)} %get-tuple-element.91) | copy-start | bytes 4718596
  582.7 13.6 %slice-start = ((s8[7077888]{0:T(1024)(128)(4,1)}), s8[4194304]{0:T(1024)(128)(4,1)S(1)}, s32[]{:S(2)}) async-start(s8[7077888]{0:T(1024)(128)(4,1)} %bitcast.110), calls=%async_computation.3 | async-start | bytes 8388608
  582.7 13.8 %slice-start.2 = ((s8[7077888]{0:T(1024)(128)(4,1)}), s8[4194304]{0:T(1024)(128)(4,1)S(1)}, s32[]{:S(2)}) async-start(s8[7077888]{0:T(1024)(128)(4,1)} %bitcast.112), calls=%async_computation.5 | async-start | bytes 8388608
  582.7 12.2 %copy-start.4 = (f32[1,6168]{1,0:T(1,128)S(1)}, f32[1,6168]{1,0:T(1,128)}, u32[]{:S(2)}) copy-start(f32[1,6168]{1,0:T(1,128)} %small_first.1) | copy-start | bytes 74020
  582.7 12.2 %copy-start.5 = (f32[1,6168]{1,0:T(1,128)S(1)}, f32[1,6168]{1,0:T(1,128)}, u32[]{:S(2)}) copy-start(f32[1,6168]{1,0:T(1,128)} %small_second.1) | copy-start | bytes 74020
  582.7 12.2 %copy-start.7 = (f32[1,6168]{1,0:T(1,128)S(1)}, f32[1,6168]{1,0:T(1,128)}, u32[]{:S(2)}) copy-start(f32[1,6168]{1,0:T(1,128)} %get-tuple-element.100) | copy-start | bytes 74020
  582.7 12.2 %copy-start.8 = (f32[1,6168]{1,0:T(1,128)S(1)}, f32[1,6168]{1,0:T(1,128)}, u32[]{:S(2)}) copy-start(f32[1,6168]{1,0:T(1,128)} %get-tuple-element.99) | copy-start | bytes 74020
  582.8 12.9 %copy-start.6 = (f32[6168]{0:T(1024)S(1)}, f32[6168]{0:T(1024)}, u32[]{:S(2)}) copy-start(f32[6168]{0:T(1024)} %param.21) | copy-start | bytes 74020
  582.8 14.6 %slice-start.1 = ((s8[7077888]{0:T(1024)(128)(4,1)}), s8[2883584]{0:T(1024)(128)(4,1)S(1)}, s32[]{:S(2)}) async-start(s8[7077888]{0:T(1024)(128)(4,1)} %bitcast.110), calls=%async_computation.4 | async-start | bytes 5767168
  582.8 15.4 %slice-start.3 = ((s8[7077888]{0:T(1024)(128)(4,1)}), s8[2883584]{0:T(1024)(128)(4,1)S(1)}, s32[]{:S(2)}) async-start(s8[7077888]{0:T(1024)(128)(4,1)} %bitcast.112), calls=%async_computation.6 | async-start | bytes 5767168
  595.7 13.2 %copy-start.3 = (f32[6168]{0:T(1024)}, f32[6168]{0:T(1024)S(1)}, u32[]{:S(2)}) copy-start(f32[6168]{0:T(1024)S(1)} %get-tuple-element.117) | copy-start | bytes 74020
  (8 other events, 22.6 us)
Sparse Core Ops, SparseCore 0:
  12.7 150.4 all-gather.2
  278.2 143.3 reduce-scatter.1

commit v7 on v6

--- a/solution.py
+++ b/solution.py
@@ -934,8 +934,9 @@
         @pl.when(self.active)
         def _():
             self.copies[index].wait()
-            if index + self.depth < len(self.copies):
-                self.copies[index + self.depth].start()
+            first = self.depth * (index + 1)
+            for copy in self.copies[first : first + self.depth]:
+                copy.start()
 
 
 def feed_cuts(width, inner):

time: 627 us -> 624 us (level)
  no operation moved by 1% of the time
where the time goes in v7:
time: 624 us; the launch traced here: 613 us
  Pallas kernels  454 us (73%)
  matrix products  64.9 us (10%)
  waiting for transfers between devices  42.6 us (7%)
  other arithmetic  28.5 us (5%)
  between operations  14.6 us (2%)
  local copies, waits for them, and re-layouts  8.11 us (1%)
    pallas_call x1, Pallas kernels, finish(): pl.pallas_call(functools.partial(finish_kernel, chips, group_count), grid...  161 us
    pallas_call x1, Pallas kernels, gather_rows(): pl.pallas_call(functools.partial(gather_kernel, members // 2, group_count...  112 us
    pallas_call x1, Pallas kernels, layer_last(): pl.pallas_call(functools.partial(last_kernel, head_count), grid_spec=pltp...  70 us
    pallas_call x1, Pallas kernels, layer_back(): pl.pallas_call(functools.partial(back_kernel, is_first, head_count, place...  59 us
    dot_general x12, matrix products, weight_product(): lax.dot_general(left, right, (((0, 1), (0, 1)), ((), ())), preferred_elem...  54.4 us
    pallas_call x1, Pallas kernels, layer_ahead(): pl.pallas_call(functools.partial(ahead_kernel, is_first, head_count, plac...  52.1 us
    reduce_scatter x1, waiting for transfers between devices, shards(): lax.psum_scatter(matrix_grad_two, 'fsdp', scatter_dimension=0, tiled=True)  42.5 us
    add x2, other arithmetic, adam_step(): second_new = BETA_TWO * second_mom + (1.0 - BETA_TWO) * gradient * gradient  12.9 us
  transfers between devices with their start and end apart: 2, of which 1 were waited for; matrix products, arithmetic and copies ran while one was open for 7% of the time, Pallas kernels for 36%

profile of v7, /device:TPU:0, one launch (start us, length us, event | category | flops | bytes accessed | tf_op | source)
XLA Modules:
  0.0 612.9 jit_solution(8429003914294144886)
XLA Ops:
  7.2 3.4 convert.42
  10.6 2.0 fusion.22
  12.7 111.9 %gather_rows.1.weight_hbm = bf16[9216,768]{1,0:T(8,128)(2,1)} custom-call(bf16[1152,768]{1,0:T(8,128)(2,1)} %get-tuple-element.110.shard_ref), custom_call_target="tpu_custom_call" | custom-call | tf_op jit(solution)/shard_map/gather_rows/pallas_call | solution.py:315
  126.4 52.1 %layer_ahead.1 = (bf16[4,256,768]{2,1,0:T(8,128)(2,1)}, bf16[4,512,768]{2,1,0:T(8,128)(2,1)}, bf16[4,512,768]{2,1,0:T(8,128)(2,1)}, f32[4,16,256]{2,1,0:T(8,128)...) custom-call(s32[4]{0:T(128)} %lengths_ref.5, ...), custom_call_target="tpu_custom_call" | custom-call | flops 18522046464 | bytes 44155776 | tf_op jit(solution)/shard_map/layer_ahead/pallas_call | solution.py:1123
  178.6 70.0 %layer_last.1 = (bf16[4,256,768]{2,1,0:T(8,128)(2,1)}, bf16[4,256,768]{2,1,0:T(8,128)(2,1)}, bf16[4,256,768]{2,1,0:T(8,128)(2,1)}, bf16[4,256,3072]{2,1,0:T(8,12...) custom-call(s32[4]{0:T(128)} %lengths_ref.5, ...), custom_call_target="tpu_custom_call" | custom-call | flops 60000002048 | bytes 80000000 | tf_op jit(solution)/shard_map/layer_last/pallas_call | solution.py:1672
  248.6 4.6 fusion.8
  253.2 2.5 fusion.9
  255.7 2.5 fusion.10
  258.2 2.5 fusion.11
  260.8 7.0 %fusion.4 = bf16[9216,768]{1,0:T(8,128)(2,1)} fusion(bf16[9216,768]{1,0:T(8,128)(2,1)} %fusion.11, bf16[4,256,3072]{2,1,0:T(8,128)(2,1)S(1)} %bitcast.122, bf16[4,256,768]{2,1,0:T(8,128)(2,1)S(1)} %copy-done.25), kind=kOutput, calls=%fused_computation.13 | convolution fusion | flops 4834197504 | bytes 12582912 | tf_op jit(solution)/shard_map/dot_general | solution.py:1713
  267.8 7.3 %fusion.5 = bf16[9216,768]{1,0:T(8,128)(2,1)} fusion(bf16[9216,768]{1,0:T(8,128)(2,1)} %fusion.4, bf16[4,256,3072]{2,1,0:T(8,128)(2,1)S(1)} %bitcast.120, bf16[4,256,768]{2,1,0:T(8,128)(2,1)S(1)} %copy-done.24), kind=kOutput, calls=%fused_computation.14 | convolution fusion | flops 4834197504 | bytes 12582912 | tf_op jit(solution)/shard_map/dot_general | solution.py:1713
  275.1 0.6 broadcast_in_dim.8.small_ref
  275.7 3.3 fusion.19
  279.0 2.9 fusion.18
  282.1 4.4 add_add_fusion.grad_ref
  286.5 59.0 %layer_back.1 = (bf16[4,256,768]{2,1,0:T(8,128)(2,1)}, bf16[4,256,3072]{2,1,0:T(8,128)(2,1)}, bf16[4,256,768]{2,1,0:T(8,128)(2,1)}, bf16[4,256,768]{2,1,0:T(8,12...) custom-call(s32[4]{0:T(128)} %lengths_ref.5, ...), custom_call_target="tpu_custom_call" | custom-call | flops 20937965568 | bytes 54155776 | tf_op jit(solution)/shard_map/layer_back/pallas_call | solution.py:1406
  345.5 0.7 reshape.48
  346.2 0.8 slice_reduce_fusion.1
  347.3 0.6 broadcast_in_dim.7.small_grad
  347.9 4.1 fusion.12
  352.0 3.7 fusion.15
  355.7 3.7 fusion.17
  359.4 2.5 fusion.13
  361.9 7.0 %fusion.6 = bf16[9216,768]{1,0:T(8,128)(2,1)} fusion(bf16[9216,768]{1,0:T(8,128)(2,1)} %fusion.13, bf16[4,256,3072]{2,1,0:T(8,128)(2,1)S(1)} %bitcast.118, bf16[4,256,768]{2,1,0:T(8,128)(2,1)S(1)} %copy-done.23), kind=kOutput, calls=%fused_computation.15 | convolution fusion | flops 4834197504 | bytes 12582912 | tf_op jit(solution)/shard_map/dot_general | solution.py:1713
  368.9 7.1 %fusion.7.grad_zero = bf16[9216,768]{1,0:T(8,128)(2,1)} fusion(bf16[9216,768]{1,0:T(8,128)(2,1)} %fusion.6, bf16[4,256,3072]{2,1,0:T(8,128)(2,1)S(1)} %bitcast.116, bf16[4,256,768]{2,1,0:T(8,128)(2,1)S(1)} %copy-done.22), kind=kOutput, calls=%fused_computation.16 | convolution fusion | flops 4834197504 | bytes 12582912 | tf_op jit(solution)/shard_map/dot_general | solution.py:1713
  376.1 42.5 %reduce-scatter.2.cloned.1.call-done.shard_one = bf16[1152,768]{1,0:T(8,128)(2,1)} async-done(((bf16[9216,768]{1,0:T(8,128)(2,1)}), bf16[1152,768]{1,0:T(8,128)(2,1)}) %reduce-scatter.2.cloned.1.call-update) | async-done | bytes 1769488 | tf_op jit(solution)/shard_map/reduce_scatter | solution.py:1792
  418.6 161.1 %finish.1 = (bf16[2,1152,768]{2,1,0:T(8,128)(2,1)}, bf16[2,1152,768]{2,1,0:T(8,128)(2,1)}, f32[1,6168]{1,0:T(1,128)}, f32[1,6168]{1,0:T(1,128)}, bf16[4608,768]{1,0:T(8,128)(2,1)}, /*index=5*/bf16[6912,768]{1,0:T(8,128)(2,1)}) custom-call(bf16[9216,768]{1,0:T(8,128)(2,1)} %fusion.7.grad_zero, bf16[1152,768]{1,0:T(8,128)(2,1)} %reduce-scatter.2.cloned.1.call-done.shard_one, ...), custom_call_target="tpu_custom_call" | custom-call | tf_op jit(solution)/shard_map/finish/pallas_call | solution.py:871
  579.7 12.2 %fusion.3 = (f32[1,2,1152,768]{3,2,1,0:T(8,128)}, f32[1,2,1152,768]{3,2,1,0:T(8,128)}) fusion(bf16[2,1152,768]{2,1,0:T(8,128)(2,1)} %get-tuple-element.98, f32[1,2,1152,768]{3,2,1,0:T(8,128)} %second_hbm.1, f32[1,2,1152,768]{3,2,1,0:T(8,128)} %first_hbm.1), kind=kLoop, calls=%fused_computation.9 | loop fusion | flops 14155776 | bytes 31850496 | tf_op jit(solution)/shard_map/add | solution.py:1735
  591.9 0.7 fusion.20
  593.4 0.8 slice-done.1
  594.3 0.8 slice-done.3
  595.1 10.7 %fusion.21 = (bf16[2,1152,768]{2,1,0:T(8,128)(2,1)}, f32[2,1152,768]{2,1,0:T(8,128)}, f32[2,1152,768]{2,1,0:T(8,128)}, f32[2,1152,768]{2,1,0:T(8,128)}) fusion(f32[2,1152,768]{2,1,0:T(8,128)S(1)} %bitcast.111, f32[2,1152,768]{2,1,0:T(8,128)S(1)} %bitcast.113, bf16[2,1152,768]{2,1,0:T(8,128)(2,1)} %get-tuple-element.97), kind=kLoop, calls=%fused_computation.50 | loop fusion | flops 15925248 | bytes 42467328 | tf_op jit(solution)/shard_map/convert_element_type | solution.py:1831
  (95 shorter events, 3.3 us)
Async XLA Ops:
  7.2 171.4 %all-gather.3.cloned.1.call-start = ((), (), s32[]{:S(2)}) async-start(), calls=%async_computation.2 | async-start | bytes 15925248 | tf_op jit(solution)/shard_map/all_gather | solution.py:1772
  12.6 406.0 %reduce-scatter.2.cloned.1.call-start = ((), (), s32[]{:S(2)}) async-start(), calls=%async_computation.1 | async-start | bytes 15925248 | tf_op jit(solution)/shard_map/reduce_scatter | solution.py:1792
  12.7 111.9 %copy-start.2 = (f32[6168]{0:T(1024)S(1)}, f32[6168]{0:T(1024)}, u32[]{:S(2)}) copy-start(f32[6168]{0:T(1024)} %param.18) | copy-start | bytes 74020
  248.6 4.6 copy-start.12
  248.6 4.6 copy-start.18
  253.2 7.5 %slice-start.10 = ((s8[6291456]{0:T(1024)(128)(4,1)}), s8[4194304]{0:T(1024)(128)(4,1)S(1)}, s32[]{:S(2)}) async-start(s8[6291456]{0:T(1024)(128)(4,1)} %bitcast.121), calls=%async_computation.13 | async-start | bytes 8388608
  255.7 5.0 slice-start.11
  258.2 9.5 %slice-start.8 = ((s8[6291456]{0:T(1024)(128)(4,1)}), s8[4194304]{0:T(1024)(128)(4,1)S(1)}, s32[]{:S(2)}) async-start(s8[6291456]{0:T(1024)(128)(4,1)} %bitcast.119), calls=%async_computation.11 | async-start | bytes 8388608
  260.8 7.0 %slice-start.9 = ((s8[6291456]{0:T(1024)(128)(4,1)}), s8[2097152]{0:T(1024)(128)(4,1)S(1)}, s32[]{:S(2)}) async-start(s8[6291456]{0:T(1024)(128)(4,1)} %bitcast.119), calls=%async_computation.12 | async-start | bytes 4194304
  260.8 7.0 %copy-start.24 = (bf16[4,256,768]{2,1,0:T(8,128)(2,1)S(1)}, bf16[4,256,768]{2,1,0:T(8,128)(2,1)}, u32[]{:S(2)}) copy-start(bf16[4,256,768]{2,1,0:T(8,128)(2,1)} %get-tuple-element.69) | copy-start | bytes 4718596
  286.5 60.5 %copy-start.10 = (f32[4,768]{1,0:T(4,128)S(1)}, f32[4,768]{1,0:T(4,128)}, u32[]{:S(2)}) copy-start(f32[4,768]{1,0:T(4,128)} %get-tuple-element.95) | copy-start | bytes 36868
  286.5 60.6 %copy-start.9 = (f32[16,256]{1,0:T(8,128)S(1)}, f32[16,256]{1,0:T(8,128)}, u32[]{:S(2)}) copy-start(f32[16,256]{1,0:T(8,128)} %get-tuple-element.96) | copy-start | bytes 49156
  286.5 61.4 %copy-start.19 = (bf16[4,256,768]{2,1,0:T(8,128)(2,1)S(1)}, bf16[4,256,768]{2,1,0:T(8,128)(2,1)}, u32[]{:S(2)}) copy-start(bf16[4,256,768]{2,1,0:T(8,128)(2,1)} %get-tuple-element.83) | copy-start | bytes 4718596
  347.9 4.1 copy-start.11
  347.9 4.1 copy-start.21
  352.0 3.7 copy-start.20
  352.0 9.9 %slice-start.6 = ((s8[6291456]{0:T(1024)(128)(4,1)}), s8[4194304]{0:T(1024)(128)(4,1)S(1)}, s32[]{:S(2)}) async-start(s8[6291456]{0:T(1024)(128)(4,1)} %bitcast.117), calls=%async_computation.9 | async-start | bytes 8388608
  355.7 3.7 copy-start.15
  355.7 6.2 %slice-start.7 = ((s8[6291456]{0:T(1024)(128)(4,1)}), s8[2097152]{0:T(1024)(128)(4,1)S(1)}, s32[]{:S(2)}) async-start(s8[6291456]{0:T(1024)(128)(4,1)} %bitcast.117), calls=%async_computation.10 | async-start | bytes 4194304
  359.4 9.5 %slice-start.4 = ((s8[6291456]{0:T(1024)(128)(4,1)}), s8[2097152]{0:T(1024)(128)(4,1)S(1)}, s32[]{:S(2)}) async-start(s8[6291456]{0:T(1024)(128)(4,1)} %bitcast.115), calls=%async_computation.7 | async-start | bytes 4194304
  361.9 7.0 %slice-start.5 = ((s8[6291456]{0:T(1024)(128)(4,1)}), s8[4194304]{0:T(1024)(128)(4,1)S(1)}, s32[]{:S(2)}) async-start(s8[6291456]{0:T(1024)(128)(4,1)} %bitcast.115), calls=%async_computation.8 | async-start | bytes 8388608
  361.9 7.0 %copy-start.22 = (bf16[4,256,768]{2,1,0:T(8,128)(2,1)S(1)}, bf16[4,256,768]{2,1,0:T(8,128)(2,1)}, u32[]{:S(2)}) copy-start(bf16[4,256,768]{2,1,0:T(8,128)(2,1)} %get-tuple-element.91) | copy-start | bytes 4718596
  579.6 13.6 %slice-start = ((s8[7077888]{0:T(1024)(128)(4,1)}), s8[4194304]{0:T(1024)(128)(4,1)S(1)}, s32[]{:S(2)}) async-start(s8[7077888]{0:T(1024)(128)(4,1)} %bitcast.110), calls=%async_computation.3 | async-start | bytes 8388608
  579.7 13.8 %slice-start.2 = ((s8[7077888]{0:T(1024)(128)(4,1)}), s8[4194304]{0:T(1024)(128)(4,1)S(1)}, s32[]{:S(2)}) async-start(s8[7077888]{0:T(1024)(128)(4,1)} %bitcast.112), calls=%async_computation.5 | async-start | bytes 8388608
  579.7 12.2 %copy-start.4 = (f32[1,6168]{1,0:T(1,128)S(1)}, f32[1,6168]{1,0:T(1,128)}, u32[]{:S(2)}) copy-start(f32[1,6168]{1,0:T(1,128)} %small_first.1) | copy-start | bytes 74020
  579.7 12.2 %copy-start.5 = (f32[1,6168]{1,0:T(1,128)S(1)}, f32[1,6168]{1,0:T(1,128)}, u32[]{:S(2)}) copy-start(f32[1,6168]{1,0:T(1,128)} %small_second.1) | copy-start | bytes 74020
  579.7 12.2 %copy-start.7 = (f32[1,6168]{1,0:T(1,128)S(1)}, f32[1,6168]{1,0:T(1,128)}, u32[]{:S(2)}) copy-start(f32[1,6168]{1,0:T(1,128)} %get-tuple-element.100) | copy-start | bytes 74020
  579.7 12.2 %copy-start.8 = (f32[1,6168]{1,0:T(1,128)S(1)}, f32[1,6168]{1,0:T(1,128)}, u32[]{:S(2)}) copy-start(f32[1,6168]{1,0:T(1,128)} %get-tuple-element.99) | copy-start | bytes 74020
  579.7 12.9 %copy-start.6 = (f32[6168]{0:T(1024)S(1)}, f32[6168]{0:T(1024)}, u32[]{:S(2)}) copy-start(f32[6168]{0:T(1024)} %param.21) | copy-start | bytes 74020
  579.7 14.6 %slice-start.1 = ((s8[7077888]{0:T(1024)(128)(4,1)}), s8[2883584]{0:T(1024)(128)(4,1)S(1)}, s32[]{:S(2)}) async-start(s8[7077888]{0:T(1024)(128)(4,1)} %bitcast.110), calls=%async_computation.4 | async-start | bytes 5767168
  579.7 15.4 %slice-start.3 = ((s8[7077888]{0:T(1024)(128)(4,1)}), s8[2883584]{0:T(1024)(128)(4,1)S(1)}, s32[]{:S(2)}) async-start(s8[7077888]{0:T(1024)(128)(4,1)} %bitcast.112), calls=%async_computation.6 | async-start | bytes 5767168
  592.6 13.2 %copy-start.3 = (f32[6168]{0:T(1024)}, f32[6168]{0:T(1024)S(1)}, u32[]{:S(2)}) copy-start(f32[6168]{0:T(1024)S(1)} %get-tuple-element.117) | copy-start | bytes 74020
  (8 other events, 22.6 us)
Sparse Core Ops, SparseCore 0:
  12.7 150.4 all-gather.2
  275.2 143.3 reduce-scatter.1
